TPU v7x, 128 devices: a whole 4x4x4 slice. The times are simulated.
128 devices in a mesh: row: 16 (over y, x), col: 8 (over z, core).
Axes of the slice: x: 4, y: 4, z: 4, core: 2. Of those that a mesh axis runs over, the one named last changes fastest.
Arguments:
- features: float32 [32768, 256], P(('row', 'col')), may hold values from -6 to 6
- loader_perm: int32 [32768], P(('row', 'col')), may hold values from 0 to 32767, as said below
- block_values: float32 [16, 8, 256, 4096], P('row', 'col'), may hold values from -0.09375 to 0.09375
- block_row: int32 [16, 8, 256], P('row', 'col'), may hold values from 0 to 63
- block_column: int32 [16, 8, 256], P('row', 'col'), may hold values from 0 to 31
- tile_count: int32 [16, 8], P('row', 'col'), may hold values from 32 to 256, as said below
- weight: float32 [256, 256], replicated, may hold values from -0.375 to 0.375
- bias_vector: float32 [256], replicated, may hold values from -0.5 to 0.5
- cotangent: float32 [32768, 256], P(('row', 'col')), may hold values from -6 to 6
Outputs:
- output: float32 [32768, 256], P(('row', 'col'))
- grad_x: float32 [32768, 256], P(('row', 'col'))
- grad_w: float32 [256, 256], replicated
- grad_b: float32 [256], replicated
Inputs may be any that keep to these rules, and one draw needn't show every extreme that they name: `loader_perm`: every grid position appears once; the 256 loader rows of any one device name the same number of positions, 256 divided by the number of devices, in each aligned block of 256 grid positions. `tile_count`: every count is 256 divided by 1, 2, 4 or 8; a block position may appear in several slots of a tile, and such blocks add.
All inputs are finite; a program needn't handle non-finite values.
Results may differ from a plain program's by a relative error of at most 0.0003.
Values sent between devices are 32-bit elements; how exact they have to be, the bound alone decides.
No kernel may reach another device: no remote copies, remote signals or barrier semaphores. Data moves between devices by JAX's collectives and lax.ppermute only.
A program may use at most 128 MiB of HBM per device.

v0:
```python
import functools
import math

import jax
import jax.numpy as jnp
from jax import lax
from jax.experimental import pallas as pl
from jax.experimental.pallas import tpu as pltpu
from jax.sharding import PartitionSpec as P

precise = lax.Precision.HIGHEST
F = 256
BS = 64
NODE = 256
SLOTS = 256
STEP = 32
DEPTH = 192
ROWS = 16
COLS = 8
SIDE = 4
LANES = 128
W_ROWS = 40


f32 = jnp.float32
bf16 = jnp.bfloat16


def room(mib):
    return pltpu.CompilerParams(vmem_limit_bytes=mib << 20)


def whole():
    return pl.BlockSpec(memory_space=pltpu.VMEM)


def anywhere():
    return pl.BlockSpec(memory_space=pl.ANY)


def row_hop(dy, dx):
    return [
        (y * SIDE + x, (y + dy) % SIDE * SIDE + (x + dx) % SIDE)
        for y in range(SIDE)
        for x in range(SIDE)
    ]


def col_hop(dz, dc):
    return [
        (z * 2 + c, (z + dz) % SIDE * 2 + (c + dc) % 2) for z in range(SIDE) for c in range(2)
    ]


def pack_kernel(features, perm_row, sent):
    owner_row = jnp.broadcast_to(lax.shift_right_logical(perm_row[...], 8), (NODE, NODE))
    owner_col = owner_row.astype(f32).T.astype(jnp.int32)
    first = lax.broadcasted_iota(jnp.int32, (NODE, NODE), 0)
    second = lax.broadcasted_iota(jnp.int32, (NODE, NODE), 1)
    earlier = (owner_col == owner_row) & (first < second)
    rank = jnp.sum(earlier.astype(f32), axis=0, keepdims=True).astype(jnp.int32)
    slot = owner_row[:1] * 2 + rank
    spot = (perm_row[...] & (NODE - 1)).astype(f32)
    rows = lax.broadcasted_iota(jnp.int32, (NODE // 2, NODE), 0)
    for n in range(2):
        chosen = (rows * 2 + n == slot).astype(f32)
        sent[:, n, :F] = jnp.dot(
            chosen, features[...], precision=precise, preferred_element_type=f32
        )
        spots = jnp.sum(chosen * spot, axis=1, keepdims=True)
        sent[:, n, F:] = jnp.broadcast_to(spots, (NODE // 2, LANES))


def pack(features, perm):
    return pl.pallas_call(
        pack_kernel,
        out_shape=jax.ShapeDtypeStruct((NODE // 2, 2, F + LANES), f32),
        in_specs=[whole()] * 2,
        out_specs=whole(),
        compiler_params=room(8),
        name="pack",
    )(pltpu.with_memory_space_constraint(features, pltpu.HBM), perm.reshape(1, NODE))


def place_kernel(got, own):
    second = lax.broadcasted_iota(jnp.int32, (NODE // 2, NODE), 1)
    chosen, rows = [], []
    for n in range(2):
        spot = got[:, n, F:].astype(jnp.int32)
        chosen.append((jnp.concatenate([spot, spot], axis=1) == second).astype(f32))
        rows.append(got[:, n, :F])
    chosen = jnp.concatenate(chosen, axis=0).T
    rows = jnp.concatenate(rows, axis=0)
    own[...] = jnp.dot(chosen, rows, precision=precise, preferred_element_type=f32)


def place(got):
    return pl.pallas_call(
        place_kernel,
        out_shape=jax.ShapeDtypeStruct((NODE, F), f32),
        in_specs=[whole()],
        out_specs=whole(),
        compiler_params=room(8),
        name="place",
    )(got)


def prepare_kernel(flip, count, vals, blocks, lines):
    @pl.when(pl.program_id(0) * STEP < count[0])
    def _():
        for group in range(STEP // 8):
            for tile in range(0, BS * BS // LANES, 8):
                square = jnp.stack(
                    [
                        vals[pl.ds(group * 8, 8), pl.ds((tile + t) * LANES, LANES)]
                        for t in range(8)
                    ]
                )
                square = jnp.transpose(square, (1, 0, 2))
                for slot in range(8):
                    lines[pl.ds((group * 8 + slot) * 32 + tile, 8), :] = square[slot]
        left = lax.broadcasted_iota(jnp.int32, (32, LANES), 1) < BS

        def one(slot, carry):
            pair = lines[pl.ds(pl.multiple_of(slot * 32, 32), 32), :]
            turned = pltpu.roll(pair, BS, 1)
            block = jnp.concatenate(
                [jnp.where(left, pair, turned), jnp.where(left, turned, pair)], axis=0
            )
            if flip:
                block = jnp.concatenate([block, block], axis=0).T[:BS]
            high = block.astype(bf16)
            blocks[slot, :, :LANES] = high
            blocks[slot, :, LANES:] = (block - high.astype(f32)).astype(bf16)
            return carry

        lax.fori_loop(0, STEP, one, 0, unroll=8)


def prepare(vals, count, flip):
    def at(step, count):
        return jnp.minimum(step, count[0] // STEP - 1)

    return pl.pallas_call(
        functools.partial(prepare_kernel, flip),
        out_shape=pltpu.HBM((SLOTS, BS, F), bf16),
        grid_spec=pltpu.PrefetchScalarGridSpec(
            num_scalar_prefetch=1,
            grid=(SLOTS // STEP,),
            in_specs=[pl.BlockSpec((STEP, BS * BS), lambda s, n: (at(s, n), 0))],
            out_specs=pl.BlockSpec((STEP, BS, F), lambda s, n: (at(s, n), 0, 0)),
            scratch_shapes=[pltpu.VMEM((STEP * 32, LANES), f32)],
        ),
        cost_estimate=pl.CostEstimate(flops=10**8, bytes_accessed=12 << 20, transcendentals=0),
        compiler_params=room(8),
        name="prepare_back" if flip else "prepare",
    )(count, pltpu.with_memory_space_constraint(vals, pltpu.HBM))


def aggregate_kernel(n_src, n_dst, *refs):
    source_at, target_at, count = refs[:3]
    blocks = refs[3]
    sources = refs[4 : 4 + n_src]
    targets = refs[4 + n_src : 4 + n_src + n_dst]
    held, split, total, in_sems, out_sems = refs[4 + n_src + n_dst :]
    step = pl.program_id(0)
    in_rows = sources[0].shape[0]
    out_rows = targets[0].shape[0]

    def load(n):
        return pltpu.make_async_copy(
            sources[n], held.at[pl.ds(n * in_rows, in_rows)], in_sems.at[n]
        )

    def keep(n):
        return pltpu.make_async_copy(
            total.at[pl.ds(n * out_rows, out_rows)], targets[n], out_sems.at[n]
        )

    @pl.when(step == 0)
    def _():
        for n in range(n_src):
            load(n).start()
        total[...] = jnp.zeros_like(total)
        per = in_rows // BS
        for n in range(n_src):
            load(n).wait()

            def one(k, carry):
                at = n * per + k
                rows = held[pl.ds(pl.multiple_of(at * BS, BS), BS), :]
                high = rows.astype(bf16)
                low = (rows - high.astype(f32)).astype(bf16)
                split[at, 0:BS, :] = high
                split[at, BS : 2 * BS, :] = low
                split[at, 2 * BS :, :] = high
                return carry

            lax.fori_loop(0, per, one, 0, unroll=2)

    @pl.when(step * STEP < count[0])
    def _():
        for slot in range(STEP):
            at = step * STEP + slot
            term = jnp.dot(
                blocks[slot][:, :DEPTH], split[source_at[at]], preferred_element_type=f32
            )
            into = pl.ds(pl.multiple_of(target_at[at] * BS, BS), BS)
            total[into, :] += term

    @pl.when(step == pl.num_programs(0) - 1)
    def _():
        for n in range(n_dst):
            keep(n).start()
        for n in range(n_dst):
            keep(n).wait()


def aggregate(blocks, sources, source_at, target_at, count, n_dst, out_rows):
    n_src = len(sources)
    total_in = sum(s.shape[0] for s in sources)
    steps = SLOTS // STEP
    return pl.pallas_call(
        functools.partial(aggregate_kernel, n_src, n_dst),
        out_shape=[jax.ShapeDtypeStruct((out_rows // n_dst, F), f32)] * n_dst,
        grid_spec=pltpu.PrefetchScalarGridSpec(
            num_scalar_prefetch=3,
            grid=(steps,),
            in_specs=[
                pl.BlockSpec(
                    (STEP, BS, F),
                    lambda s, a, b, n: (jnp.minimum(s, n[0] // STEP - 1), 0, 0),
                )
            ]
            + [anywhere()] * n_src,
            out_specs=[anywhere()] * n_dst,
            scratch_shapes=[
                pltpu.VMEM((total_in, F), f32),
                pltpu.VMEM((total_in // BS, DEPTH, F), bf16),
                pltpu.VMEM((out_rows, F), f32),
                pltpu.SemaphoreType.DMA((n_src,)),
                pltpu.SemaphoreType.DMA((n_dst,)),
            ],
        ),
        cost_estimate=pl.CostEstimate(
            flops=2 * SLOTS * BS * F * F, bytes_accessed=16 << 20, transcendentals=0
        ),
        compiler_params=room(16),
    )(
        source_at,
        target_at,
        count,
        pltpu.with_memory_space_constraint(blocks, pltpu.HBM),
        *sources,
    )


def middle_kernel(*refs):
    where, parts, (weight, bias, cotangent) = refs[0], refs[1:9], refs[9:12]
    output, grad_a, grad_b, sums, gives, hidden, turned, strip = refs[12:]
    half = NODE // 2
    hidden[:half] = parts[0][...] + parts[1][...] + parts[2][...] + parts[3][...]
    hidden[half:] = parts[4][...] + parts[5][...] + parts[6][...] + parts[7][...]
    for side in range(2):
        lanes = slice(side * LANES, (side + 1) * LANES)
        strip[side * NODE : (side + 1) * NODE] = cotangent[:, lanes]
        for q in range(NODE // BS):
            for odd in range(2):
                turned[pl.ds(q * BS + odd * 32, 32), lanes] = strip[
                    pl.ds(side * NODE + q * BS + odd, 32, stride=2), :
                ]
    rows = hidden[...]
    preact = jnp.dot(rows, weight[...], precision=precise, preferred_element_type=f32)
    preact = preact + bias[...]
    squashed = 1.0 / (1.0 + jnp.exp(-preact))
    grad_pre = turned[...] * squashed * (1.0 + preact * (1.0 - squashed))
    turned[...] = preact * squashed
    grad = lax.dot_general(
        grad_pre, weight[...], (((1,), (1,)), ((), ())), precision=precise,
        preferred_element_type=f32,
    )
    grad_a[...] = grad[:half]
    grad_b[...] = grad[half:]
    for side in range(2):
        lanes = slice(side * LANES, (side + 1) * LANES)
        for q in range(NODE // BS):
            for odd in range(2):
                strip[pl.ds(side * NODE + q * BS + odd, 32, stride=2), :] = turned[
                    pl.ds(q * BS + odd * 32, 32), lanes
                ]
        output[:, lanes] = strip[side * NODE : (side + 1) * NODE]
    turned[...] = jnp.dot(rows.T, grad_pre, precision=precise, preferred_element_type=f32)
    local_b = jnp.sum(grad_pre, axis=0, keepdims=True)
    for f in range(SIDE):
        ahead = ((where[0] + f) & 3) * 2
        for side, into in ((where[1], sums), (1 - where[1], gives)):
            at = pl.multiple_of((ahead + side) * 32, 32)
            into[f * W_ROWS : f * W_ROWS + 32, :] = turned[pl.ds(at, 32), :]
            into[f * W_ROWS + 32 : (f + 1) * W_ROWS, :] = jnp.broadcast_to(
                local_b, (W_ROWS - 32, F)
            )


def middle(parts, weight, bias, cotangent, where):
    return pl.pallas_call(
        middle_kernel,
        out_shape=[
            jax.ShapeDtypeStruct((NODE, F), f32),
            jax.ShapeDtypeStruct((NODE // 2, F), f32),
            jax.ShapeDtypeStruct((NODE // 2, F), f32),
            jax.ShapeDtypeStruct((SIDE * W_ROWS, F), f32),
            jax.ShapeDtypeStruct((SIDE * W_ROWS, F), f32),
        ],
        in_specs=[pl.BlockSpec(memory_space=pltpu.SMEM)] + [whole()] * 11,
        out_specs=[whole()] * 5,
        scratch_shapes=[pltpu.VMEM((NODE, F), f32)] * 2 + [pltpu.VMEM((2 * NODE, LANES), f32)],
        compiler_params=room(12),
        name="middle",
    )(where, *parts, weight, bias.reshape(1, F), cotangent)


def finish_kernel(where, *refs):
    pieces, sums, (grad_x, grad_w, grad_b) = refs[:4], refs[4:8], refs[8:]
    grad_x[...] = pieces[0][...] + pieces[1][...] + pieces[2][...] + pieces[3][...]
    scale = 1.0 / math.sqrt(NODE * ROWS * COLS)
    for f in range(SIDE):
        chip = ((where[0] - f) & 3) * 2
        for side in range(2):
            n = chip + (where[1] ^ side)
            rows = sums[f][side * W_ROWS : (side + 1) * W_ROWS, :] * scale
            grad_w[pl.ds(pl.multiple_of(n * 32, 32), 32), :] = rows[:32]

            @pl.when(n == 0)
            def _():
                grad_b[...] = rows[32:33]


def finish(pieces, sums, where):
    return pl.pallas_call(
        finish_kernel,
        out_shape=[
            jax.ShapeDtypeStruct((NODE, F), f32),
            jax.ShapeDtypeStruct((F, F), f32),
            jax.ShapeDtypeStruct((1, F), f32),
        ],
        in_specs=[pl.BlockSpec(memory_space=pltpu.SMEM)] + [whole()] * 8,
        out_specs=[whole()] * 3,
        compiler_params=room(8),
        name="finish",
    )(where, *pieces, *sums)


def on_device(
    features,
    loader_perm,
    block_values,
    block_row,
    block_column,
    tile_count,
    weight,
    bias_vector,
    cotangent,
):
    row = lax.axis_index("row")
    col = lax.axis_index("col")
    my_y, my_x = row // SIDE, row % SIDE
    my_z, my_c = col // 2, col % 2
    where = jnp.stack([my_z, my_c])
    count = tile_count.reshape(1)
    tile_rows = block_row.reshape(SLOTS)
    tile_columns = block_column.reshape(SLOTS)

    r_dev, r_q = tile_rows >> 2, tile_rows & 3
    r_y, r_x = r_dev >> 2, r_dev & 3
    c_dev, c_q = tile_columns >> 2, tile_columns & 3
    c_z, c_c = c_dev >> 1, c_dev & 1
    out_d, out_e = (r_x - my_x) & 3, (r_y - my_y) & 3
    in_d, in_e = (my_x - r_x) & 3, (my_y - r_y) & 3

    def row_slot(d, e):
        first = d * 8 + e * 2 + (r_q & 1)
        second = 32 + e * 8 + d * 2 + (r_q & 1)
        return jnp.where(r_q < 2, first, second)

    fwd_to = row_slot(out_d, out_e)
    bwd_from = row_slot(in_d, in_e)
    other = c_c ^ my_c
    fwd_from = (((my_z - c_z) & 3) * 2 + other) * 4 + c_q
    bwd_to = (other * 4 + ((c_z - my_z) & 3)) * 4 + c_q

    sent = pack(features, loader_perm)
    got = lax.all_to_all(sent, ("row", "col"), split_axis=0, concat_axis=0, tiled=True)
    vals = block_values.reshape(SLOTS, BS * BS)
    fwd_blocks = prepare(vals, count, False)
    got, fwd_blocks = lax.optimization_barrier((got, fwd_blocks))
    own = place(got)
    panel = [own] + [lax.ppermute(own, "col", col_hop(f, 0)) for f in (1, 2, 3)]
    sources = []
    for part in panel:
        sources += [part, lax.ppermute(part, "col", col_hop(0, 1))]

    half = list(aggregate(
        fwd_blocks, sources, fwd_from, fwd_to, count, 8, ROWS * NODE)
    )
    got_a = [lax.ppermute(half[d], "row", row_hop(0, d)) for d in (1, 2, 3)]
    got_b = [lax.ppermute(half[4 + e], "row", row_hop(e, 0)) for e in (1, 2, 3)]
    n = NODE // 2
    back_count, half[0] = lax.optimization_barrier((count, half[0]))
    bwd_blocks = prepare(vals, back_count, True)
    got_a[0], bwd_blocks = lax.optimization_barrier((got_a[0], bwd_blocks))

    def partial(own_part, got, k):
        cut = slice(k * n, (k + 1) * n)
        return own_part[cut] + got[0][cut] + got[1][cut] + got[2][cut]

    sum_a = [partial(half[0], got_a, k) for k in range(SIDE)]
    sum_b = [partial(half[4], got_b, k) for k in range(SIDE)]
    parts = [sum_a[0]] + [lax.ppermute(sum_a[e], "row", row_hop(e, 0)) for e in (1, 2, 3)]
    parts += [sum_b[0]] + [lax.ppermute(sum_b[d], "row", row_hop(0, d)) for d in (1, 2, 3)]

    output, grad_a, grad_b, sums, gives = middle(
        parts, weight, bias_vector, cotangent, where
    )

    near_a = [grad_a] + [lax.ppermute(grad_a, "row", row_hop(e, 0)) for e in (1, 2, 3)]
    near_b = [grad_b] + [lax.ppermute(grad_b, "row", row_hop(0, d)) for d in (1, 2, 3)]
    near_a = jnp.concatenate(near_a, axis=0)
    near_b = jnp.concatenate(near_b, axis=0)
    near_a, near_b = lax.optimization_barrier((near_a, near_b))
    far_a = [lax.ppermute(near_a, "row", row_hop(0, d)) for d in (1, 3, 2)]
    far_b = [lax.ppermute(near_b, "row", row_hop(e, 0)) for e in (1, 3, 2)]
    column = [near_a, far_a[0], far_a[2], far_a[1], near_b, far_b[0], far_b[2], far_b[1]]

    sums = sums + lax.ppermute(gives, "col", col_hop(0, 1))
    sums = sums.reshape(SIDE, W_ROWS, F)
    got_w = [lax.ppermute(sums[f], "col", col_hop(f, 0)) for f in (1, 2, 3)]
    sums = sums[0] + got_w[0] + got_w[1] + got_w[2]
    got_w = [lax.ppermute(sums, "row", row_hop(0, d)) for d in (1, 3, 2)]
    sums = (sums + got_w[2]) + (got_w[0] + got_w[1])
    bwd_from, sums = lax.optimization_barrier((bwd_from, sums))
    got_w = lax.ppermute(sums, "col", col_hop(0, 1))
    sums = jnp.concatenate([sums, got_w], axis=0)
    keep, give = aggregate(bwd_blocks, column, bwd_from, bwd_to, count, 2, COLS * NODE)
    taken = lax.ppermute(give, "col", col_hop(0, 1))
    got_w = [lax.ppermute(sums, "row", row_hop(e, 0)) for e in (1, 3, 2)]
    sums = (sums + got_w[2]) + (got_w[0] + got_w[1])
    sums_x = [
        keep[k * NODE : (k + 1) * NODE] + taken[k * NODE : (k + 1) * NODE] for k in range(SIDE)
    ]
    got_x = [lax.ppermute(sums_x[f], "col", col_hop(f, 0)) for f in (1, 2, 3)]
    got_w = [lax.ppermute(sums, "col", col_hop(f, 0)) for f in (1, 2, 3)]
    grad_x, grad_w, grad_bias = finish(sums_x[:1] + got_x, [sums] + got_w, where)
    return (output, grad_x, grad_w, grad_bias.reshape(F))


def solution(mesh):
    in_specs = (
        P(("row", "col"), None),
        P(("row", "col")),
        P("row", "col", None, None),
        P("row", "col", None),
        P("row", "col", None),
        P("row", "col"),
        P(),
        P(),
        P(("row", "col"), None),
    )
    out_specs = (P(("row", "col"), None), P(("row", "col"), None), P(), P())

    return jax.shard_map(
        on_device, mesh=mesh, in_specs=in_specs, out_specs=out_specs, check_vma=False
    )
```

profile of v0, /device:TPU:0, one launch (start us, length us, event | category | flops | bytes accessed | tf_op | source)
XLA Modules:
  0.0 206.3 jit_solution(5978797574850040547)
XLA Ops:
  1.3 2.3 %pack.1 = f32[128,2,384]{2,1,0:T(2,128)} custom-call(f32[256,256]{1,0:T(8,128)} %features.1, s32[1,256]{1,0:T(1,128)S(1)} %bitcast.19), custom_call_target="tpu_custom_call" | custom-call | tf_op jit(solution)/shard_map/pack/pallas_call | solution.py:75
  3.6 11.2 %all-to-all-start = ((f32[128,2,384]{2,1,0:T(2,128)}), f32[128,2,384]{2,1,0:T(2,128)S(1)}, u32[]{:S(2)}, u32[]{:S(2)}) async-start(f32[128,2,384]{2,1,0:T(2,128)} %pack.1), calls=%async_computation | async-start | bytes 786432 | tf_op jit(solution)/shard_map/all_to_all | solution.py:392
  15.4 3.0 %prepare.1.refs_3_ = bf16[256,64,256]{2,1,0:T(8,128)(2,1)} custom-call(s32[1]{0:T(128)} %bitcast.12.count, f32[256,4096]{1,0:T(8,128)} %bitcast.21), custom_call_target="tpu_custom_call" | custom-call | flops 100000000 | bytes 12582912 | tf_op jit(solution)/shard_map/prepare/pallas_call | solution.py:144
  18.5 8.6 %all-to-all-done.got = f32[128,2,384]{2,1,0:T(2,128)S(1)} async-done(((f32[128,2,384]{2,1,0:T(2,128)}), f32[128,2,384]{2,1,0:T(2,128)S(1)}, u32[]{:S(2)}, u32[]{:S(2)}) %all-to-all-start) | async-done | bytes 393248 | tf_op jit(solution)/shard_map/all_to_all | solution.py:392
  28.1 1.8 collective-permute-start.3
  29.9 1.3 collective-permute-start.5
  31.2 11.0 %collective-permute-done.1.refs_6_ = f32[256,256]{1,0:T(8,128)S(1)} collective-permute-done((f32[256,256]{1,0:T(8,128)S(1)}, f32[256,256]{1,0:T(8,128)S(1)}, u32[]{:S(2)}, u32[]{:S(2)}) %collective-permute-start.1) | collective-permute-done | bytes 262176 | tf_op jit(solution)/shard_map/ppermute | solution.py:397
  44.5 4.0 %shard_map.120 = (f32[512,256]{1,0:T(8,128)S(1)}, f32[512,256]{1,0:T(8,128)S(1)}, f32[512,256]{1,0:T(8,128)S(1)}, f32[512,256]{1,0:T(8,128)S(1)}, f32[512,256]{1...) custom-call(s32[256]{0:T(256)S(1)} %bitcast.15, s32[256]{0:T(256)S(1)} %bitcast.16, ...), custom_call_target="tpu_custom_call" | custom-call | flops 2147483648 | bytes 16777216 | tf_op jit(solution)/shard_map/pallas_call | solution.py:223
  48.4 7.2 %collective-permute-start.7 = (f32[512,256]{1,0:T(8,128)S(1)}, f32[512,256]{1,0:T(8,128)S(1)}, u32[]{:S(2)}, u32[]{:S(2)}) collective-permute-start(f32[512,256]{1,0:T(8,128)S(1)} %get-tuple-element.36), channel_id=1, source_target_pairs={{0,8},{8,16},{16,24},{24,0},{32,40},{40,48},{48,56},{56,32},{64,72... | collective-permute-start | bytes 1572872 | tf_op jit(solution)/shard_map/ppermute | solution.py:405
  55.6 2.1 %collective-permute-start.8 = (f32[512,256]{1,0:T(8,128)S(1)}, f32[512,256]{1,0:T(8,128)S(1)}, u32[]{:S(2)}, u32[]{:S(2)}) collective-permute-start(f32[512,256]{1,0:T(8,128)S(1)} %get-tuple-element.39), channel_id=1, source_target_pairs={{0,16},{8,24},{16,0},{24,8},{32,48},{40,56},{48,32},{56,40},{64,80... | collective-permute-start | bytes 1572872 | tf_op jit(solution)/shard_map/ppermute | solution.py:405
  57.8 3.1 %collective-permute-start.15 = (f32[512,256]{1,0:T(8,128)S(1)}, f32[512,256]{1,0:T(8,128)S(1)}, u32[]{:S(2)}, u32[]{:S(2)}) collective-permute-start(f32[512,256]{1,0:T(8,128)S(1)} %get-tuple-element.44), channel_id=1, source_target_pairs={{0,96},{8,104},{16,112},{24,120},{32,0},{40,8},{48,16},{56,24},{64... | collective-permute-start | bytes 1572872 | tf_op jit(solution)/shard_map/ppermute | solution.py:406
  60.9 7.0 %collective-permute-done.7 = f32[512,256]{1,0:T(8,128)S(1)} collective-permute-done((f32[512,256]{1,0:T(8,128)S(1)}, f32[512,256]{1,0:T(8,128)S(1)}, u32[]{:S(2)}, u32[]{:S(2)}) %collective-permute-start.7) | collective-permute-done | bytes 524320 | tf_op jit(solution)/shard_map/ppermute | solution.py:405
  67.9 14.1 %collective-permute-start.13 = (f32[512,256]{1,0:T(8,128)S(1)}, f32[512,256]{1,0:T(8,128)S(1)}, u32[]{:S(2)}, u32[]{:S(2)}) collective-permute-start(f32[512,256]{1,0:T(8,128)S(1)} %get-tuple-element.42), channel_id=1, source_target_pairs={{0,32},{8,40},{16,48},{24,56},{32,64},{40,72},{48,80},{56,88},{64,... | collective-permute-start | bytes 1572872 | tf_op jit(solution)/shard_map/ppermute | solution.py:406
  82.0 3.6 %prepare_back.1.refs_3_ = bf16[256,64,256]{2,1,0:T(8,128)(2,1)} custom-call(s32[1]{0:T(128)} %bitcast.11.count, f32[256,4096]{1,0:T(8,128)} %bitcast.22), custom_call_target="tpu_custom_call" | custom-call | flops 100000000 | bytes 12582912 | tf_op jit(solution)/shard_map/prepare_back/pallas_call | solution.py:144
  85.8 8.8 %collective-permute-start.10 = (f32[128,256]{1,0:T(8,128)S(1)}, f32[128,256]{1,0:T(8,128)S(1)}, u32[]{:S(2)}, u32[]{:S(2)}) collective-permute-start(f32[128,256]{1,0:T(8,128)S(1)} %get-tuple-element.70), channel_id=1, source_target_pairs={{0,32},{8,40},{16,48},{24,56},{32,64},{40,72},{48,80},{56,88},{64,... | collective-permute-start | bytes 393224 | tf_op jit(solution)/shard_map/ppermute | solution.py:418
  94.6 2.8 %collective-permute-start.12 = (f32[128,256]{1,0:T(8,128)S(1)}, f32[128,256]{1,0:T(8,128)S(1)}, u32[]{:S(2)}, u32[]{:S(2)}) collective-permute-start(f32[128,256]{1,0:T(8,128)S(1)} %get-tuple-element.68), channel_id=1, source_target_pairs={{0,96},{8,104},{16,112},{24,120},{32,0},{40,8},{48,16},{56,24},{64... | collective-permute-start | bytes 393224 | tf_op jit(solution)/shard_map/ppermute | solution.py:418
  97.6 3.5 %collective-permute-start.17 = (f32[128,256]{1,0:T(8,128)S(1)}, f32[128,256]{1,0:T(8,128)S(1)}, u32[]{:S(2)}, u32[]{:S(2)}) collective-permute-start(f32[128,256]{1,0:T(8,128)S(1)} %get-tuple-element.65), channel_id=1, source_target_pairs={{0,16},{8,24},{16,0},{24,8},{32,48},{40,56},{48,32},{56,40},{64,80... | collective-permute-start | bytes 393224 | tf_op jit(solution)/shard_map/ppermute | solution.py:419
  101.0 2.5 %collective-permute-start.18 = (f32[128,256]{1,0:T(8,128)S(1)}, f32[128,256]{1,0:T(8,128)S(1)}, u32[]{:S(2)}, u32[]{:S(2)}) collective-permute-start(f32[128,256]{1,0:T(8,128)S(1)} %get-tuple-element.64), channel_id=1, source_target_pairs={{0,24},{8,0},{16,8},{24,16},{32,56},{40,32},{48,40},{56,48},{64,88... | collective-permute-start | bytes 393224 | tf_op jit(solution)/shard_map/ppermute | solution.py:419
  103.6 2.1 collective-permute-done.16.refs_6_
  106.3 2.3 %middle.1 = (f32[256,256]{1,0:T(8,128)}, f32[128,256]{1,0:T(8,128)S(1)}, f32[128,256]{1,0:T(8,128)S(1)}, f32[160,256]{1,0:T(8,128)S(1)}, f32[160,256]{1,0:T(8,128)S(1)}) custom-call(s32[2]{0:T(128)S(1)} %pad_add_fusion.refs_0_.where, f32[128,256]{1,0:T(8,128)S(1)} %get-tuple-element.71.refs_1_, f32[128,256]{1,0:T(8,128)S(1)} %collective-permute-done.10.refs_2_, ...), custom_call_target="tpu_custom_call" | custom-call | tf_op jit(solution)/shard_map/middle/pallas_call | solution.py:305
  110.8 3.3 %collective-permute-start.31 = (f32[128,256]{1,0:T(8,128)S(1)}, f32[128,256]{1,0:T(8,128)S(1)}, u32[]{:S(2)}, u32[]{:S(2)}) collective-permute-start(f32[128,256]{1,0:T(8,128)S(1)} %get-tuple-element.51), channel_id=1, source_target_pairs={{0,24},{8,0},{16,8},{24,16},{32,56},{40,32},{48,40},{56,48},{64,88... | collective-permute-start | bytes 393224 | tf_op jit(solution)/shard_map/ppermute | solution.py:426
  114.4 1.1 collective-permute-start.29
  116.2 1.3 collective-permute-done.26
  118.0 2.6 %collective-permute-done.30 = f32[128,256]{1,0:T(8,128)S(1)} collective-permute-done((f32[128,256]{1,0:T(8,128)S(1)}, f32[128,256]{1,0:T(8,128)S(1)}, u32[]{:S(2)}, u32[]{:S(2)}) %collective-permute-start.30) | collective-permute-done | bytes 131104 | tf_op jit(solution)/shard_map/ppermute | solution.py:426
  120.6 1.8 collective-permute-done.29
  124.7 2.0 collective-permute-done.22
  126.7 2.5 %collective-permute-done.21 = f32[40,256]{1,0:T(8,128)S(1)} collective-permute-done((f32[40,256]{1,0:T(8,128)S(1)}, f32[40,256]{1,0:T(8,128)S(1)}, u32[]{:S(2)}, u32[]{:S(2)}) %collective-permute-start.21) | collective-permute-done | bytes 40992 | tf_op jit(solution)/shard_map/ppermute | solution.py:436
  129.6 1.2 collective-permute-start.24
  130.8 2.2 %collective-permute-start.25 = (f32[40,256]{1,0:T(8,128)S(1)}, f32[40,256]{1,0:T(8,128)S(1)}, u32[]{:S(2)}, u32[]{:S(2)}) collective-permute-start(f32[40,256]{1,0:T(8,128)S(1)} %fusion.1), channel_id=1, source_target_pairs={{0,24},{8,0},{16,8},{24,16},{32,56},{40,32},{48,40},{56,48},{64,88... | collective-permute-start | bytes 122888 | tf_op jit(solution)/shard_map/ppermute | solution.py:438
  132.9 1.3 collective-permute-start.23
  134.2 2.2 %collective-permute-start.33 = (f32[512,256]{1,0:T(8,128)S(1)}, f32[512,256]{1,0:T(8,128)S(1)}, u32[]{:S(2)}, u32[]{:S(2)}) collective-permute-start(f32[512,256]{1,0:T(8,128)S(1)} %pad_maximum_fusion.refs_4_), channel_id=1, source_target_pairs={{0,16},{8,24},{16,0},{24,8},{32,48},{40,56},{48,32},{56,40},{64,80... | collective-permute-start | bytes 1572872 | tf_op jit(solution)/shard_map/ppermute | solution.py:430
  136.4 1.9 collective-permute-start.34
  138.3 2.4 %collective-permute-done.25 = f32[40,256]{1,0:T(8,128)S(1)} collective-permute-done((f32[40,256]{1,0:T(8,128)S(1)}, f32[40,256]{1,0:T(8,128)S(1)}, u32[]{:S(2)}, u32[]{:S(2)}) %collective-permute-start.25) | collective-permute-done | bytes 40992 | tf_op jit(solution)/shard_map/ppermute | solution.py:438
  140.7 7.8 %collective-permute-start.35 = (f32[512,256]{1,0:T(8,128)S(1)}, f32[512,256]{1,0:T(8,128)S(1)}, u32[]{:S(2)}, u32[]{:S(2)}) collective-permute-start(f32[512,256]{1,0:T(8,128)S(1)} %pad_maximum_fusion.1.refs_8_), channel_id=1, source_target_pairs={{0,32},{8,40},{16,48},{24,56},{32,64},{40,72},{48,80},{56,88},{64,... | collective-permute-start | bytes 1572872 | tf_op jit(solution)/shard_map/ppermute | solution.py:431
  148.5 2.5 %collective-permute-start.36 = (f32[512,256]{1,0:T(8,128)S(1)}, f32[512,256]{1,0:T(8,128)S(1)}, u32[]{:S(2)}, u32[]{:S(2)}) collective-permute-start(f32[512,256]{1,0:T(8,128)S(1)} %pad_maximum_fusion.1.refs_8_), channel_id=1, source_target_pairs={{0,64},{8,72},{16,80},{24,88},{32,96},{40,104},{48,112},{56,120},{... | collective-permute-start | bytes 1572872 | tf_op jit(solution)/shard_map/ppermute | solution.py:431
  151.0 2.5 %collective-permute-start.37 = (f32[512,256]{1,0:T(8,128)S(1)}, f32[512,256]{1,0:T(8,128)S(1)}, u32[]{:S(2)}, u32[]{:S(2)}) collective-permute-start(f32[512,256]{1,0:T(8,128)S(1)} %pad_maximum_fusion.1.refs_8_), channel_id=1, source_target_pairs={{0,96},{8,104},{16,112},{24,120},{32,0},{40,8},{48,16},{56,24},{64... | collective-permute-start | bytes 1572872 | tf_op jit(solution)/shard_map/ppermute | solution.py:431
  153.6 2.7 %collective-permute-done.34.refs_7_ = f32[512,256]{1,0:T(8,128)S(1)} collective-permute-done((f32[512,256]{1,0:T(8,128)S(1)}, f32[512,256]{1,0:T(8,128)S(1)}, u32[]{:S(2)}, u32[]{:S(2)}) %collective-permute-start.34) | collective-permute-done | bytes 524320 | tf_op jit(solution)/shard_map/ppermute | solution.py:430
  156.3 7.4 %collective-permute-done.36.refs_10_ = f32[512,256]{1,0:T(8,128)S(1)} collective-permute-done((f32[512,256]{1,0:T(8,128)S(1)}, f32[512,256]{1,0:T(8,128)S(1)}, u32[]{:S(2)}, u32[]{:S(2)}) %collective-permute-start.36) | collective-permute-done | bytes 524320 | tf_op jit(solution)/shard_map/ppermute | solution.py:431
  163.7 4.1 %shard_map.121 = (f32[1024,256]{1,0:T(8,128)S(1)}, f32[1024,256]{1,0:T(8,128)S(1)}) custom-call(s32[256]{0:T(256)S(1)} %bitcast.18, s32[256]{0:T(256)S(1)} %bitcast.17, s32[1]{0:T(128)} %bitcast.14.refs_2_, bf16[256,64,256]{2,1,0:T(8,128)(2,1)} %prepare_back.1.refs_3_, f32[512,256]{1,0:T(8,128)S(1)} %pad_maximum_fusion.refs_4_, ...), custom_call_target="tpu_custom_call" | custom-call | flops 2147483648 | bytes 16777216 | tf_op jit(solution)/shard_map/pallas_call | solution.py:223
  168.4 2.2 %collective-permute-done.42 = f32[40,256]{1,0:T(8,128)S(1)} collective-permute-done((f32[40,256]{1,0:T(8,128)S(1)}, f32[40,256]{1,0:T(8,128)S(1)}, u32[]{:S(2)}, u32[]{:S(2)}) %collective-permute-start.42) | collective-permute-done | bytes 40992 | tf_op jit(solution)/shard_map/ppermute | solution.py:441
  170.6 8.6 %collective-permute-start.44 = (f32[80,256]{1,0:T(8,128)S(1)}, f32[80,256]{1,0:T(8,128)S(1)}, u32[]{:S(2)}, u32[]{:S(2)}) collective-permute-start(f32[80,256]{1,0:T(8,128)S(1)} %constant_dynamic-update-slice_fusion), channel_id=1, source_target_pairs={{0,32},{8,40},{16,48},{24,56},{32,64},{40,72},{48,80},{56,88},{64,... | collective-permute-start | bytes 245768 | tf_op jit(solution)/shard_map/ppermute | solution.py:445
  179.2 2.1 %collective-permute-start.43 = (f32[80,256]{1,0:T(8,128)S(1)}, f32[80,256]{1,0:T(8,128)S(1)}, u32[]{:S(2)}, u32[]{:S(2)}) collective-permute-start(f32[80,256]{1,0:T(8,128)S(1)} %constant_dynamic-update-slice_fusion), channel_id=1, source_target_pairs={{0,64},{8,72},{16,80},{24,88},{32,96},{40,104},{48,112},{56,120},{... | collective-permute-start | bytes 245768 | tf_op jit(solution)/shard_map/ppermute | solution.py:445
  181.6 6.8 %collective-permute-start.40 = (f32[256,256]{1,0:T(8,128)S(1)}, f32[256,256]{1,0:T(8,128)S(1)}, u32[]{:S(2)}, u32[]{:S(2)}) collective-permute-start(f32[256,256]{1,0:T(8,128)S(1)} %get-tuple-element.61), channel_id=1, source_target_pairs={{0,4},{1,5},{2,6},{3,7},{4,0},{5,1},{6,2},{7,3},{8,12},{9,13},{10,... | collective-permute-start | bytes 786440 | tf_op jit(solution)/shard_map/ppermute | solution.py:450
  188.5 2.1 %collective-permute-start.46 = (f32[80,256]{1,0:T(8,128)S(1)}, f32[80,256]{1,0:T(8,128)S(1)}, u32[]{:S(2)}, u32[]{:S(2)}) collective-permute-start(f32[80,256]{1,0:T(8,128)S(1)} %add_add_fusion.refs_4_), channel_id=1, source_target_pairs={{0,2},{1,3},{2,4},{3,5},{4,6},{5,7},{6,0},{7,1},{8,10},{9,11},{10,... | collective-permute-start | bytes 245768 | tf_op jit(solution)/shard_map/ppermute | solution.py:451
  191.6 7.4 %collective-permute-done.46.refs_5_ = f32[80,256]{1,0:T(8,128)S(1)} collective-permute-done((f32[80,256]{1,0:T(8,128)S(1)}, f32[80,256]{1,0:T(8,128)S(1)}, u32[]{:S(2)}, u32[]{:S(2)}) %collective-permute-start.46) | collective-permute-done | bytes 81952 | tf_op jit(solution)/shard_map/ppermute | solution.py:451
  199.0 3.8 %collective-permute-start.48 = (f32[80,256]{1,0:T(8,128)S(1)}, f32[80,256]{1,0:T(8,128)S(1)}, u32[]{:S(2)}, u32[]{:S(2)}) collective-permute-start(f32[80,256]{1,0:T(8,128)S(1)} %add_add_fusion.refs_4_), channel_id=1, source_target_pairs={{0,6},{1,7},{2,0},{3,1},{4,2},{5,3},{6,4},{7,5},{8,14},{9,15},{10,... | collective-permute-start | bytes 245768 | tf_op jit(solution)/shard_map/ppermute | solution.py:451
  203.1 1.7 collective-permute-done.48.refs_7_
  204.8 1.5 finish.1
  (87 shorter events, 13.6 us)
Async XLA Ops:
  3.6 23.5 %all-to-all-start = ((f32[128,2,384]{2,1,0:T(2,128)}), f32[128,2,384]{2,1,0:T(2,128)S(1)}, u32[]{:S(2)}, u32[]{:S(2)}) async-start(f32[128,2,384]{2,1,0:T(2,128)} %pack.1), calls=%async_computation | async-start | bytes 786432 | tf_op jit(solution)/shard_map/all_to_all | solution.py:392
  27.7 14.4 %collective-permute-start.1 = (f32[256,256]{1,0:T(8,128)S(1)}, f32[256,256]{1,0:T(8,128)S(1)}, u32[]{:S(2)}, u32[]{:S(2)}) collective-permute-start(f32[256,256]{1,0:T(8,128)S(1)} %place.1.refs_4_), channel_id=1, source_target_pairs={{0,2},{1,3},{2,4},{3,5},{4,6},{5,7},{6,0},{7,1},{8,10},{9,11},{10,... | collective-permute-start | bytes 786440 | tf_op jit(solution)/shard_map/ppermute | solution.py:397
  28.1 14.1 %collective-permute-start.3 = (f32[256,256]{1,0:T(8,128)S(1)}, f32[256,256]{1,0:T(8,128)S(1)}, u32[]{:S(2)}, u32[]{:S(2)}) collective-permute-start(f32[256,256]{1,0:T(8,128)S(1)} %place.1.refs_4_), channel_id=1, source_target_pairs={{0,4},{1,5},{2,6},{3,7},{4,0},{5,1},{6,2},{7,3},{8,12},{9,13},{10,... | collective-permute-start | bytes 786440 | tf_op jit(solution)/shard_map/ppermute | solution.py:397
  29.9 12.9 %collective-permute-start.5 = (f32[256,256]{1,0:T(8,128)S(1)}, f32[256,256]{1,0:T(8,128)S(1)}, u32[]{:S(2)}, u32[]{:S(2)}) collective-permute-start(f32[256,256]{1,0:T(8,128)S(1)} %place.1.refs_4_), channel_id=1, source_target_pairs={{0,6},{1,7},{2,0},{3,1},{4,2},{5,3},{6,4},{7,5},{8,14},{9,15},{10,... | collective-permute-start | bytes 786440 | tf_op jit(solution)/shard_map/ppermute | solution.py:397
  31.2 11.7 %collective-permute-start = (f32[256,256]{1,0:T(8,128)S(1)}, f32[256,256]{1,0:T(8,128)S(1)}, u32[]{:S(2)}, u32[]{:S(2)}) collective-permute-start(f32[256,256]{1,0:T(8,128)S(1)} %place.1.refs_4_), channel_id=1, source_target_pairs={{0,1},{1,0},{2,3},{3,2},{4,5},{5,4},{6,7},{7,6},{8,9},{9,8},{10,11... | collective-permute-start | bytes 786440 | tf_op jit(solution)/shard_map/ppermute | solution.py:400
  42.2 1.9 collective-permute-start.4
  48.4 19.5 %collective-permute-start.7 = (f32[512,256]{1,0:T(8,128)S(1)}, f32[512,256]{1,0:T(8,128)S(1)}, u32[]{:S(2)}, u32[]{:S(2)}) collective-permute-start(f32[512,256]{1,0:T(8,128)S(1)} %get-tuple-element.36), channel_id=1, source_target_pairs={{0,8},{8,16},{16,24},{24,0},{32,40},{40,48},{48,56},{56,32},{64,72... | collective-permute-start | bytes 1572872 | tf_op jit(solution)/shard_map/ppermute | solution.py:405
  55.6 30.0 %collective-permute-start.9 = (f32[512,256]{1,0:T(8,128)S(1)}, f32[512,256]{1,0:T(8,128)S(1)}, u32[]{:S(2)}, u32[]{:S(2)}) collective-permute-start(f32[512,256]{1,0:T(8,128)S(1)} %get-tuple-element.40), channel_id=1, source_target_pairs={{0,24},{8,0},{16,8},{24,16},{32,56},{40,32},{48,40},{56,48},{64,88... | collective-permute-start | bytes 1572872 | tf_op jit(solution)/shard_map/ppermute | solution.py:405
  55.6 30.0 %collective-permute-start.8 = (f32[512,256]{1,0:T(8,128)S(1)}, f32[512,256]{1,0:T(8,128)S(1)}, u32[]{:S(2)}, u32[]{:S(2)}) collective-permute-start(f32[512,256]{1,0:T(8,128)S(1)} %get-tuple-element.39), channel_id=1, source_target_pairs={{0,16},{8,24},{16,0},{24,8},{32,48},{40,56},{48,32},{56,40},{64,80... | collective-permute-start | bytes 1572872 | tf_op jit(solution)/shard_map/ppermute | solution.py:405
  57.8 36.8 %collective-permute-start.15 = (f32[512,256]{1,0:T(8,128)S(1)}, f32[512,256]{1,0:T(8,128)S(1)}, u32[]{:S(2)}, u32[]{:S(2)}) collective-permute-start(f32[512,256]{1,0:T(8,128)S(1)} %get-tuple-element.44), channel_id=1, source_target_pairs={{0,96},{8,104},{16,112},{24,120},{32,0},{40,8},{48,16},{56,24},{64... | collective-permute-start | bytes 1572872 | tf_op jit(solution)/shard_map/ppermute | solution.py:406
  60.9 36.4 %collective-permute-start.14 = (f32[512,256]{1,0:T(8,128)S(1)}, f32[512,256]{1,0:T(8,128)S(1)}, u32[]{:S(2)}, u32[]{:S(2)}) collective-permute-start(f32[512,256]{1,0:T(8,128)S(1)} %get-tuple-element.43), channel_id=1, source_target_pairs={{0,64},{8,72},{16,80},{24,88},{32,96},{40,104},{48,112},{56,120},{... | collective-permute-start | bytes 1572872 | tf_op jit(solution)/shard_map/ppermute | solution.py:406
  67.9 29.4 %collective-permute-start.13 = (f32[512,256]{1,0:T(8,128)S(1)}, f32[512,256]{1,0:T(8,128)S(1)}, u32[]{:S(2)}, u32[]{:S(2)}) collective-permute-start(f32[512,256]{1,0:T(8,128)S(1)} %get-tuple-element.42), channel_id=1, source_target_pairs={{0,32},{8,40},{16,48},{24,56},{32,64},{40,72},{48,80},{56,88},{64,... | collective-permute-start | bytes 1572872 | tf_op jit(solution)/shard_map/ppermute | solution.py:406
  85.8 15.2 %collective-permute-start.10 = (f32[128,256]{1,0:T(8,128)S(1)}, f32[128,256]{1,0:T(8,128)S(1)}, u32[]{:S(2)}, u32[]{:S(2)}) collective-permute-start(f32[128,256]{1,0:T(8,128)S(1)} %get-tuple-element.70), channel_id=1, source_target_pairs={{0,32},{8,40},{16,48},{24,56},{32,64},{40,72},{48,80},{56,88},{64,... | collective-permute-start | bytes 393224 | tf_op jit(solution)/shard_map/ppermute | solution.py:418
  94.5 9.1 %collective-permute-start.11 = (f32[128,256]{1,0:T(8,128)S(1)}, f32[128,256]{1,0:T(8,128)S(1)}, u32[]{:S(2)}, u32[]{:S(2)}) collective-permute-start(f32[128,256]{1,0:T(8,128)S(1)} %get-tuple-element.69), channel_id=1, source_target_pairs={{0,64},{8,72},{16,80},{24,88},{32,96},{40,104},{48,112},{56,120},{... | collective-permute-start | bytes 393224 | tf_op jit(solution)/shard_map/ppermute | solution.py:418
  94.6 9.1 %collective-permute-start.12 = (f32[128,256]{1,0:T(8,128)S(1)}, f32[128,256]{1,0:T(8,128)S(1)}, u32[]{:S(2)}, u32[]{:S(2)}) collective-permute-start(f32[128,256]{1,0:T(8,128)S(1)} %get-tuple-element.68), channel_id=1, source_target_pairs={{0,96},{8,104},{16,112},{24,120},{32,0},{40,8},{48,16},{56,24},{64... | collective-permute-start | bytes 393224 | tf_op jit(solution)/shard_map/ppermute | solution.py:418
  97.5 8.2 %collective-permute-start.16 = (f32[128,256]{1,0:T(8,128)S(1)}, f32[128,256]{1,0:T(8,128)S(1)}, u32[]{:S(2)}, u32[]{:S(2)}) collective-permute-start(f32[128,256]{1,0:T(8,128)S(1)} %get-tuple-element.66), channel_id=1, source_target_pairs={{0,8},{8,16},{16,24},{24,0},{32,40},{40,48},{48,56},{56,32},{64,72... | collective-permute-start | bytes 393224 | tf_op jit(solution)/shard_map/ppermute | solution.py:419
  97.6 8.1 %collective-permute-start.17 = (f32[128,256]{1,0:T(8,128)S(1)}, f32[128,256]{1,0:T(8,128)S(1)}, u32[]{:S(2)}, u32[]{:S(2)}) collective-permute-start(f32[128,256]{1,0:T(8,128)S(1)} %get-tuple-element.65), channel_id=1, source_target_pairs={{0,16},{8,24},{16,0},{24,8},{32,48},{40,56},{48,32},{56,40},{64,80... | collective-permute-start | bytes 393224 | tf_op jit(solution)/shard_map/ppermute | solution.py:419
  101.0 5.3 %collective-permute-start.18 = (f32[128,256]{1,0:T(8,128)S(1)}, f32[128,256]{1,0:T(8,128)S(1)}, u32[]{:S(2)}, u32[]{:S(2)}) collective-permute-start(f32[128,256]{1,0:T(8,128)S(1)} %get-tuple-element.64), channel_id=1, source_target_pairs={{0,24},{8,0},{16,8},{24,16},{32,56},{40,32},{48,40},{56,48},{64,88... | collective-permute-start | bytes 393224 | tf_op jit(solution)/shard_map/ppermute | solution.py:419
  108.6 5.8 %collective-permute-start.28 = (f32[128,256]{1,0:T(8,128)S(1)}, f32[128,256]{1,0:T(8,128)S(1)}, u32[]{:S(2)}, u32[]{:S(2)}) collective-permute-start(f32[128,256]{1,0:T(8,128)S(1)} %get-tuple-element.50), channel_id=1, source_target_pairs={{0,96},{8,104},{16,112},{24,120},{32,0},{40,8},{48,16},{56,24},{64... | collective-permute-start | bytes 393224 | tf_op jit(solution)/shard_map/ppermute | solution.py:425
  109.7 6.6 %collective-permute-start.27 = (f32[128,256]{1,0:T(8,128)S(1)}, f32[128,256]{1,0:T(8,128)S(1)}, u32[]{:S(2)}, u32[]{:S(2)}) collective-permute-start(f32[128,256]{1,0:T(8,128)S(1)} %get-tuple-element.50), channel_id=1, source_target_pairs={{0,64},{8,72},{16,80},{24,88},{32,96},{40,104},{48,112},{56,120},{... | collective-permute-start | bytes 393224 | tf_op jit(solution)/shard_map/ppermute | solution.py:425
  110.0 7.6 %collective-permute-start.26 = (f32[128,256]{1,0:T(8,128)S(1)}, f32[128,256]{1,0:T(8,128)S(1)}, u32[]{:S(2)}, u32[]{:S(2)}) collective-permute-start(f32[128,256]{1,0:T(8,128)S(1)} %get-tuple-element.50), channel_id=1, source_target_pairs={{0,32},{8,40},{16,48},{24,56},{32,64},{40,72},{48,80},{56,88},{64,... | collective-permute-start | bytes 393224 | tf_op jit(solution)/shard_map/ppermute | solution.py:425
  110.8 7.2 %collective-permute-start.31 = (f32[128,256]{1,0:T(8,128)S(1)}, f32[128,256]{1,0:T(8,128)S(1)}, u32[]{:S(2)}, u32[]{:S(2)}) collective-permute-start(f32[128,256]{1,0:T(8,128)S(1)} %get-tuple-element.51), channel_id=1, source_target_pairs={{0,24},{8,0},{16,8},{24,16},{32,56},{40,32},{48,40},{56,48},{64,88... | collective-permute-start | bytes 393224 | tf_op jit(solution)/shard_map/ppermute | solution.py:426
  114.1 6.6 %collective-permute-start.30 = (f32[128,256]{1,0:T(8,128)S(1)}, f32[128,256]{1,0:T(8,128)S(1)}, u32[]{:S(2)}, u32[]{:S(2)}) collective-permute-start(f32[128,256]{1,0:T(8,128)S(1)} %get-tuple-element.51), channel_id=1, source_target_pairs={{0,16},{8,24},{16,0},{24,8},{32,48},{40,56},{48,32},{56,40},{64,80... | collective-permute-start | bytes 393224 | tf_op jit(solution)/shard_map/ppermute | solution.py:426
  114.4 8.0 %collective-permute-start.29 = (f32[128,256]{1,0:T(8,128)S(1)}, f32[128,256]{1,0:T(8,128)S(1)}, u32[]{:S(2)}, u32[]{:S(2)}) collective-permute-start(f32[128,256]{1,0:T(8,128)S(1)} %get-tuple-element.51), channel_id=1, source_target_pairs={{0,8},{8,16},{16,24},{24,0},{32,40},{40,48},{48,56},{56,32},{64,72... | collective-permute-start | bytes 393224 | tf_op jit(solution)/shard_map/ppermute | solution.py:426
  116.2 6.3 %collective-permute-start.19 = (f32[160,256]{1,0:T(8,128)S(1)}, f32[160,256]{1,0:T(8,128)S(1)}, u32[]{:S(2)}, u32[]{:S(2)}) collective-permute-start(f32[160,256]{1,0:T(8,128)S(1)} %get-tuple-element.47), channel_id=1, source_target_pairs={{0,1},{1,0},{2,3},{3,2},{4,5},{5,4},{6,7},{7,6},{8,9},{9,8},{10,11... | collective-permute-start | bytes 491528 | tf_op jit(solution)/shard_map/ppermute | solution.py:434
  122.5 28.6 %collective-permute-start.32 = (f32[512,256]{1,0:T(8,128)S(1)}, f32[512,256]{1,0:T(8,128)S(1)}, u32[]{:S(2)}, u32[]{:S(2)}) collective-permute-start(f32[512,256]{1,0:T(8,128)S(1)} %pad_maximum_fusion.refs_4_), channel_id=1, source_target_pairs={{0,8},{8,16},{16,24},{24,0},{32,40},{40,48},{48,56},{56,32},{64,72... | collective-permute-start | bytes 1572872 | tf_op jit(solution)/shard_map/ppermute | solution.py:430
  122.6 4.1 %collective-permute-start.22 = (f32[40,256]{1,0:T(8,128)S(1)}, f32[40,256]{1,0:T(8,128)S(1)}, u32[]{:S(2)}, u32[]{:S(2)}) collective-permute-start(f32[40,256]{1,0:T(8,128)S(1)} %get-tuple-element.73), channel_id=1, source_target_pairs={{0,6},{1,7},{2,0},{3,1},{4,2},{5,3},{6,4},{7,5},{8,14},{9,15},{10,... | collective-permute-start | bytes 122888 | tf_op jit(solution)/shard_map/ppermute | solution.py:436
  123.6 5.5 %collective-permute-start.21 = (f32[40,256]{1,0:T(8,128)S(1)}, f32[40,256]{1,0:T(8,128)S(1)}, u32[]{:S(2)}, u32[]{:S(2)}) collective-permute-start(f32[40,256]{1,0:T(8,128)S(1)} %get-tuple-element.74), channel_id=1, source_target_pairs={{0,4},{1,5},{2,6},{3,7},{4,0},{5,1},{6,2},{7,3},{8,12},{9,13},{10,... | collective-permute-start | bytes 122888 | tf_op jit(solution)/shard_map/ppermute | solution.py:436
  123.6 5.9 %collective-permute-start.20 = (f32[40,256]{1,0:T(8,128)S(1)}, f32[40,256]{1,0:T(8,128)S(1)}, u32[]{:S(2)}, u32[]{:S(2)}) collective-permute-start(f32[40,256]{1,0:T(8,128)S(1)} %get-tuple-element.72), channel_id=1, source_target_pairs={{0,2},{1,3},{2,4},{3,5},{4,6},{5,7},{6,0},{7,1},{8,10},{9,11},{10,... | collective-permute-start | bytes 122888 | tf_op jit(solution)/shard_map/ppermute | solution.py:436
  129.6 6.8 %collective-permute-start.24 = (f32[40,256]{1,0:T(8,128)S(1)}, f32[40,256]{1,0:T(8,128)S(1)}, u32[]{:S(2)}, u32[]{:S(2)}) collective-permute-start(f32[40,256]{1,0:T(8,128)S(1)} %fusion.1), channel_id=1, source_target_pairs={{0,8},{8,16},{16,24},{24,0},{32,40},{40,48},{48,56},{56,32},{64,72... | collective-permute-start | bytes 122888 | tf_op jit(solution)/shard_map/ppermute | solution.py:438
  130.8 9.9 %collective-permute-start.25 = (f32[40,256]{1,0:T(8,128)S(1)}, f32[40,256]{1,0:T(8,128)S(1)}, u32[]{:S(2)}, u32[]{:S(2)}) collective-permute-start(f32[40,256]{1,0:T(8,128)S(1)} %fusion.1), channel_id=1, source_target_pairs={{0,24},{8,0},{16,8},{24,16},{32,56},{40,32},{48,40},{56,48},{64,88... | collective-permute-start | bytes 122888 | tf_op jit(solution)/shard_map/ppermute | solution.py:438
  132.9 15.6 %collective-permute-start.23 = (f32[40,256]{1,0:T(8,128)S(1)}, f32[40,256]{1,0:T(8,128)S(1)}, u32[]{:S(2)}, u32[]{:S(2)}) collective-permute-start(f32[40,256]{1,0:T(8,128)S(1)} %fusion.1), channel_id=1, source_target_pairs={{0,16},{8,24},{16,0},{24,8},{32,48},{40,56},{48,32},{56,40},{64,80... | collective-permute-start | bytes 122888 | tf_op jit(solution)/shard_map/ppermute | solution.py:438
  134.2 19.4 %collective-permute-start.33 = (f32[512,256]{1,0:T(8,128)S(1)}, f32[512,256]{1,0:T(8,128)S(1)}, u32[]{:S(2)}, u32[]{:S(2)}) collective-permute-start(f32[512,256]{1,0:T(8,128)S(1)} %pad_maximum_fusion.refs_4_), channel_id=1, source_target_pairs={{0,16},{8,24},{16,0},{24,8},{32,48},{40,56},{48,32},{56,40},{64,80... | collective-permute-start | bytes 1572872 | tf_op jit(solution)/shard_map/ppermute | solution.py:430
  136.4 19.9 %collective-permute-start.34 = (f32[512,256]{1,0:T(8,128)S(1)}, f32[512,256]{1,0:T(8,128)S(1)}, u32[]{:S(2)}, u32[]{:S(2)}) collective-permute-start(f32[512,256]{1,0:T(8,128)S(1)} %pad_maximum_fusion.refs_4_), channel_id=1, source_target_pairs={{0,24},{8,0},{16,8},{24,16},{32,56},{40,32},{48,40},{56,48},{64,88... | collective-permute-start | bytes 1572872 | tf_op jit(solution)/shard_map/ppermute | solution.py:430
  140.7 15.6 %collective-permute-start.35 = (f32[512,256]{1,0:T(8,128)S(1)}, f32[512,256]{1,0:T(8,128)S(1)}, u32[]{:S(2)}, u32[]{:S(2)}) collective-permute-start(f32[512,256]{1,0:T(8,128)S(1)} %pad_maximum_fusion.1.refs_8_), channel_id=1, source_target_pairs={{0,32},{8,40},{16,48},{24,56},{32,64},{40,72},{48,80},{56,88},{64,... | collective-permute-start | bytes 1572872 | tf_op jit(solution)/shard_map/ppermute | solution.py:431
  148.5 15.2 %collective-permute-start.36 = (f32[512,256]{1,0:T(8,128)S(1)}, f32[512,256]{1,0:T(8,128)S(1)}, u32[]{:S(2)}, u32[]{:S(2)}) collective-permute-start(f32[512,256]{1,0:T(8,128)S(1)} %pad_maximum_fusion.1.refs_8_), channel_id=1, source_target_pairs={{0,64},{8,72},{16,80},{24,88},{32,96},{40,104},{48,112},{56,120},{... | collective-permute-start | bytes 1572872 | tf_op jit(solution)/shard_map/ppermute | solution.py:431
  151.0 12.7 %collective-permute-start.37 = (f32[512,256]{1,0:T(8,128)S(1)}, f32[512,256]{1,0:T(8,128)S(1)}, u32[]{:S(2)}, u32[]{:S(2)}) collective-permute-start(f32[512,256]{1,0:T(8,128)S(1)} %pad_maximum_fusion.1.refs_8_), channel_id=1, source_target_pairs={{0,96},{8,104},{16,112},{24,120},{32,0},{40,8},{48,16},{56,24},{64... | collective-permute-start | bytes 1572872 | tf_op jit(solution)/shard_map/ppermute | solution.py:431
  167.8 13.6 %collective-permute-start.38 = (f32[1024,256]{1,0:T(8,128)S(1)}, f32[1024,256]{1,0:T(8,128)S(1)}, u32[]{:S(2)}, u32[]{:S(2)}) collective-permute-start(f32[1024,256]{1,0:T(8,128)S(1)} %get-tuple-element.55), channel_id=1, source_target_pairs={{0,1},{1,0},{2,3},{3,2},{4,5},{5,4},{6,7},{7,6},{8,9},{9,8},{10,11... | collective-permute-start | bytes 3145736 | tf_op jit(solution)/shard_map/ppermute | solution.py:444
  167.9 2.7 %collective-permute-start.42 = (f32[40,256]{1,0:T(8,128)S(1)}, f32[40,256]{1,0:T(8,128)S(1)}, u32[]{:S(2)}, u32[]{:S(2)}) collective-permute-start(f32[40,256]{1,0:T(8,128)S(1)} %add_add_fusion.1), channel_id=1, source_target_pairs={{0,1},{1,0},{2,3},{3,2},{4,5},{5,4},{6,7},{7,6},{8,9},{9,8},{10,11... | collective-permute-start | bytes 122888 | tf_op jit(solution)/shard_map/ppermute | solution.py:441
  170.6 17.8 %collective-permute-start.44 = (f32[80,256]{1,0:T(8,128)S(1)}, f32[80,256]{1,0:T(8,128)S(1)}, u32[]{:S(2)}, u32[]{:S(2)}) collective-permute-start(f32[80,256]{1,0:T(8,128)S(1)} %constant_dynamic-update-slice_fusion), channel_id=1, source_target_pairs={{0,32},{8,40},{16,48},{24,56},{32,64},{40,72},{48,80},{56,88},{64,... | collective-permute-start | bytes 245768 | tf_op jit(solution)/shard_map/ppermute | solution.py:445
  179.2 9.2 %collective-permute-start.45 = (f32[80,256]{1,0:T(8,128)S(1)}, f32[80,256]{1,0:T(8,128)S(1)}, u32[]{:S(2)}, u32[]{:S(2)}) collective-permute-start(f32[80,256]{1,0:T(8,128)S(1)} %constant_dynamic-update-slice_fusion), channel_id=1, source_target_pairs={{0,96},{8,104},{16,112},{24,120},{32,0},{40,8},{48,16},{56,24},{64... | collective-permute-start | bytes 245768 | tf_op jit(solution)/shard_map/ppermute | solution.py:445
  179.2 9.2 %collective-permute-start.43 = (f32[80,256]{1,0:T(8,128)S(1)}, f32[80,256]{1,0:T(8,128)S(1)}, u32[]{:S(2)}, u32[]{:S(2)}) collective-permute-start(f32[80,256]{1,0:T(8,128)S(1)} %constant_dynamic-update-slice_fusion), channel_id=1, source_target_pairs={{0,64},{8,72},{16,80},{24,88},{32,96},{40,104},{48,112},{56,120},{... | collective-permute-start | bytes 245768 | tf_op jit(solution)/shard_map/ppermute | solution.py:445
  181.5 23.3 %collective-permute-start.39 = (f32[256,256]{1,0:T(8,128)S(1)}, f32[256,256]{1,0:T(8,128)S(1)}, u32[]{:S(2)}, u32[]{:S(2)}) collective-permute-start(f32[256,256]{1,0:T(8,128)S(1)} %get-tuple-element.62), channel_id=1, source_target_pairs={{0,2},{1,3},{2,4},{3,5},{4,6},{5,7},{6,0},{7,1},{8,10},{9,11},{10,... | collective-permute-start | bytes 786440 | tf_op jit(solution)/shard_map/ppermute | solution.py:450
  181.6 23.2 %collective-permute-start.40 = (f32[256,256]{1,0:T(8,128)S(1)}, f32[256,256]{1,0:T(8,128)S(1)}, u32[]{:S(2)}, u32[]{:S(2)}) collective-permute-start(f32[256,256]{1,0:T(8,128)S(1)} %get-tuple-element.61), channel_id=1, source_target_pairs={{0,4},{1,5},{2,6},{3,7},{4,0},{5,1},{6,2},{7,3},{8,12},{9,13},{10,... | collective-permute-start | bytes 786440 | tf_op jit(solution)/shard_map/ppermute | solution.py:450
  188.4 16.4 %collective-permute-start.41 = (f32[256,256]{1,0:T(8,128)S(1)}, f32[256,256]{1,0:T(8,128)S(1)}, u32[]{:S(2)}, u32[]{:S(2)}) collective-permute-start(f32[256,256]{1,0:T(8,128)S(1)} %get-tuple-element.60), channel_id=1, source_target_pairs={{0,6},{1,7},{2,0},{3,1},{4,2},{5,3},{6,4},{7,5},{8,14},{9,15},{10,... | collective-permute-start | bytes 786440 | tf_op jit(solution)/shard_map/ppermute | solution.py:450
  188.5 10.5 %collective-permute-start.46 = (f32[80,256]{1,0:T(8,128)S(1)}, f32[80,256]{1,0:T(8,128)S(1)}, u32[]{:S(2)}, u32[]{:S(2)}) collective-permute-start(f32[80,256]{1,0:T(8,128)S(1)} %add_add_fusion.refs_4_), channel_id=1, source_target_pairs={{0,2},{1,3},{2,4},{3,5},{4,6},{5,7},{6,0},{7,1},{8,10},{9,11},{10,... | collective-permute-start | bytes 245768 | tf_op jit(solution)/shard_map/ppermute | solution.py:451
  190.6 12.5 %collective-permute-start.47 = (f32[80,256]{1,0:T(8,128)S(1)}, f32[80,256]{1,0:T(8,128)S(1)}, u32[]{:S(2)}, u32[]{:S(2)}) collective-permute-start(f32[80,256]{1,0:T(8,128)S(1)} %add_add_fusion.refs_4_), channel_id=1, source_target_pairs={{0,4},{1,5},{2,6},{3,7},{4,0},{5,1},{6,2},{7,3},{8,12},{9,13},{10,... | collective-permute-start | bytes 245768 | tf_op jit(solution)/shard_map/ppermute | solution.py:451
  199.0 5.9 %collective-permute-start.48 = (f32[80,256]{1,0:T(8,128)S(1)}, f32[80,256]{1,0:T(8,128)S(1)}, u32[]{:S(2)}, u32[]{:S(2)}) collective-permute-start(f32[80,256]{1,0:T(8,128)S(1)} %add_add_fusion.refs_4_), channel_id=1, source_target_pairs={{0,6},{1,7},{2,0},{3,1},{4,2},{5,3},{6,4},{7,5},{8,14},{9,15},{10,... | collective-permute-start | bytes 245768 | tf_op jit(solution)/shard_map/ppermute | solution.py:451
  (8 other events, 160.5 us)
where the time goes:
time: 207 us; the launch traced here: 206 us
  starting transfers between devices  115 us (56%)
  waiting for transfers between devices  66.9 us (32%)
  Pallas kernels  21.4 us (10%)
    ppermute x3, starting transfers between devices, on_device(): got_b = [lax.ppermute(half[4 + e], 'row', row_hop(e, 0)) for e in (1, 2, 3)]  17.2 us
    ppermute x3, starting transfers between devices, on_device(): far_b = [lax.ppermute(near_b, 'row', row_hop(e, 0)) for e in (1, 3, 2)]  12.9 us
    ppermute x3, starting transfers between devices, on_device(): lax.ppermute(sum_a[e], 'row', row_hop(e, 0))  11.5 us
    all_to_all x1, starting transfers between devices, on_device(): lax.all_to_all(sent, ('row', 'col'), split_axis=0, concat_axis=0, tiled=T...  11.2 us
    ppermute x3, waiting for transfers between devices, on_device(): panel = [own] + [lax.ppermute(own, 'col', col_hop(f, 0)) for f in (1, 2, 3)]  11.1 us
    ppermute x3, starting transfers between devices, on_device(): got_w = [lax.ppermute(sums, 'row', row_hop(e, 0)) for e in (1, 3, 2)]  10.8 us
    ppermute x3, waiting for transfers between devices, on_device(): got_w = [lax.ppermute(sums, 'col', col_hop(f, 0)) for f in (1, 2, 3)]  9.43 us
    ppermute x3, starting transfers between devices, on_device(): got_a = [lax.ppermute(half[d], 'row', row_hop(0, d)) for d in (1, 2, 3)]  9.32 us
  transfers between devices with their start and end apart: 50, of which 24 were waited for; matrix products, arithmetic and copies ran while one was open for 0% of the time, Pallas kernels for 3%

commit v1 on v0

--- a/solution.py
+++ b/solution.py
@@ -13,7 +13,8 @@
 BS = 64
 NODE = 256
 SLOTS = 256
-STEP = 32
+STEP = 64
+LEAST = 32
 DEPTH = 192
 ROWS = 16
 COLS = 8
@@ -139,7 +140,7 @@
 
 def prepare(vals, count, flip):
     def at(step, count):
-        return jnp.minimum(step, count[0] // STEP - 1)
+        return jnp.minimum(step, jnp.maximum(count[0] // STEP, 1) - 1)
 
     return pl.pallas_call(
         functools.partial(prepare_kernel, flip),
@@ -152,7 +153,7 @@
             scratch_shapes=[pltpu.VMEM((STEP * 32, LANES), f32)],
         ),
         cost_estimate=pl.CostEstimate(flops=10**8, bytes_accessed=12 << 20, transcendentals=0),
-        compiler_params=room(8),
+        compiler_params=room(12),
         name="prepare_back" if flip else "prepare",
     )(count, pltpu.with_memory_space_constraint(vals, pltpu.HBM))
 
@@ -198,15 +199,22 @@
 
             lax.fori_loop(0, per, one, 0, unroll=2)
 
-    @pl.when(step * STEP < count[0])
-    def _():
-        for slot in range(STEP):
+    def slots(number):
+        for slot in range(number):
             at = step * STEP + slot
             term = jnp.dot(
                 blocks[slot][:, :DEPTH], split[source_at[at]], preferred_element_type=f32
             )
             into = pl.ds(pl.multiple_of(target_at[at] * BS, BS), BS)
             total[into, :] += term
+
+    @pl.when((step + 1) * STEP <= count[0])
+    def _():
+        slots(STEP)
+
+    @pl.when((step == 0) & (count[0] == LEAST))
+    def _():
+        slots(LEAST)
 
     @pl.when(step == pl.num_programs(0) - 1)
     def _():
@@ -229,7 +237,9 @@
             in_specs=[
                 pl.BlockSpec(
                     (STEP, BS, F),
-                    lambda s, a, b, n: (jnp.minimum(s, n[0] // STEP - 1), 0, 0),
+                    lambda s, a, b, n: (
+                        jnp.minimum(s, jnp.maximum(n[0] // STEP, 1) - 1), 0, 0
+                    ),
                 )
             ]
             + [anywhere()] * n_src,
@@ -245,7 +255,7 @@
         cost_estimate=pl.CostEstimate(
             flops=2 * SLOTS * BS * F * F, bytes_accessed=16 << 20, transcendentals=0
         ),
-        compiler_params=room(16),
+        compiler_params=room(18),
     )(
         source_at,
         target_at,

time: 207 us -> 201 us (0.971)
  starting transfers between devices: 115 us -> 106 us
  Pallas kernels: 21.4 us -> 24.2 us
    ppermute x3, starting transfers between devices: 10.8 us -> 6.3 us  [on_device(): got_w = [lax.ppermute(sums, 'row', row_hop(e, 0)) for e in (1, 3, 2)]]
    ppermute x3, waiting for transfers between devices: 2.75 us -> 5.71 us  [on_device(): far_a = [lax.ppermute(near_a, 'row', row_hop(0, d)) for d in (1, 3, 2)]]
    pallas_call x2, Pallas kernels: 6.61 us -> 8.91 us  [prepare(): pl.pallas_call(functools.partial(prepare_kernel, flip), out_shape=pltpu.H...]
    ppermute x3, waiting for transfers between devices: 2.38 us -> 0.28 us  [on_device(): got_w = [lax.ppermute(sums, 'row', row_hop(0, d)) for d in (1, 3, 2)]]
  transfers between devices with their start and end apart: 50 -> 50, of which waited for: 24 -> 22; matrix products, arithmetic and copies ran while one was open for 0% -> 0% of each run, Pallas kernels for 3% -> 4%
where the time goes in v1:
time: 201 us; the launch traced here: 199 us
  starting transfers between devices  106 us (53%)
  waiting for transfers between devices  65.1 us (32%)
  Pallas kernels  24.2 us (12%)
    ppermute x3, starting transfers between devices, on_device(): got_b = [lax.ppermute(half[4 + e], 'row', row_hop(e, 0)) for e in (1, 2, 3)]  17.2 us
    all_to_all x1, starting transfers between devices, on_device(): lax.all_to_all(sent, ('row', 'col'), split_axis=0, concat_axis=0, tiled=T...  11.2 us
    ppermute x3, waiting for transfers between devices, on_device(): panel = [own] + [lax.ppermute(own, 'col', col_hop(f, 0)) for f in (1, 2, 3)]  11.1 us
    ppermute x3, starting transfers between devices, on_device(): far_b = [lax.ppermute(near_b, 'row', row_hop(e, 0)) for e in (1, 3, 2)]  10.9 us
    ppermute x3, starting transfers between devices, on_device(): lax.ppermute(sum_a[e], 'row', row_hop(e, 0))  9.6 us
    pallas_call x2, Pallas kernels, prepare(): pl.pallas_call(functools.partial(prepare_kernel, flip), out_shape=pltpu.H...  8.91 us
    pallas_call x2, Pallas kernels, aggregate(): pl.pallas_call(functools.partial(aggregate_kernel, n_src, n_dst), out_sha...  8.58 us
    ppermute x3, starting transfers between devices, on_device(): got_w = [lax.ppermute(sums, 'col', col_hop(f, 0)) for f in (1, 2, 3)]  8.53 us
  transfers between devices with their start and end apart: 50, of which 22 were waited for; matrix products, arithmetic and copies ran while one was open for 0% of the time, Pallas kernels for 4%

profile of v1, /device:TPU:0, one launch (start us, length us, event | category | flops | bytes accessed | tf_op | source)
XLA Modules:
  0.0 198.6 jit_solution(11716726787446135598)
XLA Ops:
  1.3 2.3 %pack.1 = f32[128,2,384]{2,1,0:T(2,128)} custom-call(f32[256,256]{1,0:T(8,128)} %features.1, s32[1,256]{1,0:T(1,128)S(1)} %bitcast.19), custom_call_target="tpu_custom_call" | custom-call | tf_op jit(solution)/shard_map/pack/pallas_call | solution.py:76
  3.6 11.2 %all-to-all-start = ((f32[128,2,384]{2,1,0:T(2,128)}), f32[128,2,384]{2,1,0:T(2,128)S(1)}, u32[]{:S(2)}, u32[]{:S(2)}) async-start(f32[128,2,384]{2,1,0:T(2,128)} %pack.1), calls=%async_computation | async-start | bytes 786432 | tf_op jit(solution)/shard_map/all_to_all | solution.py:402
  15.4 3.9 %prepare.1.refs_3_ = bf16[256,64,256]{2,1,0:T(8,128)(2,1)} custom-call(s32[1]{0:T(128)} %bitcast.12.count, f32[256,4096]{1,0:T(8,128)} %bitcast.21), custom_call_target="tpu_custom_call" | custom-call | flops 100000000 | bytes 12582912 | tf_op jit(solution)/shard_map/prepare/pallas_call | solution.py:145
  19.3 7.8 %all-to-all-done.got = f32[128,2,384]{2,1,0:T(2,128)S(1)} async-done(((f32[128,2,384]{2,1,0:T(2,128)}), f32[128,2,384]{2,1,0:T(2,128)S(1)}, u32[]{:S(2)}, u32[]{:S(2)}) %all-to-all-start) | async-done | bytes 393248 | tf_op jit(solution)/shard_map/all_to_all | solution.py:402
  28.1 1.7 collective-permute-start.3
  29.8 1.4 collective-permute-start.5
  31.2 11.0 %collective-permute-done.1.refs_6_ = f32[256,256]{1,0:T(8,128)S(1)} collective-permute-done((f32[256,256]{1,0:T(8,128)S(1)}, f32[256,256]{1,0:T(8,128)S(1)}, u32[]{:S(2)}, u32[]{:S(2)}) %collective-permute-start.1) | collective-permute-done | bytes 262176 | tf_op jit(solution)/shard_map/ppermute | solution.py:407
  44.5 4.2 %shard_map.120 = (f32[512,256]{1,0:T(8,128)S(1)}, f32[512,256]{1,0:T(8,128)S(1)}, f32[512,256]{1,0:T(8,128)S(1)}, f32[512,256]{1,0:T(8,128)S(1)}, f32[512,256]{1...) custom-call(s32[256]{0:T(256)S(1)} %bitcast.15, s32[256]{0:T(256)S(1)} %bitcast.16, ...), custom_call_target="tpu_custom_call" | custom-call | flops 2147483648 | bytes 16777216 | tf_op jit(solution)/shard_map/pallas_call | solution.py:231
  48.7 5.3 %collective-permute-start.7 = (f32[512,256]{1,0:T(8,128)S(1)}, f32[512,256]{1,0:T(8,128)S(1)}, u32[]{:S(2)}, u32[]{:S(2)}) collective-permute-start(f32[512,256]{1,0:T(8,128)S(1)} %get-tuple-element.36), channel_id=1, source_target_pairs={{0,8},{8,16},{16,24},{24,0},{32,40},{40,48},{48,56},{56,32},{64,72... | collective-permute-start | bytes 1572872 | tf_op jit(solution)/shard_map/ppermute | solution.py:415
  54.0 2.1 %collective-permute-start.8 = (f32[512,256]{1,0:T(8,128)S(1)}, f32[512,256]{1,0:T(8,128)S(1)}, u32[]{:S(2)}, u32[]{:S(2)}) collective-permute-start(f32[512,256]{1,0:T(8,128)S(1)} %get-tuple-element.39), channel_id=1, source_target_pairs={{0,16},{8,24},{16,0},{24,8},{32,48},{40,56},{48,32},{56,40},{64,80... | collective-permute-start | bytes 1572872 | tf_op jit(solution)/shard_map/ppermute | solution.py:415
  56.1 2.0 %collective-permute-start.15 = (f32[512,256]{1,0:T(8,128)S(1)}, f32[512,256]{1,0:T(8,128)S(1)}, u32[]{:S(2)}, u32[]{:S(2)}) collective-permute-start(f32[512,256]{1,0:T(8,128)S(1)} %get-tuple-element.44), channel_id=1, source_target_pairs={{0,96},{8,104},{16,112},{24,120},{32,0},{40,8},{48,16},{56,24},{64... | collective-permute-start | bytes 1572872 | tf_op jit(solution)/shard_map/ppermute | solution.py:416
  58.2 1.1 collective-permute-start.14
  59.3 7.0 %collective-permute-done.7 = f32[512,256]{1,0:T(8,128)S(1)} collective-permute-done((f32[512,256]{1,0:T(8,128)S(1)}, f32[512,256]{1,0:T(8,128)S(1)}, u32[]{:S(2)}, u32[]{:S(2)}) %collective-permute-start.7) | collective-permute-done | bytes 524320 | tf_op jit(solution)/shard_map/ppermute | solution.py:415
  66.3 14.1 %collective-permute-start.13 = (f32[512,256]{1,0:T(8,128)S(1)}, f32[512,256]{1,0:T(8,128)S(1)}, u32[]{:S(2)}, u32[]{:S(2)}) collective-permute-start(f32[512,256]{1,0:T(8,128)S(1)} %get-tuple-element.42), channel_id=1, source_target_pairs={{0,32},{8,40},{16,48},{24,56},{32,64},{40,72},{48,80},{56,88},{64,... | collective-permute-start | bytes 1572872 | tf_op jit(solution)/shard_map/ppermute | solution.py:416
  80.4 5.0 %prepare_back.1.refs_3_ = bf16[256,64,256]{2,1,0:T(8,128)(2,1)} custom-call(s32[1]{0:T(128)} %bitcast.11.count, f32[256,4096]{1,0:T(8,128)} %bitcast.22), custom_call_target="tpu_custom_call" | custom-call | flops 100000000 | bytes 12582912 | tf_op jit(solution)/shard_map/prepare_back/pallas_call | solution.py:145
  85.6 6.8 %collective-permute-start.10 = (f32[128,256]{1,0:T(8,128)S(1)}, f32[128,256]{1,0:T(8,128)S(1)}, u32[]{:S(2)}, u32[]{:S(2)}) collective-permute-start(f32[128,256]{1,0:T(8,128)S(1)} %get-tuple-element.70), channel_id=1, source_target_pairs={{0,32},{8,40},{16,48},{24,56},{32,64},{40,72},{48,80},{56,88},{64,... | collective-permute-start | bytes 393224 | tf_op jit(solution)/shard_map/ppermute | solution.py:428
  92.4 2.8 %collective-permute-start.12 = (f32[128,256]{1,0:T(8,128)S(1)}, f32[128,256]{1,0:T(8,128)S(1)}, u32[]{:S(2)}, u32[]{:S(2)}) collective-permute-start(f32[128,256]{1,0:T(8,128)S(1)} %get-tuple-element.68), channel_id=1, source_target_pairs={{0,96},{8,104},{16,112},{24,120},{32,0},{40,8},{48,16},{56,24},{64... | collective-permute-start | bytes 393224 | tf_op jit(solution)/shard_map/ppermute | solution.py:428
  95.4 2.4 %collective-permute-start.17 = (f32[128,256]{1,0:T(8,128)S(1)}, f32[128,256]{1,0:T(8,128)S(1)}, u32[]{:S(2)}, u32[]{:S(2)}) collective-permute-start(f32[128,256]{1,0:T(8,128)S(1)} %get-tuple-element.65), channel_id=1, source_target_pairs={{0,16},{8,24},{16,0},{24,8},{32,48},{40,56},{48,32},{56,40},{64,80... | collective-permute-start | bytes 393224 | tf_op jit(solution)/shard_map/ppermute | solution.py:429
  97.8 2.5 %collective-permute-start.18 = (f32[128,256]{1,0:T(8,128)S(1)}, f32[128,256]{1,0:T(8,128)S(1)}, u32[]{:S(2)}, u32[]{:S(2)}) collective-permute-start(f32[128,256]{1,0:T(8,128)S(1)} %get-tuple-element.64), channel_id=1, source_target_pairs={{0,24},{8,0},{16,8},{24,16},{32,56},{40,32},{48,40},{56,48},{64,88... | collective-permute-start | bytes 393224 | tf_op jit(solution)/shard_map/ppermute | solution.py:429
  100.4 3.1 %collective-permute-done.16.refs_6_ = f32[128,256]{1,0:T(8,128)S(1)} collective-permute-done((f32[128,256]{1,0:T(8,128)S(1)}, f32[128,256]{1,0:T(8,128)S(1)}, u32[]{:S(2)}, u32[]{:S(2)}) %collective-permute-start.16) | collective-permute-done | bytes 131104 | tf_op jit(solution)/shard_map/ppermute | solution.py:429
  104.2 2.3 %middle.1 = (f32[256,256]{1,0:T(8,128)}, f32[128,256]{1,0:T(8,128)S(1)}, f32[128,256]{1,0:T(8,128)S(1)}, f32[160,256]{1,0:T(8,128)S(1)}, f32[160,256]{1,0:T(8,128)S(1)}) custom-call(s32[2]{0:T(128)S(1)} %pad_add_fusion.refs_0_.where, f32[128,256]{1,0:T(8,128)S(1)} %get-tuple-element.71.refs_1_, f32[128,256]{1,0:T(8,128)S(1)} %collective-permute-done.10.refs_2_, ...), custom_call_target="tpu_custom_call" | custom-call | tf_op jit(solution)/shard_map/middle/pallas_call | solution.py:315
  106.5 1.1 collective-permute-start.28
  108.7 2.5 %collective-permute-start.31 = (f32[128,256]{1,0:T(8,128)S(1)}, f32[128,256]{1,0:T(8,128)S(1)}, u32[]{:S(2)}, u32[]{:S(2)}) collective-permute-start(f32[128,256]{1,0:T(8,128)S(1)} %get-tuple-element.51), channel_id=1, source_target_pairs={{0,24},{8,0},{16,8},{24,16},{32,56},{40,32},{48,40},{56,48},{64,88... | collective-permute-start | bytes 393224 | tf_op jit(solution)/shard_map/ppermute | solution.py:436
  112.8 1.4 collective-permute-done.27
  114.2 1.3 collective-permute-done.26
  115.5 2.2 %collective-permute-done.30 = f32[128,256]{1,0:T(8,128)S(1)} collective-permute-done((f32[128,256]{1,0:T(8,128)S(1)}, f32[128,256]{1,0:T(8,128)S(1)}, u32[]{:S(2)}, u32[]{:S(2)}) %collective-permute-start.30) | collective-permute-done | bytes 131104 | tf_op jit(solution)/shard_map/ppermute | solution.py:436
  117.8 1.7 collective-permute-done.29
  119.6 2.7 %collective-permute-start.22 = (f32[40,256]{1,0:T(8,128)S(1)}, f32[40,256]{1,0:T(8,128)S(1)}, u32[]{:S(2)}, u32[]{:S(2)}) collective-permute-start(f32[40,256]{1,0:T(8,128)S(1)} %get-tuple-element.73), channel_id=1, source_target_pairs={{0,6},{1,7},{2,0},{3,1},{4,2},{5,3},{6,4},{7,5},{8,14},{9,15},{10,... | collective-permute-start | bytes 122888 | tf_op jit(solution)/shard_map/ppermute | solution.py:446
  123.9 3.9 %collective-permute-done.21 = f32[40,256]{1,0:T(8,128)S(1)} collective-permute-done((f32[40,256]{1,0:T(8,128)S(1)}, f32[40,256]{1,0:T(8,128)S(1)}, u32[]{:S(2)}, u32[]{:S(2)}) %collective-permute-start.21) | collective-permute-done | bytes 40992 | tf_op jit(solution)/shard_map/ppermute | solution.py:446
  128.7 2.6 %collective-permute-start.25 = (f32[40,256]{1,0:T(8,128)S(1)}, f32[40,256]{1,0:T(8,128)S(1)}, u32[]{:S(2)}, u32[]{:S(2)}) collective-permute-start(f32[40,256]{1,0:T(8,128)S(1)} %fusion.1), channel_id=1, source_target_pairs={{0,24},{8,0},{16,8},{24,16},{32,56},{40,32},{48,40},{56,48},{64,88... | collective-permute-start | bytes 122888 | tf_op jit(solution)/shard_map/ppermute | solution.py:448
  131.3 1.7 collective-permute-start.23
  133.0 1.8 collective-permute-start.33
  135.1 1.7 collective-permute-start.34
  136.8 2.4 %collective-permute-start.35 = (f32[512,256]{1,0:T(8,128)S(1)}, f32[512,256]{1,0:T(8,128)S(1)}, u32[]{:S(2)}, u32[]{:S(2)}) collective-permute-start(f32[512,256]{1,0:T(8,128)S(1)} %pad_maximum_fusion.1.refs_8_), channel_id=1, source_target_pairs={{0,32},{8,40},{16,48},{24,56},{32,64},{40,72},{48,80},{56,88},{64,... | collective-permute-start | bytes 1572872 | tf_op jit(solution)/shard_map/ppermute | solution.py:441
  139.2 8.5 %collective-permute-start.36 = (f32[512,256]{1,0:T(8,128)S(1)}, f32[512,256]{1,0:T(8,128)S(1)}, u32[]{:S(2)}, u32[]{:S(2)}) collective-permute-start(f32[512,256]{1,0:T(8,128)S(1)} %pad_maximum_fusion.1.refs_8_), channel_id=1, source_target_pairs={{0,64},{8,72},{16,80},{24,88},{32,96},{40,104},{48,112},{56,120},{... | collective-permute-start | bytes 1572872 | tf_op jit(solution)/shard_map/ppermute | solution.py:441
  147.7 5.7 %collective-permute-done.34.refs_7_ = f32[512,256]{1,0:T(8,128)S(1)} collective-permute-done((f32[512,256]{1,0:T(8,128)S(1)}, f32[512,256]{1,0:T(8,128)S(1)}, u32[]{:S(2)}, u32[]{:S(2)}) %collective-permute-start.34) | collective-permute-done | bytes 524320 | tf_op jit(solution)/shard_map/ppermute | solution.py:440
  153.4 7.0 %collective-permute-done.36.refs_10_ = f32[512,256]{1,0:T(8,128)S(1)} collective-permute-done((f32[512,256]{1,0:T(8,128)S(1)}, f32[512,256]{1,0:T(8,128)S(1)}, u32[]{:S(2)}, u32[]{:S(2)}) %collective-permute-start.36) | collective-permute-done | bytes 524320 | tf_op jit(solution)/shard_map/ppermute | solution.py:441
  160.4 4.3 %shard_map.121 = (f32[1024,256]{1,0:T(8,128)S(1)}, f32[1024,256]{1,0:T(8,128)S(1)}) custom-call(s32[256]{0:T(256)S(1)} %bitcast.18, s32[256]{0:T(256)S(1)} %bitcast.17, s32[1]{0:T(128)} %bitcast.14.refs_2_, bf16[256,64,256]{2,1,0:T(8,128)(2,1)} %prepare_back.1.refs_3_, f32[512,256]{1,0:T(8,128)S(1)} %pad_maximum_fusion.refs_4_, ...), custom_call_target="tpu_custom_call" | custom-call | flops 2147483648 | bytes 16777216 | tf_op jit(solution)/shard_map/pallas_call | solution.py:231
  165.4 2.2 %collective-permute-done.42 = f32[40,256]{1,0:T(8,128)S(1)} collective-permute-done((f32[40,256]{1,0:T(8,128)S(1)}, f32[40,256]{1,0:T(8,128)S(1)}, u32[]{:S(2)}, u32[]{:S(2)}) %collective-permute-start.42) | collective-permute-done | bytes 40992 | tf_op jit(solution)/shard_map/ppermute | solution.py:451
  167.6 4.2 %collective-permute-start.44 = (f32[80,256]{1,0:T(8,128)S(1)}, f32[80,256]{1,0:T(8,128)S(1)}, u32[]{:S(2)}, u32[]{:S(2)}) collective-permute-start(f32[80,256]{1,0:T(8,128)S(1)} %constant_dynamic-update-slice_fusion), channel_id=1, source_target_pairs={{0,32},{8,40},{16,48},{24,56},{32,64},{40,72},{48,80},{56,88},{64,... | collective-permute-start | bytes 245768 | tf_op jit(solution)/shard_map/ppermute | solution.py:455
  171.8 2.1 %collective-permute-start.43 = (f32[80,256]{1,0:T(8,128)S(1)}, f32[80,256]{1,0:T(8,128)S(1)}, u32[]{:S(2)}, u32[]{:S(2)}) collective-permute-start(f32[80,256]{1,0:T(8,128)S(1)} %constant_dynamic-update-slice_fusion), channel_id=1, source_target_pairs={{0,64},{8,72},{16,80},{24,88},{32,96},{40,104},{48,112},{56,120},{... | collective-permute-start | bytes 245768 | tf_op jit(solution)/shard_map/ppermute | solution.py:455
  174.2 6.3 %collective-permute-start.40 = (f32[256,256]{1,0:T(8,128)S(1)}, f32[256,256]{1,0:T(8,128)S(1)}, u32[]{:S(2)}, u32[]{:S(2)}) collective-permute-start(f32[256,256]{1,0:T(8,128)S(1)} %get-tuple-element.61), channel_id=1, source_target_pairs={{0,4},{1,5},{2,6},{3,7},{4,0},{5,1},{6,2},{7,3},{8,12},{9,13},{10,... | collective-permute-start | bytes 786440 | tf_op jit(solution)/shard_map/ppermute | solution.py:460
  181.2 1.4 collective-permute-start.46
  182.6 3.6 %collective-permute-start.47 = (f32[80,256]{1,0:T(8,128)S(1)}, f32[80,256]{1,0:T(8,128)S(1)}, u32[]{:S(2)}, u32[]{:S(2)}) collective-permute-start(f32[80,256]{1,0:T(8,128)S(1)} %add_add_fusion.refs_4_), channel_id=1, source_target_pairs={{0,4},{1,5},{2,6},{3,7},{4,0},{5,1},{6,2},{7,3},{8,12},{9,13},{10,... | collective-permute-start | bytes 245768 | tf_op jit(solution)/shard_map/ppermute | solution.py:461
  186.2 5.3 %collective-permute-done.46.refs_5_ = f32[80,256]{1,0:T(8,128)S(1)} collective-permute-done((f32[80,256]{1,0:T(8,128)S(1)}, f32[80,256]{1,0:T(8,128)S(1)}, u32[]{:S(2)}, u32[]{:S(2)}) %collective-permute-start.46) | collective-permute-done | bytes 81952 | tf_op jit(solution)/shard_map/ppermute | solution.py:461
  191.6 3.5 %collective-permute-start.48 = (f32[80,256]{1,0:T(8,128)S(1)}, f32[80,256]{1,0:T(8,128)S(1)}, u32[]{:S(2)}, u32[]{:S(2)}) collective-permute-start(f32[80,256]{1,0:T(8,128)S(1)} %add_add_fusion.refs_4_), channel_id=1, source_target_pairs={{0,6},{1,7},{2,0},{3,1},{4,2},{5,3},{6,4},{7,5},{8,14},{9,15},{10,... | collective-permute-start | bytes 245768 | tf_op jit(solution)/shard_map/ppermute | solution.py:461
  195.4 1.7 collective-permute-done.48.refs_7_
  197.2 1.5 finish.1
  (87 shorter events, 12.7 us)
Async XLA Ops:
  3.6 23.5 %all-to-all-start = ((f32[128,2,384]{2,1,0:T(2,128)}), f32[128,2,384]{2,1,0:T(2,128)S(1)}, u32[]{:S(2)}, u32[]{:S(2)}) async-start(f32[128,2,384]{2,1,0:T(2,128)} %pack.1), calls=%async_computation | async-start | bytes 786432 | tf_op jit(solution)/shard_map/all_to_all | solution.py:402
  27.7 14.4 %collective-permute-start.1 = (f32[256,256]{1,0:T(8,128)S(1)}, f32[256,256]{1,0:T(8,128)S(1)}, u32[]{:S(2)}, u32[]{:S(2)}) collective-permute-start(f32[256,256]{1,0:T(8,128)S(1)} %place.1.refs_4_), channel_id=1, source_target_pairs={{0,2},{1,3},{2,4},{3,5},{4,6},{5,7},{6,0},{7,1},{8,10},{9,11},{10,... | collective-permute-start | bytes 786440 | tf_op jit(solution)/shard_map/ppermute | solution.py:407
  28.1 14.1 %collective-permute-start.3 = (f32[256,256]{1,0:T(8,128)S(1)}, f32[256,256]{1,0:T(8,128)S(1)}, u32[]{:S(2)}, u32[]{:S(2)}) collective-permute-start(f32[256,256]{1,0:T(8,128)S(1)} %place.1.refs_4_), channel_id=1, source_target_pairs={{0,4},{1,5},{2,6},{3,7},{4,0},{5,1},{6,2},{7,3},{8,12},{9,13},{10,... | collective-permute-start | bytes 786440 | tf_op jit(solution)/shard_map/ppermute | solution.py:407
  29.8 13.0 %collective-permute-start.5 = (f32[256,256]{1,0:T(8,128)S(1)}, f32[256,256]{1,0:T(8,128)S(1)}, u32[]{:S(2)}, u32[]{:S(2)}) collective-permute-start(f32[256,256]{1,0:T(8,128)S(1)} %place.1.refs_4_), channel_id=1, source_target_pairs={{0,6},{1,7},{2,0},{3,1},{4,2},{5,3},{6,4},{7,5},{8,14},{9,15},{10,... | collective-permute-start | bytes 786440 | tf_op jit(solution)/shard_map/ppermute | solution.py:407
  31.2 11.7 %collective-permute-start = (f32[256,256]{1,0:T(8,128)S(1)}, f32[256,256]{1,0:T(8,128)S(1)}, u32[]{:S(2)}, u32[]{:S(2)}) collective-permute-start(f32[256,256]{1,0:T(8,128)S(1)} %place.1.refs_4_), channel_id=1, source_target_pairs={{0,1},{1,0},{2,3},{3,2},{4,5},{5,4},{6,7},{7,6},{8,9},{9,8},{10,11... | collective-permute-start | bytes 786440 | tf_op jit(solution)/shard_map/ppermute | solution.py:410
  42.2 1.9 collective-permute-start.4
  48.7 17.6 %collective-permute-start.7 = (f32[512,256]{1,0:T(8,128)S(1)}, f32[512,256]{1,0:T(8,128)S(1)}, u32[]{:S(2)}, u32[]{:S(2)}) collective-permute-start(f32[512,256]{1,0:T(8,128)S(1)} %get-tuple-element.36), channel_id=1, source_target_pairs={{0,8},{8,16},{16,24},{24,0},{32,40},{40,48},{48,56},{56,32},{64,72... | collective-permute-start | bytes 1572872 | tf_op jit(solution)/shard_map/ppermute | solution.py:415
  54.0 31.4 %collective-permute-start.9 = (f32[512,256]{1,0:T(8,128)S(1)}, f32[512,256]{1,0:T(8,128)S(1)}, u32[]{:S(2)}, u32[]{:S(2)}) collective-permute-start(f32[512,256]{1,0:T(8,128)S(1)} %get-tuple-element.40), channel_id=1, source_target_pairs={{0,24},{8,0},{16,8},{24,16},{32,56},{40,32},{48,40},{56,48},{64,88... | collective-permute-start | bytes 1572872 | tf_op jit(solution)/shard_map/ppermute | solution.py:415
  54.0 31.4 %collective-permute-start.8 = (f32[512,256]{1,0:T(8,128)S(1)}, f32[512,256]{1,0:T(8,128)S(1)}, u32[]{:S(2)}, u32[]{:S(2)}) collective-permute-start(f32[512,256]{1,0:T(8,128)S(1)} %get-tuple-element.39), channel_id=1, source_target_pairs={{0,16},{8,24},{16,0},{24,8},{32,48},{40,56},{48,32},{56,40},{64,80... | collective-permute-start | bytes 1572872 | tf_op jit(solution)/shard_map/ppermute | solution.py:415
  56.1 36.3 %collective-permute-start.15 = (f32[512,256]{1,0:T(8,128)S(1)}, f32[512,256]{1,0:T(8,128)S(1)}, u32[]{:S(2)}, u32[]{:S(2)}) collective-permute-start(f32[512,256]{1,0:T(8,128)S(1)} %get-tuple-element.44), channel_id=1, source_target_pairs={{0,96},{8,104},{16,112},{24,120},{32,0},{40,8},{48,16},{56,24},{64... | collective-permute-start | bytes 1572872 | tf_op jit(solution)/shard_map/ppermute | solution.py:416
  58.2 37.0 %collective-permute-start.14 = (f32[512,256]{1,0:T(8,128)S(1)}, f32[512,256]{1,0:T(8,128)S(1)}, u32[]{:S(2)}, u32[]{:S(2)}) collective-permute-start(f32[512,256]{1,0:T(8,128)S(1)} %get-tuple-element.43), channel_id=1, source_target_pairs={{0,64},{8,72},{16,80},{24,88},{32,96},{40,104},{48,112},{56,120},{... | collective-permute-start | bytes 1572872 | tf_op jit(solution)/shard_map/ppermute | solution.py:416
  66.3 28.9 %collective-permute-start.13 = (f32[512,256]{1,0:T(8,128)S(1)}, f32[512,256]{1,0:T(8,128)S(1)}, u32[]{:S(2)}, u32[]{:S(2)}) collective-permute-start(f32[512,256]{1,0:T(8,128)S(1)} %get-tuple-element.42), channel_id=1, source_target_pairs={{0,32},{8,40},{16,48},{24,56},{32,64},{40,72},{48,80},{56,88},{64,... | collective-permute-start | bytes 1572872 | tf_op jit(solution)/shard_map/ppermute | solution.py:416
  85.6 12.2 %collective-permute-start.10 = (f32[128,256]{1,0:T(8,128)S(1)}, f32[128,256]{1,0:T(8,128)S(1)}, u32[]{:S(2)}, u32[]{:S(2)}) collective-permute-start(f32[128,256]{1,0:T(8,128)S(1)} %get-tuple-element.70), channel_id=1, source_target_pairs={{0,32},{8,40},{16,48},{24,56},{32,64},{40,72},{48,80},{56,88},{64,... | collective-permute-start | bytes 393224 | tf_op jit(solution)/shard_map/ppermute | solution.py:428
  92.4 8.0 %collective-permute-start.11 = (f32[128,256]{1,0:T(8,128)S(1)}, f32[128,256]{1,0:T(8,128)S(1)}, u32[]{:S(2)}, u32[]{:S(2)}) collective-permute-start(f32[128,256]{1,0:T(8,128)S(1)} %get-tuple-element.69), channel_id=1, source_target_pairs={{0,64},{8,72},{16,80},{24,88},{32,96},{40,104},{48,112},{56,120},{... | collective-permute-start | bytes 393224 | tf_op jit(solution)/shard_map/ppermute | solution.py:428
  92.4 8.0 %collective-permute-start.12 = (f32[128,256]{1,0:T(8,128)S(1)}, f32[128,256]{1,0:T(8,128)S(1)}, u32[]{:S(2)}, u32[]{:S(2)}) collective-permute-start(f32[128,256]{1,0:T(8,128)S(1)} %get-tuple-element.68), channel_id=1, source_target_pairs={{0,96},{8,104},{16,112},{24,120},{32,0},{40,8},{48,16},{56,24},{64... | collective-permute-start | bytes 393224 | tf_op jit(solution)/shard_map/ppermute | solution.py:428
  95.3 8.2 %collective-permute-start.16 = (f32[128,256]{1,0:T(8,128)S(1)}, f32[128,256]{1,0:T(8,128)S(1)}, u32[]{:S(2)}, u32[]{:S(2)}) collective-permute-start(f32[128,256]{1,0:T(8,128)S(1)} %get-tuple-element.66), channel_id=1, source_target_pairs={{0,8},{8,16},{16,24},{24,0},{32,40},{40,48},{48,56},{56,32},{64,72... | collective-permute-start | bytes 393224 | tf_op jit(solution)/shard_map/ppermute | solution.py:429
  95.4 8.1 %collective-permute-start.17 = (f32[128,256]{1,0:T(8,128)S(1)}, f32[128,256]{1,0:T(8,128)S(1)}, u32[]{:S(2)}, u32[]{:S(2)}) collective-permute-start(f32[128,256]{1,0:T(8,128)S(1)} %get-tuple-element.65), channel_id=1, source_target_pairs={{0,16},{8,24},{16,0},{24,8},{32,48},{40,56},{48,32},{56,40},{64,80... | collective-permute-start | bytes 393224 | tf_op jit(solution)/shard_map/ppermute | solution.py:429
  97.8 6.4 %collective-permute-start.18 = (f32[128,256]{1,0:T(8,128)S(1)}, f32[128,256]{1,0:T(8,128)S(1)}, u32[]{:S(2)}, u32[]{:S(2)}) collective-permute-start(f32[128,256]{1,0:T(8,128)S(1)} %get-tuple-element.64), channel_id=1, source_target_pairs={{0,24},{8,0},{16,8},{24,16},{32,56},{40,32},{48,40},{56,48},{64,88... | collective-permute-start | bytes 393224 | tf_op jit(solution)/shard_map/ppermute | solution.py:429
  106.5 5.5 %collective-permute-start.28 = (f32[128,256]{1,0:T(8,128)S(1)}, f32[128,256]{1,0:T(8,128)S(1)}, u32[]{:S(2)}, u32[]{:S(2)}) collective-permute-start(f32[128,256]{1,0:T(8,128)S(1)} %get-tuple-element.50), channel_id=1, source_target_pairs={{0,96},{8,104},{16,112},{24,120},{32,0},{40,8},{48,16},{56,24},{64... | collective-permute-start | bytes 393224 | tf_op jit(solution)/shard_map/ppermute | solution.py:435
  107.6 6.6 %collective-permute-start.27 = (f32[128,256]{1,0:T(8,128)S(1)}, f32[128,256]{1,0:T(8,128)S(1)}, u32[]{:S(2)}, u32[]{:S(2)}) collective-permute-start(f32[128,256]{1,0:T(8,128)S(1)} %get-tuple-element.50), channel_id=1, source_target_pairs={{0,64},{8,72},{16,80},{24,88},{32,96},{40,104},{48,112},{56,120},{... | collective-permute-start | bytes 393224 | tf_op jit(solution)/shard_map/ppermute | solution.py:435
  107.8 7.6 %collective-permute-start.26 = (f32[128,256]{1,0:T(8,128)S(1)}, f32[128,256]{1,0:T(8,128)S(1)}, u32[]{:S(2)}, u32[]{:S(2)}) collective-permute-start(f32[128,256]{1,0:T(8,128)S(1)} %get-tuple-element.50), channel_id=1, source_target_pairs={{0,32},{8,40},{16,48},{24,56},{32,64},{40,72},{48,80},{56,88},{64,... | collective-permute-start | bytes 393224 | tf_op jit(solution)/shard_map/ppermute | solution.py:435
  108.7 6.9 %collective-permute-start.31 = (f32[128,256]{1,0:T(8,128)S(1)}, f32[128,256]{1,0:T(8,128)S(1)}, u32[]{:S(2)}, u32[]{:S(2)}) collective-permute-start(f32[128,256]{1,0:T(8,128)S(1)} %get-tuple-element.51), channel_id=1, source_target_pairs={{0,24},{8,0},{16,8},{24,16},{32,56},{40,32},{48,40},{56,48},{64,88... | collective-permute-start | bytes 393224 | tf_op jit(solution)/shard_map/ppermute | solution.py:436
  111.2 6.6 %collective-permute-start.30 = (f32[128,256]{1,0:T(8,128)S(1)}, f32[128,256]{1,0:T(8,128)S(1)}, u32[]{:S(2)}, u32[]{:S(2)}) collective-permute-start(f32[128,256]{1,0:T(8,128)S(1)} %get-tuple-element.51), channel_id=1, source_target_pairs={{0,16},{8,24},{16,0},{24,8},{32,48},{40,56},{48,32},{56,40},{64,80... | collective-permute-start | bytes 393224 | tf_op jit(solution)/shard_map/ppermute | solution.py:436
  111.9 7.5 %collective-permute-start.29 = (f32[128,256]{1,0:T(8,128)S(1)}, f32[128,256]{1,0:T(8,128)S(1)}, u32[]{:S(2)}, u32[]{:S(2)}) collective-permute-start(f32[128,256]{1,0:T(8,128)S(1)} %get-tuple-element.51), channel_id=1, source_target_pairs={{0,8},{8,16},{16,24},{24,0},{32,40},{40,48},{48,56},{56,32},{64,72... | collective-permute-start | bytes 393224 | tf_op jit(solution)/shard_map/ppermute | solution.py:436
  114.2 5.3 %collective-permute-start.19 = (f32[160,256]{1,0:T(8,128)S(1)}, f32[160,256]{1,0:T(8,128)S(1)}, u32[]{:S(2)}, u32[]{:S(2)}) collective-permute-start(f32[160,256]{1,0:T(8,128)S(1)} %get-tuple-element.47), channel_id=1, source_target_pairs={{0,1},{1,0},{2,3},{3,2},{4,5},{5,4},{6,7},{7,6},{8,9},{9,8},{10,11... | collective-permute-start | bytes 491528 | tf_op jit(solution)/shard_map/ppermute | solution.py:444
  119.4 28.2 %collective-permute-start.32 = (f32[512,256]{1,0:T(8,128)S(1)}, f32[512,256]{1,0:T(8,128)S(1)}, u32[]{:S(2)}, u32[]{:S(2)}) collective-permute-start(f32[512,256]{1,0:T(8,128)S(1)} %pad_maximum_fusion.refs_4_), channel_id=1, source_target_pairs={{0,8},{8,16},{16,24},{24,0},{32,40},{40,48},{48,56},{56,32},{64,72... | collective-permute-start | bytes 1572872 | tf_op jit(solution)/shard_map/ppermute | solution.py:440
  119.6 4.4 %collective-permute-start.22 = (f32[40,256]{1,0:T(8,128)S(1)}, f32[40,256]{1,0:T(8,128)S(1)}, u32[]{:S(2)}, u32[]{:S(2)}) collective-permute-start(f32[40,256]{1,0:T(8,128)S(1)} %get-tuple-element.73), channel_id=1, source_target_pairs={{0,6},{1,7},{2,0},{3,1},{4,2},{5,3},{6,4},{7,5},{8,14},{9,15},{10,... | collective-permute-start | bytes 122888 | tf_op jit(solution)/shard_map/ppermute | solution.py:446
  122.3 5.6 %collective-permute-start.21 = (f32[40,256]{1,0:T(8,128)S(1)}, f32[40,256]{1,0:T(8,128)S(1)}, u32[]{:S(2)}, u32[]{:S(2)}) collective-permute-start(f32[40,256]{1,0:T(8,128)S(1)} %get-tuple-element.74), channel_id=1, source_target_pairs={{0,4},{1,5},{2,6},{3,7},{4,0},{5,1},{6,2},{7,3},{8,12},{9,13},{10,... | collective-permute-start | bytes 122888 | tf_op jit(solution)/shard_map/ppermute | solution.py:446
  122.3 5.7 %collective-permute-start.20 = (f32[40,256]{1,0:T(8,128)S(1)}, f32[40,256]{1,0:T(8,128)S(1)}, u32[]{:S(2)}, u32[]{:S(2)}) collective-permute-start(f32[40,256]{1,0:T(8,128)S(1)} %get-tuple-element.72), channel_id=1, source_target_pairs={{0,2},{1,3},{2,4},{3,5},{4,6},{5,7},{6,0},{7,1},{8,10},{9,11},{10,... | collective-permute-start | bytes 122888 | tf_op jit(solution)/shard_map/ppermute | solution.py:446
  127.9 7.2 %collective-permute-start.24 = (f32[40,256]{1,0:T(8,128)S(1)}, f32[40,256]{1,0:T(8,128)S(1)}, u32[]{:S(2)}, u32[]{:S(2)}) collective-permute-start(f32[40,256]{1,0:T(8,128)S(1)} %fusion.1), channel_id=1, source_target_pairs={{0,8},{8,16},{16,24},{24,0},{32,40},{40,48},{48,56},{56,32},{64,72... | collective-permute-start | bytes 122888 | tf_op jit(solution)/shard_map/ppermute | solution.py:448
  128.7 8.1 %collective-permute-start.25 = (f32[40,256]{1,0:T(8,128)S(1)}, f32[40,256]{1,0:T(8,128)S(1)}, u32[]{:S(2)}, u32[]{:S(2)}) collective-permute-start(f32[40,256]{1,0:T(8,128)S(1)} %fusion.1), channel_id=1, source_target_pairs={{0,24},{8,0},{16,8},{24,16},{32,56},{40,32},{48,40},{56,48},{64,88... | collective-permute-start | bytes 122888 | tf_op jit(solution)/shard_map/ppermute | solution.py:448
  131.3 7.9 %collective-permute-start.23 = (f32[40,256]{1,0:T(8,128)S(1)}, f32[40,256]{1,0:T(8,128)S(1)}, u32[]{:S(2)}, u32[]{:S(2)}) collective-permute-start(f32[40,256]{1,0:T(8,128)S(1)} %fusion.1), channel_id=1, source_target_pairs={{0,16},{8,24},{16,0},{24,8},{32,48},{40,56},{48,32},{56,40},{64,80... | collective-permute-start | bytes 122888 | tf_op jit(solution)/shard_map/ppermute | solution.py:448
  133.0 14.7 %collective-permute-start.33 = (f32[512,256]{1,0:T(8,128)S(1)}, f32[512,256]{1,0:T(8,128)S(1)}, u32[]{:S(2)}, u32[]{:S(2)}) collective-permute-start(f32[512,256]{1,0:T(8,128)S(1)} %pad_maximum_fusion.refs_4_), channel_id=1, source_target_pairs={{0,16},{8,24},{16,0},{24,8},{32,48},{40,56},{48,32},{56,40},{64,80... | collective-permute-start | bytes 1572872 | tf_op jit(solution)/shard_map/ppermute | solution.py:440
  135.1 18.3 %collective-permute-start.34 = (f32[512,256]{1,0:T(8,128)S(1)}, f32[512,256]{1,0:T(8,128)S(1)}, u32[]{:S(2)}, u32[]{:S(2)}) collective-permute-start(f32[512,256]{1,0:T(8,128)S(1)} %pad_maximum_fusion.refs_4_), channel_id=1, source_target_pairs={{0,24},{8,0},{16,8},{24,16},{32,56},{40,32},{48,40},{56,48},{64,88... | collective-permute-start | bytes 1572872 | tf_op jit(solution)/shard_map/ppermute | solution.py:440
  136.8 16.6 %collective-permute-start.35 = (f32[512,256]{1,0:T(8,128)S(1)}, f32[512,256]{1,0:T(8,128)S(1)}, u32[]{:S(2)}, u32[]{:S(2)}) collective-permute-start(f32[512,256]{1,0:T(8,128)S(1)} %pad_maximum_fusion.1.refs_8_), channel_id=1, source_target_pairs={{0,32},{8,40},{16,48},{24,56},{32,64},{40,72},{48,80},{56,88},{64,... | collective-permute-start | bytes 1572872 | tf_op jit(solution)/shard_map/ppermute | solution.py:441
  139.2 21.2 %collective-permute-start.36 = (f32[512,256]{1,0:T(8,128)S(1)}, f32[512,256]{1,0:T(8,128)S(1)}, u32[]{:S(2)}, u32[]{:S(2)}) collective-permute-start(f32[512,256]{1,0:T(8,128)S(1)} %pad_maximum_fusion.1.refs_8_), channel_id=1, source_target_pairs={{0,64},{8,72},{16,80},{24,88},{32,96},{40,104},{48,112},{56,120},{... | collective-permute-start | bytes 1572872 | tf_op jit(solution)/shard_map/ppermute | solution.py:441
  147.7 12.8 %collective-permute-start.37 = (f32[512,256]{1,0:T(8,128)S(1)}, f32[512,256]{1,0:T(8,128)S(1)}, u32[]{:S(2)}, u32[]{:S(2)}) collective-permute-start(f32[512,256]{1,0:T(8,128)S(1)} %pad_maximum_fusion.1.refs_8_), channel_id=1, source_target_pairs={{0,96},{8,104},{16,112},{24,120},{32,0},{40,8},{48,16},{56,24},{64... | collective-permute-start | bytes 1572872 | tf_op jit(solution)/shard_map/ppermute | solution.py:441
  164.8 9.1 %collective-permute-start.38 = (f32[1024,256]{1,0:T(8,128)S(1)}, f32[1024,256]{1,0:T(8,128)S(1)}, u32[]{:S(2)}, u32[]{:S(2)}) collective-permute-start(f32[1024,256]{1,0:T(8,128)S(1)} %get-tuple-element.55), channel_id=1, source_target_pairs={{0,1},{1,0},{2,3},{3,2},{4,5},{5,4},{6,7},{7,6},{8,9},{9,8},{10,11... | collective-permute-start | bytes 3145736 | tf_op jit(solution)/shard_map/ppermute | solution.py:454
  164.9 2.7 %collective-permute-start.42 = (f32[40,256]{1,0:T(8,128)S(1)}, f32[40,256]{1,0:T(8,128)S(1)}, u32[]{:S(2)}, u32[]{:S(2)}) collective-permute-start(f32[40,256]{1,0:T(8,128)S(1)} %add_add_fusion.1), channel_id=1, source_target_pairs={{0,1},{1,0},{2,3},{3,2},{4,5},{5,4},{6,7},{7,6},{8,9},{9,8},{10,11... | collective-permute-start | bytes 122888 | tf_op jit(solution)/shard_map/ppermute | solution.py:451
  167.6 12.9 %collective-permute-start.44 = (f32[80,256]{1,0:T(8,128)S(1)}, f32[80,256]{1,0:T(8,128)S(1)}, u32[]{:S(2)}, u32[]{:S(2)}) collective-permute-start(f32[80,256]{1,0:T(8,128)S(1)} %constant_dynamic-update-slice_fusion), channel_id=1, source_target_pairs={{0,32},{8,40},{16,48},{24,56},{32,64},{40,72},{48,80},{56,88},{64,... | collective-permute-start | bytes 245768 | tf_op jit(solution)/shard_map/ppermute | solution.py:455
  171.8 9.4 %collective-permute-start.45 = (f32[80,256]{1,0:T(8,128)S(1)}, f32[80,256]{1,0:T(8,128)S(1)}, u32[]{:S(2)}, u32[]{:S(2)}) collective-permute-start(f32[80,256]{1,0:T(8,128)S(1)} %constant_dynamic-update-slice_fusion), channel_id=1, source_target_pairs={{0,96},{8,104},{16,112},{24,120},{32,0},{40,8},{48,16},{56,24},{64... | collective-permute-start | bytes 245768 | tf_op jit(solution)/shard_map/ppermute | solution.py:455
  171.8 9.4 %collective-permute-start.43 = (f32[80,256]{1,0:T(8,128)S(1)}, f32[80,256]{1,0:T(8,128)S(1)}, u32[]{:S(2)}, u32[]{:S(2)}) collective-permute-start(f32[80,256]{1,0:T(8,128)S(1)} %constant_dynamic-update-slice_fusion), channel_id=1, source_target_pairs={{0,64},{8,72},{16,80},{24,88},{32,96},{40,104},{48,112},{56,120},{... | collective-permute-start | bytes 245768 | tf_op jit(solution)/shard_map/ppermute | solution.py:455
  174.1 23.1 %collective-permute-start.39 = (f32[256,256]{1,0:T(8,128)S(1)}, f32[256,256]{1,0:T(8,128)S(1)}, u32[]{:S(2)}, u32[]{:S(2)}) collective-permute-start(f32[256,256]{1,0:T(8,128)S(1)} %get-tuple-element.62), channel_id=1, source_target_pairs={{0,2},{1,3},{2,4},{3,5},{4,6},{5,7},{6,0},{7,1},{8,10},{9,11},{10,... | collective-permute-start | bytes 786440 | tf_op jit(solution)/shard_map/ppermute | solution.py:460
  174.2 23.0 %collective-permute-start.40 = (f32[256,256]{1,0:T(8,128)S(1)}, f32[256,256]{1,0:T(8,128)S(1)}, u32[]{:S(2)}, u32[]{:S(2)}) collective-permute-start(f32[256,256]{1,0:T(8,128)S(1)} %get-tuple-element.61), channel_id=1, source_target_pairs={{0,4},{1,5},{2,6},{3,7},{4,0},{5,1},{6,2},{7,3},{8,12},{9,13},{10,... | collective-permute-start | bytes 786440 | tf_op jit(solution)/shard_map/ppermute | solution.py:460
  180.5 16.7 %collective-permute-start.41 = (f32[256,256]{1,0:T(8,128)S(1)}, f32[256,256]{1,0:T(8,128)S(1)}, u32[]{:S(2)}, u32[]{:S(2)}) collective-permute-start(f32[256,256]{1,0:T(8,128)S(1)} %get-tuple-element.60), channel_id=1, source_target_pairs={{0,6},{1,7},{2,0},{3,1},{4,2},{5,3},{6,4},{7,5},{8,14},{9,15},{10,... | collective-permute-start | bytes 786440 | tf_op jit(solution)/shard_map/ppermute | solution.py:460
  181.2 10.3 %collective-permute-start.46 = (f32[80,256]{1,0:T(8,128)S(1)}, f32[80,256]{1,0:T(8,128)S(1)}, u32[]{:S(2)}, u32[]{:S(2)}) collective-permute-start(f32[80,256]{1,0:T(8,128)S(1)} %add_add_fusion.refs_4_), channel_id=1, source_target_pairs={{0,2},{1,3},{2,4},{3,5},{4,6},{5,7},{6,0},{7,1},{8,10},{9,11},{10,... | collective-permute-start | bytes 245768 | tf_op jit(solution)/shard_map/ppermute | solution.py:461
  182.6 12.8 %collective-permute-start.47 = (f32[80,256]{1,0:T(8,128)S(1)}, f32[80,256]{1,0:T(8,128)S(1)}, u32[]{:S(2)}, u32[]{:S(2)}) collective-permute-start(f32[80,256]{1,0:T(8,128)S(1)} %add_add_fusion.refs_4_), channel_id=1, source_target_pairs={{0,4},{1,5},{2,6},{3,7},{4,0},{5,1},{6,2},{7,3},{8,12},{9,13},{10,... | collective-permute-start | bytes 245768 | tf_op jit(solution)/shard_map/ppermute | solution.py:461
  191.6 5.6 %collective-permute-start.48 = (f32[80,256]{1,0:T(8,128)S(1)}, f32[80,256]{1,0:T(8,128)S(1)}, u32[]{:S(2)}, u32[]{:S(2)}) collective-permute-start(f32[80,256]{1,0:T(8,128)S(1)} %add_add_fusion.refs_4_), channel_id=1, source_target_pairs={{0,6},{1,7},{2,0},{3,1},{4,2},{5,3},{6,4},{7,5},{8,14},{9,15},{10,... | collective-permute-start | bytes 245768 | tf_op jit(solution)/shard_map/ppermute | solution.py:461
  (8 other events, 159.0 us)

commit v2 on v1

--- a/solution.py
+++ b/solution.py
@@ -45,6 +45,15 @@
         for y in range(SIDE)
         for x in range(SIDE)
     ]
+
+
+def alternate(first, second):
+    got = ([None] * 3, [None] * 3)
+    for hop in (2, 1, 3):
+        for side, send in enumerate((first, second)):
+            if send is not None:
+                got[side][hop - 1] = send(hop)
+    return got
 
 
 def col_hop(dz, dc):
@@ -404,7 +413,7 @@
     fwd_blocks = prepare(vals, count, False)
     got, fwd_blocks = lax.optimization_barrier((got, fwd_blocks))
     own = place(got)
-    panel = [own] + [lax.ppermute(own, "col", col_hop(f, 0)) for f in (1, 2, 3)]
+    panel = [own] + alternate(lambda f: lax.ppermute(own, "col", col_hop(f, 0)), None)[0]
     sources = []
     for part in panel:
         sources += [part, lax.ppermute(part, "col", col_hop(0, 1))]
@@ -412,8 +421,10 @@
     half = list(aggregate(
         fwd_blocks, sources, fwd_from, fwd_to, count, 8, ROWS * NODE)
     )
-    got_a = [lax.ppermute(half[d], "row", row_hop(0, d)) for d in (1, 2, 3)]
-    got_b = [lax.ppermute(half[4 + e], "row", row_hop(e, 0)) for e in (1, 2, 3)]
+    got_a, got_b = alternate(
+        lambda d: lax.ppermute(half[d], "row", row_hop(0, d)),
+        lambda e: lax.ppermute(half[4 + e], "row", row_hop(e, 0)),
+    )
     n = NODE // 2
     back_count, half[0] = lax.optimization_barrier((count, half[0]))
     bwd_blocks = prepare(vals, back_count, True)
@@ -425,21 +436,26 @@
 
     sum_a = [partial(half[0], got_a, k) for k in range(SIDE)]
     sum_b = [partial(half[4], got_b, k) for k in range(SIDE)]
-    parts = [sum_a[0]] + [lax.ppermute(sum_a[e], "row", row_hop(e, 0)) for e in (1, 2, 3)]
-    parts += [sum_b[0]] + [lax.ppermute(sum_b[d], "row", row_hop(0, d)) for d in (1, 2, 3)]
+    rest_a = alternate(lambda e: lax.ppermute(sum_a[e], "row", row_hop(e, 0)), None)[0]
+    rest_b = alternate(lambda d: lax.ppermute(sum_b[d], "row", row_hop(0, d)), None)[0]
+    parts = [sum_a[0]] + rest_a + [sum_b[0]] + rest_b
 
     output, grad_a, grad_b, sums, gives = middle(
         parts, weight, bias_vector, cotangent, where
     )
 
-    near_a = [grad_a] + [lax.ppermute(grad_a, "row", row_hop(e, 0)) for e in (1, 2, 3)]
-    near_b = [grad_b] + [lax.ppermute(grad_b, "row", row_hop(0, d)) for d in (1, 2, 3)]
-    near_a = jnp.concatenate(near_a, axis=0)
-    near_b = jnp.concatenate(near_b, axis=0)
+    near_a, near_b = alternate(
+        lambda e: lax.ppermute(grad_a, "row", row_hop(e, 0)),
+        lambda d: lax.ppermute(grad_b, "row", row_hop(0, d)),
+    )
+    near_a = jnp.concatenate([grad_a] + near_a, axis=0)
+    near_b = jnp.concatenate([grad_b] + near_b, axis=0)
     near_a, near_b = lax.optimization_barrier((near_a, near_b))
-    far_a = [lax.ppermute(near_a, "row", row_hop(0, d)) for d in (1, 3, 2)]
-    far_b = [lax.ppermute(near_b, "row", row_hop(e, 0)) for e in (1, 3, 2)]
-    column = [near_a, far_a[0], far_a[2], far_a[1], near_b, far_b[0], far_b[2], far_b[1]]
+    far_a, far_b = alternate(
+        lambda d: lax.ppermute(near_a, "row", row_hop(0, d)),
+        lambda e: lax.ppermute(near_b, "row", row_hop(e, 0)),
+    )
+    column = [near_a] + far_a + [near_b] + far_b
 
     sums = sums + lax.ppermute(gives, "col", col_hop(0, 1))
     sums = sums.reshape(SIDE, W_ROWS, F)
@@ -457,7 +473,7 @@
     sums_x = [
         keep[k * NODE : (k + 1) * NODE] + taken[k * NODE : (k + 1) * NODE] for k in range(SIDE)
     ]
-    got_x = [lax.ppermute(sums_x[f], "col", col_hop(f, 0)) for f in (1, 2, 3)]
+    got_x, _ = alternate(lambda f: lax.ppermute(sums_x[f], "col", col_hop(f, 0)), None)
     got_w = [lax.ppermute(sums, "col", col_hop(f, 0)) for f in (1, 2, 3)]
     grad_x, grad_w, grad_bias = finish(sums_x[:1] + got_x, [sums] + got_w, where)
     return (output, grad_x, grad_w, grad_bias.reshape(F))

time: 201 us -> 201 us (level)
  no operation moved by 1% of the time
where the time goes in v2:
time: 201 us; the launch traced here: 199 us
  starting transfers between devices  106 us (53%)
  waiting for transfers between devices  65.1 us (32%)
  Pallas kernels  24.2 us (12%)
    ppermute x3, starting transfers between devices, on_device(): lax.ppermute(half[4 + e], 'row', row_hop(e, 0))  17.2 us
    all_to_all x1, starting transfers between devices, on_device(): lax.all_to_all(sent, ('row', 'col'), split_axis=0, concat_axis=0, tiled=T...  11.2 us
    ppermute x3, waiting for transfers between devices, on_device(): lax.ppermute(own, 'col', col_hop(f, 0))  11.1 us
    ppermute x3, starting transfers between devices, on_device(): lax.ppermute(near_b, 'row', row_hop(e, 0))  10.9 us
    ppermute x3, starting transfers between devices, on_device(): lax.ppermute(sum_a[e], 'row', row_hop(e, 0))  9.6 us
    pallas_call x2, Pallas kernels, prepare(): pl.pallas_call(functools.partial(prepare_kernel, flip), out_shape=pltpu.H...  8.91 us
    pallas_call x2, Pallas kernels, aggregate(): pl.pallas_call(functools.partial(aggregate_kernel, n_src, n_dst), out_sha...  8.58 us
    ppermute x3, starting transfers between devices, on_device(): got_w = [lax.ppermute(sums, 'col', col_hop(f, 0)) for f in (1, 2, 3)]  8.53 us
  transfers between devices with their start and end apart: 50, of which 22 were waited for; matrix products, arithmetic and copies ran while one was open for 0% of the time, Pallas kernels for 4%

profile of v2, /device:TPU:0, one launch (start us, length us, event | category | flops | bytes accessed | tf_op | source)
XLA Modules:
  0.0 198.6 jit_solution(11716726787446135598)
XLA Ops:
  1.3 2.3 %pack.1 = f32[128,2,384]{2,1,0:T(2,128)} custom-call(f32[256,256]{1,0:T(8,128)} %features.1, s32[1,256]{1,0:T(1,128)S(1)} %bitcast.19), custom_call_target="tpu_custom_call" | custom-call | tf_op jit(solution)/shard_map/pack/pallas_call | solution.py:85
  3.6 11.2 %all-to-all-start = ((f32[128,2,384]{2,1,0:T(2,128)}), f32[128,2,384]{2,1,0:T(2,128)S(1)}, u32[]{:S(2)}, u32[]{:S(2)}) async-start(f32[128,2,384]{2,1,0:T(2,128)} %pack.1), calls=%async_computation | async-start | bytes 786432 | tf_op jit(solution)/shard_map/all_to_all | solution.py:411
  15.4 3.9 %prepare.1.refs_3_ = bf16[256,64,256]{2,1,0:T(8,128)(2,1)} custom-call(s32[1]{0:T(128)} %bitcast.12.count, f32[256,4096]{1,0:T(8,128)} %bitcast.21), custom_call_target="tpu_custom_call" | custom-call | flops 100000000 | bytes 12582912 | tf_op jit(solution)/shard_map/prepare/pallas_call | solution.py:154
  19.3 7.8 %all-to-all-done.got = f32[128,2,384]{2,1,0:T(2,128)S(1)} async-done(((f32[128,2,384]{2,1,0:T(2,128)}), f32[128,2,384]{2,1,0:T(2,128)S(1)}, u32[]{:S(2)}, u32[]{:S(2)}) %all-to-all-start) | async-done | bytes 393248 | tf_op jit(solution)/shard_map/all_to_all | solution.py:411
  28.1 1.7 collective-permute-start.3
  29.8 1.4 collective-permute-start.5
  31.2 11.0 %collective-permute-done.1.refs_6_ = f32[256,256]{1,0:T(8,128)S(1)} collective-permute-done((f32[256,256]{1,0:T(8,128)S(1)}, f32[256,256]{1,0:T(8,128)S(1)}, u32[]{:S(2)}, u32[]{:S(2)}) %collective-permute-start.1) | collective-permute-done | bytes 262176 | tf_op jit(solution)/shard_map/ppermute | solution.py:416
  44.5 4.2 %shard_map.120 = (f32[512,256]{1,0:T(8,128)S(1)}, f32[512,256]{1,0:T(8,128)S(1)}, f32[512,256]{1,0:T(8,128)S(1)}, f32[512,256]{1,0:T(8,128)S(1)}, f32[512,256]{1...) custom-call(s32[256]{0:T(256)S(1)} %bitcast.15, s32[256]{0:T(256)S(1)} %bitcast.16, ...), custom_call_target="tpu_custom_call" | custom-call | flops 2147483648 | bytes 16777216 | tf_op jit(solution)/shard_map/pallas_call | solution.py:240
  48.7 5.3 %collective-permute-start.7 = (f32[512,256]{1,0:T(8,128)S(1)}, f32[512,256]{1,0:T(8,128)S(1)}, u32[]{:S(2)}, u32[]{:S(2)}) collective-permute-start(f32[512,256]{1,0:T(8,128)S(1)} %get-tuple-element.36), channel_id=1, source_target_pairs={{0,8},{8,16},{16,24},{24,0},{32,40},{40,48},{48,56},{56,32},{64,72... | collective-permute-start | bytes 1572872 | tf_op jit(solution)/shard_map/ppermute | solution.py:425
  54.0 2.1 %collective-permute-start.8 = (f32[512,256]{1,0:T(8,128)S(1)}, f32[512,256]{1,0:T(8,128)S(1)}, u32[]{:S(2)}, u32[]{:S(2)}) collective-permute-start(f32[512,256]{1,0:T(8,128)S(1)} %get-tuple-element.39), channel_id=1, source_target_pairs={{0,16},{8,24},{16,0},{24,8},{32,48},{40,56},{48,32},{56,40},{64,80... | collective-permute-start | bytes 1572872 | tf_op jit(solution)/shard_map/ppermute | solution.py:425
  56.1 2.0 %collective-permute-start.15 = (f32[512,256]{1,0:T(8,128)S(1)}, f32[512,256]{1,0:T(8,128)S(1)}, u32[]{:S(2)}, u32[]{:S(2)}) collective-permute-start(f32[512,256]{1,0:T(8,128)S(1)} %get-tuple-element.44), channel_id=1, source_target_pairs={{0,96},{8,104},{16,112},{24,120},{32,0},{40,8},{48,16},{56,24},{64... | collective-permute-start | bytes 1572872 | tf_op jit(solution)/shard_map/ppermute | solution.py:426
  58.2 1.1 collective-permute-start.14
  59.3 7.0 %collective-permute-done.7 = f32[512,256]{1,0:T(8,128)S(1)} collective-permute-done((f32[512,256]{1,0:T(8,128)S(1)}, f32[512,256]{1,0:T(8,128)S(1)}, u32[]{:S(2)}, u32[]{:S(2)}) %collective-permute-start.7) | collective-permute-done | bytes 524320 | tf_op jit(solution)/shard_map/ppermute | solution.py:425
  66.3 14.1 %collective-permute-start.13 = (f32[512,256]{1,0:T(8,128)S(1)}, f32[512,256]{1,0:T(8,128)S(1)}, u32[]{:S(2)}, u32[]{:S(2)}) collective-permute-start(f32[512,256]{1,0:T(8,128)S(1)} %get-tuple-element.42), channel_id=1, source_target_pairs={{0,32},{8,40},{16,48},{24,56},{32,64},{40,72},{48,80},{56,88},{64,... | collective-permute-start | bytes 1572872 | tf_op jit(solution)/shard_map/ppermute | solution.py:426
  80.4 5.0 %prepare_back.1.refs_3_ = bf16[256,64,256]{2,1,0:T(8,128)(2,1)} custom-call(s32[1]{0:T(128)} %bitcast.11.count, f32[256,4096]{1,0:T(8,128)} %bitcast.22), custom_call_target="tpu_custom_call" | custom-call | flops 100000000 | bytes 12582912 | tf_op jit(solution)/shard_map/prepare_back/pallas_call | solution.py:154
  85.6 6.8 %collective-permute-start.10 = (f32[128,256]{1,0:T(8,128)S(1)}, f32[128,256]{1,0:T(8,128)S(1)}, u32[]{:S(2)}, u32[]{:S(2)}) collective-permute-start(f32[128,256]{1,0:T(8,128)S(1)} %get-tuple-element.70), channel_id=1, source_target_pairs={{0,32},{8,40},{16,48},{24,56},{32,64},{40,72},{48,80},{56,88},{64,... | collective-permute-start | bytes 393224 | tf_op jit(solution)/shard_map/ppermute | solution.py:439
  92.4 2.8 %collective-permute-start.12 = (f32[128,256]{1,0:T(8,128)S(1)}, f32[128,256]{1,0:T(8,128)S(1)}, u32[]{:S(2)}, u32[]{:S(2)}) collective-permute-start(f32[128,256]{1,0:T(8,128)S(1)} %get-tuple-element.68), channel_id=1, source_target_pairs={{0,96},{8,104},{16,112},{24,120},{32,0},{40,8},{48,16},{56,24},{64... | collective-permute-start | bytes 393224 | tf_op jit(solution)/shard_map/ppermute | solution.py:439
  95.4 2.4 %collective-permute-start.17 = (f32[128,256]{1,0:T(8,128)S(1)}, f32[128,256]{1,0:T(8,128)S(1)}, u32[]{:S(2)}, u32[]{:S(2)}) collective-permute-start(f32[128,256]{1,0:T(8,128)S(1)} %get-tuple-element.65), channel_id=1, source_target_pairs={{0,16},{8,24},{16,0},{24,8},{32,48},{40,56},{48,32},{56,40},{64,80... | collective-permute-start | bytes 393224 | tf_op jit(solution)/shard_map/ppermute | solution.py:440
  97.8 2.5 %collective-permute-start.18 = (f32[128,256]{1,0:T(8,128)S(1)}, f32[128,256]{1,0:T(8,128)S(1)}, u32[]{:S(2)}, u32[]{:S(2)}) collective-permute-start(f32[128,256]{1,0:T(8,128)S(1)} %get-tuple-element.64), channel_id=1, source_target_pairs={{0,24},{8,0},{16,8},{24,16},{32,56},{40,32},{48,40},{56,48},{64,88... | collective-permute-start | bytes 393224 | tf_op jit(solution)/shard_map/ppermute | solution.py:440
  100.4 3.1 %collective-permute-done.16.refs_6_ = f32[128,256]{1,0:T(8,128)S(1)} collective-permute-done((f32[128,256]{1,0:T(8,128)S(1)}, f32[128,256]{1,0:T(8,128)S(1)}, u32[]{:S(2)}, u32[]{:S(2)}) %collective-permute-start.16) | collective-permute-done | bytes 131104 | tf_op jit(solution)/shard_map/ppermute | solution.py:440
  104.2 2.3 %middle.1 = (f32[256,256]{1,0:T(8,128)}, f32[128,256]{1,0:T(8,128)S(1)}, f32[128,256]{1,0:T(8,128)S(1)}, f32[160,256]{1,0:T(8,128)S(1)}, f32[160,256]{1,0:T(8,128)S(1)}) custom-call(s32[2]{0:T(128)S(1)} %pad_add_fusion.refs_0_.where, f32[128,256]{1,0:T(8,128)S(1)} %get-tuple-element.71.refs_1_, f32[128,256]{1,0:T(8,128)S(1)} %collective-permute-done.10.refs_2_, ...), custom_call_target="tpu_custom_call" | custom-call | tf_op jit(solution)/shard_map/middle/pallas_call | solution.py:324
  106.5 1.1 collective-permute-start.28
  108.7 2.5 %collective-permute-start.31 = (f32[128,256]{1,0:T(8,128)S(1)}, f32[128,256]{1,0:T(8,128)S(1)}, u32[]{:S(2)}, u32[]{:S(2)}) collective-permute-start(f32[128,256]{1,0:T(8,128)S(1)} %get-tuple-element.51), channel_id=1, source_target_pairs={{0,24},{8,0},{16,8},{24,16},{32,56},{40,32},{48,40},{56,48},{64,88... | collective-permute-start | bytes 393224 | tf_op jit(solution)/shard_map/ppermute | solution.py:449
  112.8 1.4 collective-permute-done.27
  114.2 1.3 collective-permute-done.26
  115.5 2.2 %collective-permute-done.30 = f32[128,256]{1,0:T(8,128)S(1)} collective-permute-done((f32[128,256]{1,0:T(8,128)S(1)}, f32[128,256]{1,0:T(8,128)S(1)}, u32[]{:S(2)}, u32[]{:S(2)}) %collective-permute-start.30) | collective-permute-done | bytes 131104 | tf_op jit(solution)/shard_map/ppermute | solution.py:449
  117.8 1.7 collective-permute-done.29
  119.6 2.7 %collective-permute-start.22 = (f32[40,256]{1,0:T(8,128)S(1)}, f32[40,256]{1,0:T(8,128)S(1)}, u32[]{:S(2)}, u32[]{:S(2)}) collective-permute-start(f32[40,256]{1,0:T(8,128)S(1)} %get-tuple-element.73), channel_id=1, source_target_pairs={{0,6},{1,7},{2,0},{3,1},{4,2},{5,3},{6,4},{7,5},{8,14},{9,15},{10,... | collective-permute-start | bytes 122888 | tf_op jit(solution)/shard_map/ppermute | solution.py:462
  123.9 3.9 %collective-permute-done.21 = f32[40,256]{1,0:T(8,128)S(1)} collective-permute-done((f32[40,256]{1,0:T(8,128)S(1)}, f32[40,256]{1,0:T(8,128)S(1)}, u32[]{:S(2)}, u32[]{:S(2)}) %collective-permute-start.21) | collective-permute-done | bytes 40992 | tf_op jit(solution)/shard_map/ppermute | solution.py:462
  128.7 2.6 %collective-permute-start.25 = (f32[40,256]{1,0:T(8,128)S(1)}, f32[40,256]{1,0:T(8,128)S(1)}, u32[]{:S(2)}, u32[]{:S(2)}) collective-permute-start(f32[40,256]{1,0:T(8,128)S(1)} %fusion.1), channel_id=1, source_target_pairs={{0,24},{8,0},{16,8},{24,16},{32,56},{40,32},{48,40},{56,48},{64,88... | collective-permute-start | bytes 122888 | tf_op jit(solution)/shard_map/ppermute | solution.py:464
  131.3 1.7 collective-permute-start.23
  133.0 1.8 collective-permute-start.33
  135.1 1.7 collective-permute-start.34
  136.8 2.4 %collective-permute-start.35 = (f32[512,256]{1,0:T(8,128)S(1)}, f32[512,256]{1,0:T(8,128)S(1)}, u32[]{:S(2)}, u32[]{:S(2)}) collective-permute-start(f32[512,256]{1,0:T(8,128)S(1)} %pad_maximum_fusion.1.refs_8_), channel_id=1, source_target_pairs={{0,32},{8,40},{16,48},{24,56},{32,64},{40,72},{48,80},{56,88},{64,... | collective-permute-start | bytes 1572872 | tf_op jit(solution)/shard_map/ppermute | solution.py:456
  139.2 8.5 %collective-permute-start.36 = (f32[512,256]{1,0:T(8,128)S(1)}, f32[512,256]{1,0:T(8,128)S(1)}, u32[]{:S(2)}, u32[]{:S(2)}) collective-permute-start(f32[512,256]{1,0:T(8,128)S(1)} %pad_maximum_fusion.1.refs_8_), channel_id=1, source_target_pairs={{0,64},{8,72},{16,80},{24,88},{32,96},{40,104},{48,112},{56,120},{... | collective-permute-start | bytes 1572872 | tf_op jit(solution)/shard_map/ppermute | solution.py:456
  147.7 5.7 %collective-permute-done.34.refs_7_ = f32[512,256]{1,0:T(8,128)S(1)} collective-permute-done((f32[512,256]{1,0:T(8,128)S(1)}, f32[512,256]{1,0:T(8,128)S(1)}, u32[]{:S(2)}, u32[]{:S(2)}) %collective-permute-start.34) | collective-permute-done | bytes 524320 | tf_op jit(solution)/shard_map/ppermute | solution.py:455
  153.4 7.0 %collective-permute-done.36.refs_10_ = f32[512,256]{1,0:T(8,128)S(1)} collective-permute-done((f32[512,256]{1,0:T(8,128)S(1)}, f32[512,256]{1,0:T(8,128)S(1)}, u32[]{:S(2)}, u32[]{:S(2)}) %collective-permute-start.36) | collective-permute-done | bytes 524320 | tf_op jit(solution)/shard_map/ppermute | solution.py:456
  160.4 4.3 %shard_map.121 = (f32[1024,256]{1,0:T(8,128)S(1)}, f32[1024,256]{1,0:T(8,128)S(1)}) custom-call(s32[256]{0:T(256)S(1)} %bitcast.18, s32[256]{0:T(256)S(1)} %bitcast.17, s32[1]{0:T(128)} %bitcast.14.refs_2_, bf16[256,64,256]{2,1,0:T(8,128)(2,1)} %prepare_back.1.refs_3_, f32[512,256]{1,0:T(8,128)S(1)} %pad_maximum_fusion.refs_4_, ...), custom_call_target="tpu_custom_call" | custom-call | flops 2147483648 | bytes 16777216 | tf_op jit(solution)/shard_map/pallas_call | solution.py:240
  165.4 2.2 %collective-permute-done.42 = f32[40,256]{1,0:T(8,128)S(1)} collective-permute-done((f32[40,256]{1,0:T(8,128)S(1)}, f32[40,256]{1,0:T(8,128)S(1)}, u32[]{:S(2)}, u32[]{:S(2)}) %collective-permute-start.42) | collective-permute-done | bytes 40992 | tf_op jit(solution)/shard_map/ppermute | solution.py:467
  167.6 4.2 %collective-permute-start.44 = (f32[80,256]{1,0:T(8,128)S(1)}, f32[80,256]{1,0:T(8,128)S(1)}, u32[]{:S(2)}, u32[]{:S(2)}) collective-permute-start(f32[80,256]{1,0:T(8,128)S(1)} %constant_dynamic-update-slice_fusion), channel_id=1, source_target_pairs={{0,32},{8,40},{16,48},{24,56},{32,64},{40,72},{48,80},{56,88},{64,... | collective-permute-start | bytes 245768 | tf_op jit(solution)/shard_map/ppermute | solution.py:471
  171.8 2.1 %collective-permute-start.43 = (f32[80,256]{1,0:T(8,128)S(1)}, f32[80,256]{1,0:T(8,128)S(1)}, u32[]{:S(2)}, u32[]{:S(2)}) collective-permute-start(f32[80,256]{1,0:T(8,128)S(1)} %constant_dynamic-update-slice_fusion), channel_id=1, source_target_pairs={{0,64},{8,72},{16,80},{24,88},{32,96},{40,104},{48,112},{56,120},{... | collective-permute-start | bytes 245768 | tf_op jit(solution)/shard_map/ppermute | solution.py:471
  174.2 6.3 %collective-permute-start.40 = (f32[256,256]{1,0:T(8,128)S(1)}, f32[256,256]{1,0:T(8,128)S(1)}, u32[]{:S(2)}, u32[]{:S(2)}) collective-permute-start(f32[256,256]{1,0:T(8,128)S(1)} %get-tuple-element.61), channel_id=1, source_target_pairs={{0,4},{1,5},{2,6},{3,7},{4,0},{5,1},{6,2},{7,3},{8,12},{9,13},{10,... | collective-permute-start | bytes 786440 | tf_op jit(solution)/shard_map/ppermute | solution.py:476
  181.2 1.4 collective-permute-start.46
  182.6 3.6 %collective-permute-start.47 = (f32[80,256]{1,0:T(8,128)S(1)}, f32[80,256]{1,0:T(8,128)S(1)}, u32[]{:S(2)}, u32[]{:S(2)}) collective-permute-start(f32[80,256]{1,0:T(8,128)S(1)} %add_add_fusion.refs_4_), channel_id=1, source_target_pairs={{0,4},{1,5},{2,6},{3,7},{4,0},{5,1},{6,2},{7,3},{8,12},{9,13},{10,... | collective-permute-start | bytes 245768 | tf_op jit(solution)/shard_map/ppermute | solution.py:477
  186.2 5.3 %collective-permute-done.46.refs_5_ = f32[80,256]{1,0:T(8,128)S(1)} collective-permute-done((f32[80,256]{1,0:T(8,128)S(1)}, f32[80,256]{1,0:T(8,128)S(1)}, u32[]{:S(2)}, u32[]{:S(2)}) %collective-permute-start.46) | collective-permute-done | bytes 81952 | tf_op jit(solution)/shard_map/ppermute | solution.py:477
  191.6 3.5 %collective-permute-start.48 = (f32[80,256]{1,0:T(8,128)S(1)}, f32[80,256]{1,0:T(8,128)S(1)}, u32[]{:S(2)}, u32[]{:S(2)}) collective-permute-start(f32[80,256]{1,0:T(8,128)S(1)} %add_add_fusion.refs_4_), channel_id=1, source_target_pairs={{0,6},{1,7},{2,0},{3,1},{4,2},{5,3},{6,4},{7,5},{8,14},{9,15},{10,... | collective-permute-start | bytes 245768 | tf_op jit(solution)/shard_map/ppermute | solution.py:477
  195.4 1.7 collective-permute-done.48.refs_7_
  197.2 1.5 finish.1
  (87 shorter events, 12.7 us)
Async XLA Ops:
  3.6 23.5 %all-to-all-start = ((f32[128,2,384]{2,1,0:T(2,128)}), f32[128,2,384]{2,1,0:T(2,128)S(1)}, u32[]{:S(2)}, u32[]{:S(2)}) async-start(f32[128,2,384]{2,1,0:T(2,128)} %pack.1), calls=%async_computation | async-start | bytes 786432 | tf_op jit(solution)/shard_map/all_to_all | solution.py:411
  27.7 14.4 %collective-permute-start.1 = (f32[256,256]{1,0:T(8,128)S(1)}, f32[256,256]{1,0:T(8,128)S(1)}, u32[]{:S(2)}, u32[]{:S(2)}) collective-permute-start(f32[256,256]{1,0:T(8,128)S(1)} %place.1.refs_4_), channel_id=1, source_target_pairs={{0,2},{1,3},{2,4},{3,5},{4,6},{5,7},{6,0},{7,1},{8,10},{9,11},{10,... | collective-permute-start | bytes 786440 | tf_op jit(solution)/shard_map/ppermute | solution.py:416
  28.1 14.1 %collective-permute-start.3 = (f32[256,256]{1,0:T(8,128)S(1)}, f32[256,256]{1,0:T(8,128)S(1)}, u32[]{:S(2)}, u32[]{:S(2)}) collective-permute-start(f32[256,256]{1,0:T(8,128)S(1)} %place.1.refs_4_), channel_id=1, source_target_pairs={{0,4},{1,5},{2,6},{3,7},{4,0},{5,1},{6,2},{7,3},{8,12},{9,13},{10,... | collective-permute-start | bytes 786440 | tf_op jit(solution)/shard_map/ppermute | solution.py:416
  29.8 13.0 %collective-permute-start.5 = (f32[256,256]{1,0:T(8,128)S(1)}, f32[256,256]{1,0:T(8,128)S(1)}, u32[]{:S(2)}, u32[]{:S(2)}) collective-permute-start(f32[256,256]{1,0:T(8,128)S(1)} %place.1.refs_4_), channel_id=1, source_target_pairs={{0,6},{1,7},{2,0},{3,1},{4,2},{5,3},{6,4},{7,5},{8,14},{9,15},{10,... | collective-permute-start | bytes 786440 | tf_op jit(solution)/shard_map/ppermute | solution.py:416
  31.2 11.7 %collective-permute-start = (f32[256,256]{1,0:T(8,128)S(1)}, f32[256,256]{1,0:T(8,128)S(1)}, u32[]{:S(2)}, u32[]{:S(2)}) collective-permute-start(f32[256,256]{1,0:T(8,128)S(1)} %place.1.refs_4_), channel_id=1, source_target_pairs={{0,1},{1,0},{2,3},{3,2},{4,5},{5,4},{6,7},{7,6},{8,9},{9,8},{10,11... | collective-permute-start | bytes 786440 | tf_op jit(solution)/shard_map/ppermute | solution.py:419
  42.2 1.9 collective-permute-start.4
  48.7 17.6 %collective-permute-start.7 = (f32[512,256]{1,0:T(8,128)S(1)}, f32[512,256]{1,0:T(8,128)S(1)}, u32[]{:S(2)}, u32[]{:S(2)}) collective-permute-start(f32[512,256]{1,0:T(8,128)S(1)} %get-tuple-element.36), channel_id=1, source_target_pairs={{0,8},{8,16},{16,24},{24,0},{32,40},{40,48},{48,56},{56,32},{64,72... | collective-permute-start | bytes 1572872 | tf_op jit(solution)/shard_map/ppermute | solution.py:425
  54.0 31.4 %collective-permute-start.9 = (f32[512,256]{1,0:T(8,128)S(1)}, f32[512,256]{1,0:T(8,128)S(1)}, u32[]{:S(2)}, u32[]{:S(2)}) collective-permute-start(f32[512,256]{1,0:T(8,128)S(1)} %get-tuple-element.40), channel_id=1, source_target_pairs={{0,24},{8,0},{16,8},{24,16},{32,56},{40,32},{48,40},{56,48},{64,88... | collective-permute-start | bytes 1572872 | tf_op jit(solution)/shard_map/ppermute | solution.py:425
  54.0 31.4 %collective-permute-start.8 = (f32[512,256]{1,0:T(8,128)S(1)}, f32[512,256]{1,0:T(8,128)S(1)}, u32[]{:S(2)}, u32[]{:S(2)}) collective-permute-start(f32[512,256]{1,0:T(8,128)S(1)} %get-tuple-element.39), channel_id=1, source_target_pairs={{0,16},{8,24},{16,0},{24,8},{32,48},{40,56},{48,32},{56,40},{64,80... | collective-permute-start | bytes 1572872 | tf_op jit(solution)/shard_map/ppermute | solution.py:425
  56.1 36.3 %collective-permute-start.15 = (f32[512,256]{1,0:T(8,128)S(1)}, f32[512,256]{1,0:T(8,128)S(1)}, u32[]{:S(2)}, u32[]{:S(2)}) collective-permute-start(f32[512,256]{1,0:T(8,128)S(1)} %get-tuple-element.44), channel_id=1, source_target_pairs={{0,96},{8,104},{16,112},{24,120},{32,0},{40,8},{48,16},{56,24},{64... | collective-permute-start | bytes 1572872 | tf_op jit(solution)/shard_map/ppermute | solution.py:426
  58.2 37.0 %collective-permute-start.14 = (f32[512,256]{1,0:T(8,128)S(1)}, f32[512,256]{1,0:T(8,128)S(1)}, u32[]{:S(2)}, u32[]{:S(2)}) collective-permute-start(f32[512,256]{1,0:T(8,128)S(1)} %get-tuple-element.43), channel_id=1, source_target_pairs={{0,64},{8,72},{16,80},{24,88},{32,96},{40,104},{48,112},{56,120},{... | collective-permute-start | bytes 1572872 | tf_op jit(solution)/shard_map/ppermute | solution.py:426
  66.3 28.9 %collective-permute-start.13 = (f32[512,256]{1,0:T(8,128)S(1)}, f32[512,256]{1,0:T(8,128)S(1)}, u32[]{:S(2)}, u32[]{:S(2)}) collective-permute-start(f32[512,256]{1,0:T(8,128)S(1)} %get-tuple-element.42), channel_id=1, source_target_pairs={{0,32},{8,40},{16,48},{24,56},{32,64},{40,72},{48,80},{56,88},{64,... | collective-permute-start | bytes 1572872 | tf_op jit(solution)/shard_map/ppermute | solution.py:426
  85.6 12.2 %collective-permute-start.10 = (f32[128,256]{1,0:T(8,128)S(1)}, f32[128,256]{1,0:T(8,128)S(1)}, u32[]{:S(2)}, u32[]{:S(2)}) collective-permute-start(f32[128,256]{1,0:T(8,128)S(1)} %get-tuple-element.70), channel_id=1, source_target_pairs={{0,32},{8,40},{16,48},{24,56},{32,64},{40,72},{48,80},{56,88},{64,... | collective-permute-start | bytes 393224 | tf_op jit(solution)/shard_map/ppermute | solution.py:439
  92.4 8.0 %collective-permute-start.11 = (f32[128,256]{1,0:T(8,128)S(1)}, f32[128,256]{1,0:T(8,128)S(1)}, u32[]{:S(2)}, u32[]{:S(2)}) collective-permute-start(f32[128,256]{1,0:T(8,128)S(1)} %get-tuple-element.69), channel_id=1, source_target_pairs={{0,64},{8,72},{16,80},{24,88},{32,96},{40,104},{48,112},{56,120},{... | collective-permute-start | bytes 393224 | tf_op jit(solution)/shard_map/ppermute | solution.py:439
  92.4 8.0 %collective-permute-start.12 = (f32[128,256]{1,0:T(8,128)S(1)}, f32[128,256]{1,0:T(8,128)S(1)}, u32[]{:S(2)}, u32[]{:S(2)}) collective-permute-start(f32[128,256]{1,0:T(8,128)S(1)} %get-tuple-element.68), channel_id=1, source_target_pairs={{0,96},{8,104},{16,112},{24,120},{32,0},{40,8},{48,16},{56,24},{64... | collective-permute-start | bytes 393224 | tf_op jit(solution)/shard_map/ppermute | solution.py:439
  95.3 8.2 %collective-permute-start.16 = (f32[128,256]{1,0:T(8,128)S(1)}, f32[128,256]{1,0:T(8,128)S(1)}, u32[]{:S(2)}, u32[]{:S(2)}) collective-permute-start(f32[128,256]{1,0:T(8,128)S(1)} %get-tuple-element.66), channel_id=1, source_target_pairs={{0,8},{8,16},{16,24},{24,0},{32,40},{40,48},{48,56},{56,32},{64,72... | collective-permute-start | bytes 393224 | tf_op jit(solution)/shard_map/ppermute | solution.py:440
  95.4 8.1 %collective-permute-start.17 = (f32[128,256]{1,0:T(8,128)S(1)}, f32[128,256]{1,0:T(8,128)S(1)}, u32[]{:S(2)}, u32[]{:S(2)}) collective-permute-start(f32[128,256]{1,0:T(8,128)S(1)} %get-tuple-element.65), channel_id=1, source_target_pairs={{0,16},{8,24},{16,0},{24,8},{32,48},{40,56},{48,32},{56,40},{64,80... | collective-permute-start | bytes 393224 | tf_op jit(solution)/shard_map/ppermute | solution.py:440
  97.8 6.4 %collective-permute-start.18 = (f32[128,256]{1,0:T(8,128)S(1)}, f32[128,256]{1,0:T(8,128)S(1)}, u32[]{:S(2)}, u32[]{:S(2)}) collective-permute-start(f32[128,256]{1,0:T(8,128)S(1)} %get-tuple-element.64), channel_id=1, source_target_pairs={{0,24},{8,0},{16,8},{24,16},{32,56},{40,32},{48,40},{56,48},{64,88... | collective-permute-start | bytes 393224 | tf_op jit(solution)/shard_map/ppermute | solution.py:440
  106.5 5.5 %collective-permute-start.28 = (f32[128,256]{1,0:T(8,128)S(1)}, f32[128,256]{1,0:T(8,128)S(1)}, u32[]{:S(2)}, u32[]{:S(2)}) collective-permute-start(f32[128,256]{1,0:T(8,128)S(1)} %get-tuple-element.50), channel_id=1, source_target_pairs={{0,96},{8,104},{16,112},{24,120},{32,0},{40,8},{48,16},{56,24},{64... | collective-permute-start | bytes 393224 | tf_op jit(solution)/shard_map/ppermute | solution.py:448
  107.6 6.6 %collective-permute-start.27 = (f32[128,256]{1,0:T(8,128)S(1)}, f32[128,256]{1,0:T(8,128)S(1)}, u32[]{:S(2)}, u32[]{:S(2)}) collective-permute-start(f32[128,256]{1,0:T(8,128)S(1)} %get-tuple-element.50), channel_id=1, source_target_pairs={{0,64},{8,72},{16,80},{24,88},{32,96},{40,104},{48,112},{56,120},{... | collective-permute-start | bytes 393224 | tf_op jit(solution)/shard_map/ppermute | solution.py:448
  107.8 7.6 %collective-permute-start.26 = (f32[128,256]{1,0:T(8,128)S(1)}, f32[128,256]{1,0:T(8,128)S(1)}, u32[]{:S(2)}, u32[]{:S(2)}) collective-permute-start(f32[128,256]{1,0:T(8,128)S(1)} %get-tuple-element.50), channel_id=1, source_target_pairs={{0,32},{8,40},{16,48},{24,56},{32,64},{40,72},{48,80},{56,88},{64,... | collective-permute-start | bytes 393224 | tf_op jit(solution)/shard_map/ppermute | solution.py:448
  108.7 6.9 %collective-permute-start.31 = (f32[128,256]{1,0:T(8,128)S(1)}, f32[128,256]{1,0:T(8,128)S(1)}, u32[]{:S(2)}, u32[]{:S(2)}) collective-permute-start(f32[128,256]{1,0:T(8,128)S(1)} %get-tuple-element.51), channel_id=1, source_target_pairs={{0,24},{8,0},{16,8},{24,16},{32,56},{40,32},{48,40},{56,48},{64,88... | collective-permute-start | bytes 393224 | tf_op jit(solution)/shard_map/ppermute | solution.py:449
  111.2 6.6 %collective-permute-start.30 = (f32[128,256]{1,0:T(8,128)S(1)}, f32[128,256]{1,0:T(8,128)S(1)}, u32[]{:S(2)}, u32[]{:S(2)}) collective-permute-start(f32[128,256]{1,0:T(8,128)S(1)} %get-tuple-element.51), channel_id=1, source_target_pairs={{0,16},{8,24},{16,0},{24,8},{32,48},{40,56},{48,32},{56,40},{64,80... | collective-permute-start | bytes 393224 | tf_op jit(solution)/shard_map/ppermute | solution.py:449
  111.9 7.5 %collective-permute-start.29 = (f32[128,256]{1,0:T(8,128)S(1)}, f32[128,256]{1,0:T(8,128)S(1)}, u32[]{:S(2)}, u32[]{:S(2)}) collective-permute-start(f32[128,256]{1,0:T(8,128)S(1)} %get-tuple-element.51), channel_id=1, source_target_pairs={{0,8},{8,16},{16,24},{24,0},{32,40},{40,48},{48,56},{56,32},{64,72... | collective-permute-start | bytes 393224 | tf_op jit(solution)/shard_map/ppermute | solution.py:449
  114.2 5.3 %collective-permute-start.19 = (f32[160,256]{1,0:T(8,128)S(1)}, f32[160,256]{1,0:T(8,128)S(1)}, u32[]{:S(2)}, u32[]{:S(2)}) collective-permute-start(f32[160,256]{1,0:T(8,128)S(1)} %get-tuple-element.47), channel_id=1, source_target_pairs={{0,1},{1,0},{2,3},{3,2},{4,5},{5,4},{6,7},{7,6},{8,9},{9,8},{10,11... | collective-permute-start | bytes 491528 | tf_op jit(solution)/shard_map/ppermute | solution.py:460
  119.4 28.2 %collective-permute-start.32 = (f32[512,256]{1,0:T(8,128)S(1)}, f32[512,256]{1,0:T(8,128)S(1)}, u32[]{:S(2)}, u32[]{:S(2)}) collective-permute-start(f32[512,256]{1,0:T(8,128)S(1)} %pad_maximum_fusion.refs_4_), channel_id=1, source_target_pairs={{0,8},{8,16},{16,24},{24,0},{32,40},{40,48},{48,56},{56,32},{64,72... | collective-permute-start | bytes 1572872 | tf_op jit(solution)/shard_map/ppermute | solution.py:455
  119.6 4.4 %collective-permute-start.22 = (f32[40,256]{1,0:T(8,128)S(1)}, f32[40,256]{1,0:T(8,128)S(1)}, u32[]{:S(2)}, u32[]{:S(2)}) collective-permute-start(f32[40,256]{1,0:T(8,128)S(1)} %get-tuple-element.73), channel_id=1, source_target_pairs={{0,6},{1,7},{2,0},{3,1},{4,2},{5,3},{6,4},{7,5},{8,14},{9,15},{10,... | collective-permute-start | bytes 122888 | tf_op jit(solution)/shard_map/ppermute | solution.py:462
  122.3 5.6 %collective-permute-start.21 = (f32[40,256]{1,0:T(8,128)S(1)}, f32[40,256]{1,0:T(8,128)S(1)}, u32[]{:S(2)}, u32[]{:S(2)}) collective-permute-start(f32[40,256]{1,0:T(8,128)S(1)} %get-tuple-element.74), channel_id=1, source_target_pairs={{0,4},{1,5},{2,6},{3,7},{4,0},{5,1},{6,2},{7,3},{8,12},{9,13},{10,... | collective-permute-start | bytes 122888 | tf_op jit(solution)/shard_map/ppermute | solution.py:462
  122.3 5.7 %collective-permute-start.20 = (f32[40,256]{1,0:T(8,128)S(1)}, f32[40,256]{1,0:T(8,128)S(1)}, u32[]{:S(2)}, u32[]{:S(2)}) collective-permute-start(f32[40,256]{1,0:T(8,128)S(1)} %get-tuple-element.72), channel_id=1, source_target_pairs={{0,2},{1,3},{2,4},{3,5},{4,6},{5,7},{6,0},{7,1},{8,10},{9,11},{10,... | collective-permute-start | bytes 122888 | tf_op jit(solution)/shard_map/ppermute | solution.py:462
  127.9 7.2 %collective-permute-start.24 = (f32[40,256]{1,0:T(8,128)S(1)}, f32[40,256]{1,0:T(8,128)S(1)}, u32[]{:S(2)}, u32[]{:S(2)}) collective-permute-start(f32[40,256]{1,0:T(8,128)S(1)} %fusion.1), channel_id=1, source_target_pairs={{0,8},{8,16},{16,24},{24,0},{32,40},{40,48},{48,56},{56,32},{64,72... | collective-permute-start | bytes 122888 | tf_op jit(solution)/shard_map/ppermute | solution.py:464
  128.7 8.1 %collective-permute-start.25 = (f32[40,256]{1,0:T(8,128)S(1)}, f32[40,256]{1,0:T(8,128)S(1)}, u32[]{:S(2)}, u32[]{:S(2)}) collective-permute-start(f32[40,256]{1,0:T(8,128)S(1)} %fusion.1), channel_id=1, source_target_pairs={{0,24},{8,0},{16,8},{24,16},{32,56},{40,32},{48,40},{56,48},{64,88... | collective-permute-start | bytes 122888 | tf_op jit(solution)/shard_map/ppermute | solution.py:464
  131.3 7.9 %collective-permute-start.23 = (f32[40,256]{1,0:T(8,128)S(1)}, f32[40,256]{1,0:T(8,128)S(1)}, u32[]{:S(2)}, u32[]{:S(2)}) collective-permute-start(f32[40,256]{1,0:T(8,128)S(1)} %fusion.1), channel_id=1, source_target_pairs={{0,16},{8,24},{16,0},{24,8},{32,48},{40,56},{48,32},{56,40},{64,80... | collective-permute-start | bytes 122888 | tf_op jit(solution)/shard_map/ppermute | solution.py:464
  133.0 14.7 %collective-permute-start.33 = (f32[512,256]{1,0:T(8,128)S(1)}, f32[512,256]{1,0:T(8,128)S(1)}, u32[]{:S(2)}, u32[]{:S(2)}) collective-permute-start(f32[512,256]{1,0:T(8,128)S(1)} %pad_maximum_fusion.refs_4_), channel_id=1, source_target_pairs={{0,16},{8,24},{16,0},{24,8},{32,48},{40,56},{48,32},{56,40},{64,80... | collective-permute-start | bytes 1572872 | tf_op jit(solution)/shard_map/ppermute | solution.py:455
  135.1 18.3 %collective-permute-start.34 = (f32[512,256]{1,0:T(8,128)S(1)}, f32[512,256]{1,0:T(8,128)S(1)}, u32[]{:S(2)}, u32[]{:S(2)}) collective-permute-start(f32[512,256]{1,0:T(8,128)S(1)} %pad_maximum_fusion.refs_4_), channel_id=1, source_target_pairs={{0,24},{8,0},{16,8},{24,16},{32,56},{40,32},{48,40},{56,48},{64,88... | collective-permute-start | bytes 1572872 | tf_op jit(solution)/shard_map/ppermute | solution.py:455
  136.8 16.6 %collective-permute-start.35 = (f32[512,256]{1,0:T(8,128)S(1)}, f32[512,256]{1,0:T(8,128)S(1)}, u32[]{:S(2)}, u32[]{:S(2)}) collective-permute-start(f32[512,256]{1,0:T(8,128)S(1)} %pad_maximum_fusion.1.refs_8_), channel_id=1, source_target_pairs={{0,32},{8,40},{16,48},{24,56},{32,64},{40,72},{48,80},{56,88},{64,... | collective-permute-start | bytes 1572872 | tf_op jit(solution)/shard_map/ppermute | solution.py:456
  139.2 21.2 %collective-permute-start.36 = (f32[512,256]{1,0:T(8,128)S(1)}, f32[512,256]{1,0:T(8,128)S(1)}, u32[]{:S(2)}, u32[]{:S(2)}) collective-permute-start(f32[512,256]{1,0:T(8,128)S(1)} %pad_maximum_fusion.1.refs_8_), channel_id=1, source_target_pairs={{0,64},{8,72},{16,80},{24,88},{32,96},{40,104},{48,112},{56,120},{... | collective-permute-start | bytes 1572872 | tf_op jit(solution)/shard_map/ppermute | solution.py:456
  147.7 12.8 %collective-permute-start.37 = (f32[512,256]{1,0:T(8,128)S(1)}, f32[512,256]{1,0:T(8,128)S(1)}, u32[]{:S(2)}, u32[]{:S(2)}) collective-permute-start(f32[512,256]{1,0:T(8,128)S(1)} %pad_maximum_fusion.1.refs_8_), channel_id=1, source_target_pairs={{0,96},{8,104},{16,112},{24,120},{32,0},{40,8},{48,16},{56,24},{64... | collective-permute-start | bytes 1572872 | tf_op jit(solution)/shard_map/ppermute | solution.py:456
  164.8 9.1 %collective-permute-start.38 = (f32[1024,256]{1,0:T(8,128)S(1)}, f32[1024,256]{1,0:T(8,128)S(1)}, u32[]{:S(2)}, u32[]{:S(2)}) collective-permute-start(f32[1024,256]{1,0:T(8,128)S(1)} %get-tuple-element.55), channel_id=1, source_target_pairs={{0,1},{1,0},{2,3},{3,2},{4,5},{5,4},{6,7},{7,6},{8,9},{9,8},{10,11... | collective-permute-start | bytes 3145736 | tf_op jit(solution)/shard_map/ppermute | solution.py:470
  164.9 2.7 %collective-permute-start.42 = (f32[40,256]{1,0:T(8,128)S(1)}, f32[40,256]{1,0:T(8,128)S(1)}, u32[]{:S(2)}, u32[]{:S(2)}) collective-permute-start(f32[40,256]{1,0:T(8,128)S(1)} %add_add_fusion.1), channel_id=1, source_target_pairs={{0,1},{1,0},{2,3},{3,2},{4,5},{5,4},{6,7},{7,6},{8,9},{9,8},{10,11... | collective-permute-start | bytes 122888 | tf_op jit(solution)/shard_map/ppermute | solution.py:467
  167.6 12.9 %collective-permute-start.44 = (f32[80,256]{1,0:T(8,128)S(1)}, f32[80,256]{1,0:T(8,128)S(1)}, u32[]{:S(2)}, u32[]{:S(2)}) collective-permute-start(f32[80,256]{1,0:T(8,128)S(1)} %constant_dynamic-update-slice_fusion), channel_id=1, source_target_pairs={{0,32},{8,40},{16,48},{24,56},{32,64},{40,72},{48,80},{56,88},{64,... | collective-permute-start | bytes 245768 | tf_op jit(solution)/shard_map/ppermute | solution.py:471
  171.8 9.4 %collective-permute-start.45 = (f32[80,256]{1,0:T(8,128)S(1)}, f32[80,256]{1,0:T(8,128)S(1)}, u32[]{:S(2)}, u32[]{:S(2)}) collective-permute-start(f32[80,256]{1,0:T(8,128)S(1)} %constant_dynamic-update-slice_fusion), channel_id=1, source_target_pairs={{0,96},{8,104},{16,112},{24,120},{32,0},{40,8},{48,16},{56,24},{64... | collective-permute-start | bytes 245768 | tf_op jit(solution)/shard_map/ppermute | solution.py:471
  171.8 9.4 %collective-permute-start.43 = (f32[80,256]{1,0:T(8,128)S(1)}, f32[80,256]{1,0:T(8,128)S(1)}, u32[]{:S(2)}, u32[]{:S(2)}) collective-permute-start(f32[80,256]{1,0:T(8,128)S(1)} %constant_dynamic-update-slice_fusion), channel_id=1, source_target_pairs={{0,64},{8,72},{16,80},{24,88},{32,96},{40,104},{48,112},{56,120},{... | collective-permute-start | bytes 245768 | tf_op jit(solution)/shard_map/ppermute | solution.py:471
  174.1 23.1 %collective-permute-start.39 = (f32[256,256]{1,0:T(8,128)S(1)}, f32[256,256]{1,0:T(8,128)S(1)}, u32[]{:S(2)}, u32[]{:S(2)}) collective-permute-start(f32[256,256]{1,0:T(8,128)S(1)} %get-tuple-element.62), channel_id=1, source_target_pairs={{0,2},{1,3},{2,4},{3,5},{4,6},{5,7},{6,0},{7,1},{8,10},{9,11},{10,... | collective-permute-start | bytes 786440 | tf_op jit(solution)/shard_map/ppermute | solution.py:476
  174.2 23.0 %collective-permute-start.40 = (f32[256,256]{1,0:T(8,128)S(1)}, f32[256,256]{1,0:T(8,128)S(1)}, u32[]{:S(2)}, u32[]{:S(2)}) collective-permute-start(f32[256,256]{1,0:T(8,128)S(1)} %get-tuple-element.61), channel_id=1, source_target_pairs={{0,4},{1,5},{2,6},{3,7},{4,0},{5,1},{6,2},{7,3},{8,12},{9,13},{10,... | collective-permute-start | bytes 786440 | tf_op jit(solution)/shard_map/ppermute | solution.py:476
  180.5 16.7 %collective-permute-start.41 = (f32[256,256]{1,0:T(8,128)S(1)}, f32[256,256]{1,0:T(8,128)S(1)}, u32[]{:S(2)}, u32[]{:S(2)}) collective-permute-start(f32[256,256]{1,0:T(8,128)S(1)} %get-tuple-element.60), channel_id=1, source_target_pairs={{0,6},{1,7},{2,0},{3,1},{4,2},{5,3},{6,4},{7,5},{8,14},{9,15},{10,... | collective-permute-start | bytes 786440 | tf_op jit(solution)/shard_map/ppermute | solution.py:476
  181.2 10.3 %collective-permute-start.46 = (f32[80,256]{1,0:T(8,128)S(1)}, f32[80,256]{1,0:T(8,128)S(1)}, u32[]{:S(2)}, u32[]{:S(2)}) collective-permute-start(f32[80,256]{1,0:T(8,128)S(1)} %add_add_fusion.refs_4_), channel_id=1, source_target_pairs={{0,2},{1,3},{2,4},{3,5},{4,6},{5,7},{6,0},{7,1},{8,10},{9,11},{10,... | collective-permute-start | bytes 245768 | tf_op jit(solution)/shard_map/ppermute | solution.py:477
  182.6 12.8 %collective-permute-start.47 = (f32[80,256]{1,0:T(8,128)S(1)}, f32[80,256]{1,0:T(8,128)S(1)}, u32[]{:S(2)}, u32[]{:S(2)}) collective-permute-start(f32[80,256]{1,0:T(8,128)S(1)} %add_add_fusion.refs_4_), channel_id=1, source_target_pairs={{0,4},{1,5},{2,6},{3,7},{4,0},{5,1},{6,2},{7,3},{8,12},{9,13},{10,... | collective-permute-start | bytes 245768 | tf_op jit(solution)/shard_map/ppermute | solution.py:477
  191.6 5.6 %collective-permute-start.48 = (f32[80,256]{1,0:T(8,128)S(1)}, f32[80,256]{1,0:T(8,128)S(1)}, u32[]{:S(2)}, u32[]{:S(2)}) collective-permute-start(f32[80,256]{1,0:T(8,128)S(1)} %add_add_fusion.refs_4_), channel_id=1, source_target_pairs={{0,6},{1,7},{2,0},{3,1},{4,2},{5,3},{6,4},{7,5},{8,14},{9,15},{10,... | collective-permute-start | bytes 245768 | tf_op jit(solution)/shard_map/ppermute | solution.py:477
  (8 other events, 159.0 us)

commit v3 on v2

--- a/solution.py
+++ b/solution.py
@@ -62,6 +62,18 @@
     ]
 
 
+def pick(chosen, rows):
+    chosen = chosen.astype(bf16)
+    high = rows.astype(bf16)
+    rest = rows - high.astype(f32)
+    middle_part = rest.astype(bf16)
+    low = (rest - middle_part.astype(f32)).astype(bf16)
+    first, second, third = (
+        jnp.dot(chosen, piece, preferred_element_type=f32) for piece in (high, middle_part, low)
+    )
+    return (first + second) + third
+
+
 def pack_kernel(features, perm_row, sent):
     owner_row = jnp.broadcast_to(lax.shift_right_logical(perm_row[...], 8), (NODE, NODE))
     owner_col = owner_row.astype(f32).T.astype(jnp.int32)
@@ -74,9 +86,7 @@
     rows = lax.broadcasted_iota(jnp.int32, (NODE // 2, NODE), 0)
     for n in range(2):
         chosen = (rows * 2 + n == slot).astype(f32)
-        sent[:, n, :F] = jnp.dot(
-            chosen, features[...], precision=precise, preferred_element_type=f32
-        )
+        sent[:, n, :F] = pick(chosen, features[...])
         spots = jnp.sum(chosen * spot, axis=1, keepdims=True)
         sent[:, n, F:] = jnp.broadcast_to(spots, (NODE // 2, LANES))
 
@@ -89,7 +99,10 @@
         out_specs=whole(),
         compiler_params=room(8),
         name="pack",
-    )(pltpu.with_memory_space_constraint(features, pltpu.HBM), perm.reshape(1, NODE))
+    )(
+        pltpu.with_memory_space_constraint(features, pltpu.HBM),
+        pltpu.with_memory_space_constraint(perm.reshape(1, NODE), pltpu.HBM),
+    )
 
 
 def place_kernel(got, own):
@@ -101,7 +114,7 @@
         rows.append(got[:, n, :F])
     chosen = jnp.concatenate(chosen, axis=0).T
     rows = jnp.concatenate(rows, axis=0)
-    own[...] = jnp.dot(chosen, rows, precision=precise, preferred_element_type=f32)
+    own[...] = pick(chosen, rows)
 
 
 def place(got):
@@ -410,9 +423,8 @@
     sent = pack(features, loader_perm)
     got = lax.all_to_all(sent, ("row", "col"), split_axis=0, concat_axis=0, tiled=True)
     vals = block_values.reshape(SLOTS, BS * BS)
+    own = place(got)
     fwd_blocks = prepare(vals, count, False)
-    got, fwd_blocks = lax.optimization_barrier((got, fwd_blocks))
-    own = place(got)
     panel = [own] + alternate(lambda f: lax.ppermute(own, "col", col_hop(f, 0)), None)[0]
     sources = []
     for part in panel:
@@ -450,14 +462,15 @@
     )
     near_a = jnp.concatenate([grad_a] + near_a, axis=0)
     near_b = jnp.concatenate([grad_b] + near_b, axis=0)
-    near_a, near_b = lax.optimization_barrier((near_a, near_b))
+    got_w = lax.ppermute(gives, "col", col_hop(0, 1))
+    near_a, near_b, got_w = lax.optimization_barrier((near_a, near_b, got_w))
     far_a, far_b = alternate(
         lambda d: lax.ppermute(near_a, "row", row_hop(0, d)),
         lambda e: lax.ppermute(near_b, "row", row_hop(e, 0)),
     )
     column = [near_a] + far_a + [near_b] + far_b
 
-    sums = sums + lax.ppermute(gives, "col", col_hop(0, 1))
+    sums = sums + got_w
     sums = sums.reshape(SIDE, W_ROWS, F)
     got_w = [lax.ppermute(sums[f], "col", col_hop(f, 0)) for f in (1, 2, 3)]
     sums = sums[0] + got_w[0] + got_w[1] + got_w[2]

time: 201 us -> 208 us (1.035)
  blocking collectives: 0 us -> 23.3 us
  waiting for transfers between devices: 65.1 us -> 57.1 us
  starting transfers between devices: 106 us -> 101 us
    all_to_all x0 -> x1, blocking collectives: none -> 23.3 us  [on_device(): lax.all_to_all(sent, ('row', 'col'), split_axis=0, concat_axis=0, tiled=T...]
    all_to_all x1 -> x0, starting transfers between devices: 11.2 us -> none  [on_device(): lax.all_to_all(sent, ('row', 'col'), split_axis=0, concat_axis=0, tiled=T...]
    all_to_all x1 -> x0, waiting for transfers between devices: 7.77 us -> none  [on_device(): lax.all_to_all(sent, ('row', 'col'), split_axis=0, concat_axis=0, tiled=T...]
    ppermute x3, starting transfers between devices: 7.44 us -> 11.7 us  [on_device(): lax.ppermute(half[d], 'row', row_hop(0, d))]
    ppermute x3, starting transfers between devices: 7.09 us -> 9.94 us  [on_device(): lax.ppermute(sums_x[f], 'col', col_hop(f, 0))]
    ppermute x3, waiting for transfers between devices: 7.03 us -> 4.63 us  [on_device(): lax.ppermute(near_b, 'row', row_hop(e, 0))]
    ppermute x3, waiting for transfers between devices: 7.39 us -> 9.75 us  [on_device(): got_w = [lax.ppermute(sums, 'col', col_hop(f, 0)) for f in (1, 2, 3)]]
    ppermute x3, starting transfers between devices: 10.9 us -> 8.66 us  [on_device(): lax.ppermute(near_b, 'row', row_hop(e, 0))]
  transfers between devices with their start and end apart: 50 -> 49, of which waited for: 22 -> 19; matrix products, arithmetic and copies ran while one was open for 0% -> 1% of each run, Pallas kernels for 4% -> 4%
where the time goes in v3:
time: 208 us; the launch traced here: 207 us
  starting transfers between devices  101 us (49%)
  waiting for transfers between devices  57.1 us (27%)
  blocking collectives  23.3 us (11%)
  Pallas kernels  23.2 us (11%)
    all_to_all x1, blocking collectives, on_device(): lax.all_to_all(sent, ('row', 'col'), split_axis=0, concat_axis=0, tiled=T...  23.3 us
    ppermute x3, starting transfers between devices, on_device(): lax.ppermute(half[4 + e], 'row', row_hop(e, 0))  18.3 us
    ppermute x3, starting transfers between devices, on_device(): lax.ppermute(half[d], 'row', row_hop(0, d))  11.7 us
    ppermute x3, waiting for transfers between devices, on_device(): lax.ppermute(own, 'col', col_hop(f, 0))  11.1 us
    ppermute x3, starting transfers between devices, on_device(): lax.ppermute(sums_x[f], 'col', col_hop(f, 0))  9.94 us
    ppermute x3, waiting for transfers between devices, on_device(): got_w = [lax.ppermute(sums, 'col', col_hop(f, 0)) for f in (1, 2, 3)]  9.75 us
    ppermute x3, starting transfers between devices, on_device(): lax.ppermute(sum_a[e], 'row', row_hop(e, 0))  9.59 us
    pallas_call x2, Pallas kernels, prepare(): pl.pallas_call(functools.partial(prepare_kernel, flip), out_shape=pltpu.H...  8.96 us
  transfers between devices with their start and end apart: 49, of which 19 were waited for; matrix products, arithmetic and copies ran while one was open for 1% of the time, Pallas kernels for 4%

profile of v3, /device:TPU:0, one launch (start us, length us, event | category | flops | bytes accessed | tf_op | source)
XLA Modules:
  0.0 207.4 jit_solution(10011521135949173451)
XLA Ops:
  0.6 1.4 pack.1
  2.0 23.3 %all_to_all.5.got = f32[128,2,384]{2,1,0:T(2,128)S(1)} all-to-all(f32[128,2,384]{2,1,0:T(2,128)S(1)} %pack.1), channel_id=1, replica_groups=mesh['row'=16,'col'=8] {'row','col'}, dimensions={0} | all-to-all | bytes 786432 | tf_op jit(solution)/shard_map/all_to_all | solution.py:424
  26.2 1.7 collective-permute-start.3
  27.9 1.4 collective-permute-start.5
  29.3 11.0 %collective-permute-done.1.refs_6_ = f32[256,256]{1,0:T(8,128)S(1)} collective-permute-done((f32[256,256]{1,0:T(8,128)S(1)}, f32[256,256]{1,0:T(8,128)S(1)}, u32[]{:S(2)}, u32[]{:S(2)}) %collective-permute-start.1) | collective-permute-done | bytes 262176 | tf_op jit(solution)/shard_map/ppermute | solution.py:428
  42.3 3.9 %prepare.1.refs_3_ = bf16[256,64,256]{2,1,0:T(8,128)(2,1)} custom-call(s32[1]{0:T(128)} %bitcast.12.count, f32[256,4096]{1,0:T(8,128)} %bitcast.20), custom_call_target="tpu_custom_call" | custom-call | flops 100000000 | bytes 12582912 | tf_op jit(solution)/shard_map/prepare/pallas_call | solution.py:167
  46.2 4.2 %shard_map.120 = (f32[512,256]{1,0:T(8,128)S(1)}, f32[512,256]{1,0:T(8,128)S(1)}, f32[512,256]{1,0:T(8,128)S(1)}, f32[512,256]{1,0:T(8,128)S(1)}, f32[512,256]{1...) custom-call(s32[256]{0:T(256)S(1)} %bitcast.15, s32[256]{0:T(256)S(1)} %bitcast.16, ...), custom_call_target="tpu_custom_call" | custom-call | flops 2147483648 | bytes 16777216 | tf_op jit(solution)/shard_map/pallas_call | solution.py:253
  50.5 9.6 %collective-permute-start.7 = (f32[512,256]{1,0:T(8,128)S(1)}, f32[512,256]{1,0:T(8,128)S(1)}, u32[]{:S(2)}, u32[]{:S(2)}) collective-permute-start(f32[512,256]{1,0:T(8,128)S(1)} %get-tuple-element.33), channel_id=1, source_target_pairs={{0,8},{8,16},{16,24},{24,0},{32,40},{40,48},{48,56},{56,32},{64,72... | collective-permute-start | bytes 1572872 | tf_op jit(solution)/shard_map/ppermute | solution.py:437
  60.0 2.1 %collective-permute-start.8 = (f32[512,256]{1,0:T(8,128)S(1)}, f32[512,256]{1,0:T(8,128)S(1)}, u32[]{:S(2)}, u32[]{:S(2)}) collective-permute-start(f32[512,256]{1,0:T(8,128)S(1)} %get-tuple-element.36), channel_id=1, source_target_pairs={{0,16},{8,24},{16,0},{24,8},{32,48},{40,56},{48,32},{56,40},{64,80... | collective-permute-start | bytes 1572872 | tf_op jit(solution)/shard_map/ppermute | solution.py:437
  62.2 2.0 collective-permute-start.15
  64.2 1.1 collective-permute-start.14
  65.3 6.3 %collective-permute-done.7 = f32[512,256]{1,0:T(8,128)S(1)} collective-permute-done((f32[512,256]{1,0:T(8,128)S(1)}, f32[512,256]{1,0:T(8,128)S(1)}, u32[]{:S(2)}, u32[]{:S(2)}) %collective-permute-start.7) | collective-permute-done | bytes 524320 | tf_op jit(solution)/shard_map/ppermute | solution.py:437
  71.6 15.2 %collective-permute-start.13 = (f32[512,256]{1,0:T(8,128)S(1)}, f32[512,256]{1,0:T(8,128)S(1)}, u32[]{:S(2)}, u32[]{:S(2)}) collective-permute-start(f32[512,256]{1,0:T(8,128)S(1)} %get-tuple-element.39), channel_id=1, source_target_pairs={{0,32},{8,40},{16,48},{24,56},{32,64},{40,72},{48,80},{56,88},{64,... | collective-permute-start | bytes 1572872 | tf_op jit(solution)/shard_map/ppermute | solution.py:438
  86.8 5.1 %prepare_back.1.refs_3_ = bf16[256,64,256]{2,1,0:T(8,128)(2,1)} custom-call(s32[1]{0:T(128)} %bitcast.11.count, f32[256,4096]{1,0:T(8,128)} %bitcast.21), custom_call_target="tpu_custom_call" | custom-call | flops 100000000 | bytes 12582912 | tf_op jit(solution)/shard_map/prepare_back/pallas_call | solution.py:167
  92.0 6.8 %collective-permute-start.10 = (f32[128,256]{1,0:T(8,128)S(1)}, f32[128,256]{1,0:T(8,128)S(1)}, u32[]{:S(2)}, u32[]{:S(2)}) collective-permute-start(f32[128,256]{1,0:T(8,128)S(1)} %get-tuple-element.68), channel_id=1, source_target_pairs={{0,32},{8,40},{16,48},{24,56},{32,64},{40,72},{48,80},{56,88},{64,... | collective-permute-start | bytes 393224 | tf_op jit(solution)/shard_map/ppermute | solution.py:451
  98.9 2.8 %collective-permute-start.12 = (f32[128,256]{1,0:T(8,128)S(1)}, f32[128,256]{1,0:T(8,128)S(1)}, u32[]{:S(2)}, u32[]{:S(2)}) collective-permute-start(f32[128,256]{1,0:T(8,128)S(1)} %get-tuple-element.66), channel_id=1, source_target_pairs={{0,96},{8,104},{16,112},{24,120},{32,0},{40,8},{48,16},{56,24},{64... | collective-permute-start | bytes 393224 | tf_op jit(solution)/shard_map/ppermute | solution.py:451
  101.9 2.4 %collective-permute-start.17 = (f32[128,256]{1,0:T(8,128)S(1)}, f32[128,256]{1,0:T(8,128)S(1)}, u32[]{:S(2)}, u32[]{:S(2)}) collective-permute-start(f32[128,256]{1,0:T(8,128)S(1)} %get-tuple-element.63), channel_id=1, source_target_pairs={{0,16},{8,24},{16,0},{24,8},{32,48},{40,56},{48,32},{56,40},{64,80... | collective-permute-start | bytes 393224 | tf_op jit(solution)/shard_map/ppermute | solution.py:452
  104.2 2.5 %collective-permute-start.18 = (f32[128,256]{1,0:T(8,128)S(1)}, f32[128,256]{1,0:T(8,128)S(1)}, u32[]{:S(2)}, u32[]{:S(2)}) collective-permute-start(f32[128,256]{1,0:T(8,128)S(1)} %get-tuple-element.62), channel_id=1, source_target_pairs={{0,24},{8,0},{16,8},{24,16},{32,56},{40,32},{48,40},{56,48},{64,88... | collective-permute-start | bytes 393224 | tf_op jit(solution)/shard_map/ppermute | solution.py:452
  106.9 3.5 %collective-permute-done.16.refs_6_ = f32[128,256]{1,0:T(8,128)S(1)} collective-permute-done((f32[128,256]{1,0:T(8,128)S(1)}, f32[128,256]{1,0:T(8,128)S(1)}, u32[]{:S(2)}, u32[]{:S(2)}) %collective-permute-start.16) | collective-permute-done | bytes 131104 | tf_op jit(solution)/shard_map/ppermute | solution.py:452
  111.0 2.3 %middle.1 = (f32[256,256]{1,0:T(8,128)}, f32[128,256]{1,0:T(8,128)S(1)}, f32[128,256]{1,0:T(8,128)S(1)}, f32[160,256]{1,0:T(8,128)S(1)}, f32[160,256]{1,0:T(8,128)S(1)}) custom-call(s32[2]{0:T(128)S(1)} %pad_add_fusion.refs_0_.where, f32[128,256]{1,0:T(8,128)S(1)} %get-tuple-element.69.refs_1_, f32[128,256]{1,0:T(8,128)S(1)} %collective-permute-done.10.refs_2_, ...), custom_call_target="tpu_custom_call" | custom-call | tf_op jit(solution)/shard_map/middle/pallas_call | solution.py:337
  113.3 1.0 collective-permute-start.21
  115.5 2.5 %collective-permute-start.24 = (f32[128,256]{1,0:T(8,128)S(1)}, f32[128,256]{1,0:T(8,128)S(1)}, u32[]{:S(2)}, u32[]{:S(2)}) collective-permute-start(f32[128,256]{1,0:T(8,128)S(1)} %get-tuple-element.45), channel_id=1, source_target_pairs={{0,24},{8,0},{16,8},{24,16},{32,56},{40,32},{48,40},{56,48},{64,88... | collective-permute-start | bytes 393224 | tf_op jit(solution)/shard_map/ppermute | solution.py:461
  119.2 1.8 collective-permute-done.20
  121.0 1.3 collective-permute-done.19
  122.3 2.2 %collective-permute-done.23 = f32[128,256]{1,0:T(8,128)S(1)} collective-permute-done((f32[128,256]{1,0:T(8,128)S(1)}, f32[128,256]{1,0:T(8,128)S(1)}, u32[]{:S(2)}, u32[]{:S(2)}) %collective-permute-start.23) | collective-permute-done | bytes 131104 | tf_op jit(solution)/shard_map/ppermute | solution.py:461
  124.6 1.3 collective-permute-done.22
  126.1 2.5 %collective-permute-start.28 = (f32[40,256]{1,0:T(8,128)S(1)}, f32[40,256]{1,0:T(8,128)S(1)}, u32[]{:S(2)}, u32[]{:S(2)}) collective-permute-start(f32[40,256]{1,0:T(8,128)S(1)} %get-tuple-element.71), channel_id=1, source_target_pairs={{0,6},{1,7},{2,0},{3,1},{4,2},{5,3},{6,4},{7,5},{8,14},{9,15},{10,... | collective-permute-start | bytes 122888 | tf_op jit(solution)/shard_map/ppermute | solution.py:475
  128.5 0.9 collective-permute-start.26
  130.2 3.9 %collective-permute-done.27 = f32[40,256]{1,0:T(8,128)S(1)} collective-permute-done((f32[40,256]{1,0:T(8,128)S(1)}, f32[40,256]{1,0:T(8,128)S(1)}, u32[]{:S(2)}, u32[]{:S(2)}) %collective-permute-start.27) | collective-permute-done | bytes 40992 | tf_op jit(solution)/shard_map/ppermute | solution.py:475
  134.8 2.7 %collective-permute-start.31 = (f32[40,256]{1,0:T(8,128)S(1)}, f32[40,256]{1,0:T(8,128)S(1)}, u32[]{:S(2)}, u32[]{:S(2)}) collective-permute-start(f32[40,256]{1,0:T(8,128)S(1)} %fusion.1), channel_id=1, source_target_pairs={{0,24},{8,0},{16,8},{24,16},{32,56},{40,32},{48,40},{56,48},{64,88... | collective-permute-start | bytes 122888 | tf_op jit(solution)/shard_map/ppermute | solution.py:477
  137.6 1.4 collective-permute-start.29
  139.0 2.1 %collective-permute-start.33 = (f32[512,256]{1,0:T(8,128)S(1)}, f32[512,256]{1,0:T(8,128)S(1)}, u32[]{:S(2)}, u32[]{:S(2)}) collective-permute-start(f32[512,256]{1,0:T(8,128)S(1)} %pad_maximum_fusion.refs_4_), channel_id=1, source_target_pairs={{0,16},{8,24},{16,0},{24,8},{32,48},{40,56},{48,32},{56,40},{64,80... | collective-permute-start | bytes 1572872 | tf_op jit(solution)/shard_map/ppermute | solution.py:468
  141.1 1.9 collective-permute-start.34
  143.1 1.9 collective-permute-start.35
  145.0 4.2 %collective-permute-start.36 = (f32[512,256]{1,0:T(8,128)S(1)}, f32[512,256]{1,0:T(8,128)S(1)}, u32[]{:S(2)}, u32[]{:S(2)}) collective-permute-start(f32[512,256]{1,0:T(8,128)S(1)} %pad_maximum_fusion.1.refs_8_), channel_id=1, source_target_pairs={{0,64},{8,72},{16,80},{24,88},{32,96},{40,104},{48,112},{56,120},{... | collective-permute-start | bytes 1572872 | tf_op jit(solution)/shard_map/ppermute | solution.py:469
  149.2 2.5 %collective-permute-start.37 = (f32[512,256]{1,0:T(8,128)S(1)}, f32[512,256]{1,0:T(8,128)S(1)}, u32[]{:S(2)}, u32[]{:S(2)}) collective-permute-start(f32[512,256]{1,0:T(8,128)S(1)} %pad_maximum_fusion.1.refs_8_), channel_id=1, source_target_pairs={{0,96},{8,104},{16,112},{24,120},{32,0},{40,8},{48,16},{56,24},{64... | collective-permute-start | bytes 1572872 | tf_op jit(solution)/shard_map/ppermute | solution.py:469
  151.8 7.3 %collective-permute-done.34.refs_7_ = f32[512,256]{1,0:T(8,128)S(1)} collective-permute-done((f32[512,256]{1,0:T(8,128)S(1)}, f32[512,256]{1,0:T(8,128)S(1)}, u32[]{:S(2)}, u32[]{:S(2)}) %collective-permute-start.34) | collective-permute-done | bytes 524320 | tf_op jit(solution)/shard_map/ppermute | solution.py:468
  159.1 4.0 %collective-permute-done.36.refs_10_ = f32[512,256]{1,0:T(8,128)S(1)} collective-permute-done((f32[512,256]{1,0:T(8,128)S(1)}, f32[512,256]{1,0:T(8,128)S(1)}, u32[]{:S(2)}, u32[]{:S(2)}) %collective-permute-start.36) | collective-permute-done | bytes 524320 | tf_op jit(solution)/shard_map/ppermute | solution.py:469
  163.7 4.4 %shard_map.121 = (f32[1024,256]{1,0:T(8,128)S(1)}, f32[1024,256]{1,0:T(8,128)S(1)}) custom-call(s32[256]{0:T(256)S(1)} %bitcast.18, s32[256]{0:T(256)S(1)} %bitcast.17, s32[1]{0:T(128)} %bitcast.14.refs_2_, bf16[256,64,256]{2,1,0:T(8,128)(2,1)} %prepare_back.1.refs_3_, f32[512,256]{1,0:T(8,128)S(1)} %pad_maximum_fusion.refs_4_, ...), custom_call_target="tpu_custom_call" | custom-call | flops 2147483648 | bytes 16777216 | tf_op jit(solution)/shard_map/pallas_call | solution.py:253
  168.7 2.2 %collective-permute-done.42 = f32[40,256]{1,0:T(8,128)S(1)} collective-permute-done((f32[40,256]{1,0:T(8,128)S(1)}, f32[40,256]{1,0:T(8,128)S(1)}, u32[]{:S(2)}, u32[]{:S(2)}) %collective-permute-start.42) | collective-permute-done | bytes 40992 | tf_op jit(solution)/shard_map/ppermute | solution.py:480
  170.9 6.3 %collective-permute-start.44 = (f32[80,256]{1,0:T(8,128)S(1)}, f32[80,256]{1,0:T(8,128)S(1)}, u32[]{:S(2)}, u32[]{:S(2)}) collective-permute-start(f32[80,256]{1,0:T(8,128)S(1)} %constant_dynamic-update-slice_fusion), channel_id=1, source_target_pairs={{0,32},{8,40},{16,48},{24,56},{32,64},{40,72},{48,80},{56,88},{64,... | collective-permute-start | bytes 245768 | tf_op jit(solution)/shard_map/ppermute | solution.py:484
  177.2 2.1 %collective-permute-start.43 = (f32[80,256]{1,0:T(8,128)S(1)}, f32[80,256]{1,0:T(8,128)S(1)}, u32[]{:S(2)}, u32[]{:S(2)}) collective-permute-start(f32[80,256]{1,0:T(8,128)S(1)} %constant_dynamic-update-slice_fusion), channel_id=1, source_target_pairs={{0,64},{8,72},{16,80},{24,88},{32,96},{40,104},{48,112},{56,120},{... | collective-permute-start | bytes 245768 | tf_op jit(solution)/shard_map/ppermute | solution.py:484
  179.6 9.9 %collective-permute-start.40 = (f32[256,256]{1,0:T(8,128)S(1)}, f32[256,256]{1,0:T(8,128)S(1)}, u32[]{:S(2)}, u32[]{:S(2)}) collective-permute-start(f32[256,256]{1,0:T(8,128)S(1)} %get-tuple-element.59), channel_id=1, source_target_pairs={{0,4},{1,5},{2,6},{3,7},{4,0},{5,1},{6,2},{7,3},{8,12},{9,13},{10,... | collective-permute-start | bytes 786440 | tf_op jit(solution)/shard_map/ppermute | solution.py:489
  189.6 2.1 %collective-permute-start.46 = (f32[80,256]{1,0:T(8,128)S(1)}, f32[80,256]{1,0:T(8,128)S(1)}, u32[]{:S(2)}, u32[]{:S(2)}) collective-permute-start(f32[80,256]{1,0:T(8,128)S(1)} %add_add_fusion.refs_4_), channel_id=1, source_target_pairs={{0,2},{1,3},{2,4},{3,5},{4,6},{5,7},{6,0},{7,1},{8,10},{9,11},{10,... | collective-permute-start | bytes 245768 | tf_op jit(solution)/shard_map/ppermute | solution.py:490
  192.3 7.7 %collective-permute-done.46.refs_5_ = f32[80,256]{1,0:T(8,128)S(1)} collective-permute-done((f32[80,256]{1,0:T(8,128)S(1)}, f32[80,256]{1,0:T(8,128)S(1)}, u32[]{:S(2)}, u32[]{:S(2)}) %collective-permute-start.46) | collective-permute-done | bytes 81952 | tf_op jit(solution)/shard_map/ppermute | solution.py:490
  200.0 3.8 %collective-permute-start.48 = (f32[80,256]{1,0:T(8,128)S(1)}, f32[80,256]{1,0:T(8,128)S(1)}, u32[]{:S(2)}, u32[]{:S(2)}) collective-permute-start(f32[80,256]{1,0:T(8,128)S(1)} %add_add_fusion.refs_4_), channel_id=1, source_target_pairs={{0,6},{1,7},{2,0},{3,1},{4,2},{5,3},{6,4},{7,5},{8,14},{9,15},{10,... | collective-permute-start | bytes 245768 | tf_op jit(solution)/shard_map/ppermute | solution.py:490
  204.2 1.7 collective-permute-done.48.refs_7_
  205.9 1.5 finish.1
  (82 shorter events, 10.0 us)
Async XLA Ops:
  25.9 14.4 %collective-permute-start.1 = (f32[256,256]{1,0:T(8,128)S(1)}, f32[256,256]{1,0:T(8,128)S(1)}, u32[]{:S(2)}, u32[]{:S(2)}) collective-permute-start(f32[256,256]{1,0:T(8,128)S(1)} %place.1.refs_4_), channel_id=1, source_target_pairs={{0,2},{1,3},{2,4},{3,5},{4,6},{5,7},{6,0},{7,1},{8,10},{9,11},{10,... | collective-permute-start | bytes 786440 | tf_op jit(solution)/shard_map/ppermute | solution.py:428
  26.2 14.1 %collective-permute-start.3 = (f32[256,256]{1,0:T(8,128)S(1)}, f32[256,256]{1,0:T(8,128)S(1)}, u32[]{:S(2)}, u32[]{:S(2)}) collective-permute-start(f32[256,256]{1,0:T(8,128)S(1)} %place.1.refs_4_), channel_id=1, source_target_pairs={{0,4},{1,5},{2,6},{3,7},{4,0},{5,1},{6,2},{7,3},{8,12},{9,13},{10,... | collective-permute-start | bytes 786440 | tf_op jit(solution)/shard_map/ppermute | solution.py:428
  27.9 13.0 %collective-permute-start.5 = (f32[256,256]{1,0:T(8,128)S(1)}, f32[256,256]{1,0:T(8,128)S(1)}, u32[]{:S(2)}, u32[]{:S(2)}) collective-permute-start(f32[256,256]{1,0:T(8,128)S(1)} %place.1.refs_4_), channel_id=1, source_target_pairs={{0,6},{1,7},{2,0},{3,1},{4,2},{5,3},{6,4},{7,5},{8,14},{9,15},{10,... | collective-permute-start | bytes 786440 | tf_op jit(solution)/shard_map/ppermute | solution.py:428
  29.3 16.9 %collective-permute-start = (f32[256,256]{1,0:T(8,128)S(1)}, f32[256,256]{1,0:T(8,128)S(1)}, u32[]{:S(2)}, u32[]{:S(2)}) collective-permute-start(f32[256,256]{1,0:T(8,128)S(1)} %place.1.refs_4_), channel_id=1, source_target_pairs={{0,1},{1,0},{2,3},{3,2},{4,5},{5,4},{6,7},{7,6},{8,9},{9,8},{10,11... | collective-permute-start | bytes 786440 | tf_op jit(solution)/shard_map/ppermute | solution.py:431
  40.3 5.9 %collective-permute-start.2 = (f32[256,256]{1,0:T(8,128)S(1)}, f32[256,256]{1,0:T(8,128)S(1)}, u32[]{:S(2)}, u32[]{:S(2)}) collective-permute-start(f32[256,256]{1,0:T(8,128)S(1)} %collective-permute-done.1.refs_6_), channel_id=1, source_target_pairs={{0,1},{1,0},{2,3},{3,2},{4,5},{5,4},{6,7},{7,6},{8,9},{9,8},{10,11... | collective-permute-start | bytes 786440 | tf_op jit(solution)/shard_map/ppermute | solution.py:431
  40.3 5.9 %collective-permute-start.4 = (f32[256,256]{1,0:T(8,128)S(1)}, f32[256,256]{1,0:T(8,128)S(1)}, u32[]{:S(2)}, u32[]{:S(2)}) collective-permute-start(f32[256,256]{1,0:T(8,128)S(1)} %collective-permute-done.3.refs_8_), channel_id=1, source_target_pairs={{0,1},{1,0},{2,3},{3,2},{4,5},{5,4},{6,7},{7,6},{8,9},{9,8},{10,11... | collective-permute-start | bytes 786440 | tf_op jit(solution)/shard_map/ppermute | solution.py:431
  40.9 5.3 %collective-permute-start.6 = (f32[256,256]{1,0:T(8,128)S(1)}, f32[256,256]{1,0:T(8,128)S(1)}, u32[]{:S(2)}, u32[]{:S(2)}) collective-permute-start(f32[256,256]{1,0:T(8,128)S(1)} %collective-permute-done.5.refs_10_), channel_id=1, source_target_pairs={{0,1},{1,0},{2,3},{3,2},{4,5},{5,4},{6,7},{7,6},{8,9},{9,8},{10,11... | collective-permute-start | bytes 786440 | tf_op jit(solution)/shard_map/ppermute | solution.py:431
  50.5 21.1 %collective-permute-start.7 = (f32[512,256]{1,0:T(8,128)S(1)}, f32[512,256]{1,0:T(8,128)S(1)}, u32[]{:S(2)}, u32[]{:S(2)}) collective-permute-start(f32[512,256]{1,0:T(8,128)S(1)} %get-tuple-element.33), channel_id=1, source_target_pairs={{0,8},{8,16},{16,24},{24,0},{32,40},{40,48},{48,56},{56,32},{64,72... | collective-permute-start | bytes 1572872 | tf_op jit(solution)/shard_map/ppermute | solution.py:437
  60.0 31.8 %collective-permute-start.9 = (f32[512,256]{1,0:T(8,128)S(1)}, f32[512,256]{1,0:T(8,128)S(1)}, u32[]{:S(2)}, u32[]{:S(2)}) collective-permute-start(f32[512,256]{1,0:T(8,128)S(1)} %get-tuple-element.37), channel_id=1, source_target_pairs={{0,24},{8,0},{16,8},{24,16},{32,56},{40,32},{48,40},{56,48},{64,88... | collective-permute-start | bytes 1572872 | tf_op jit(solution)/shard_map/ppermute | solution.py:437
  60.0 31.8 %collective-permute-start.8 = (f32[512,256]{1,0:T(8,128)S(1)}, f32[512,256]{1,0:T(8,128)S(1)}, u32[]{:S(2)}, u32[]{:S(2)}) collective-permute-start(f32[512,256]{1,0:T(8,128)S(1)} %get-tuple-element.36), channel_id=1, source_target_pairs={{0,16},{8,24},{16,0},{24,8},{32,48},{40,56},{48,32},{56,40},{64,80... | collective-permute-start | bytes 1572872 | tf_op jit(solution)/shard_map/ppermute | solution.py:437
  62.2 36.7 %collective-permute-start.15 = (f32[512,256]{1,0:T(8,128)S(1)}, f32[512,256]{1,0:T(8,128)S(1)}, u32[]{:S(2)}, u32[]{:S(2)}) collective-permute-start(f32[512,256]{1,0:T(8,128)S(1)} %get-tuple-element.41), channel_id=1, source_target_pairs={{0,96},{8,104},{16,112},{24,120},{32,0},{40,8},{48,16},{56,24},{64... | collective-permute-start | bytes 1572872 | tf_op jit(solution)/shard_map/ppermute | solution.py:438
  64.2 37.4 %collective-permute-start.14 = (f32[512,256]{1,0:T(8,128)S(1)}, f32[512,256]{1,0:T(8,128)S(1)}, u32[]{:S(2)}, u32[]{:S(2)}) collective-permute-start(f32[512,256]{1,0:T(8,128)S(1)} %get-tuple-element.40), channel_id=1, source_target_pairs={{0,64},{8,72},{16,80},{24,88},{32,96},{40,104},{48,112},{56,120},{... | collective-permute-start | bytes 1572872 | tf_op jit(solution)/shard_map/ppermute | solution.py:438
  71.6 30.0 %collective-permute-start.13 = (f32[512,256]{1,0:T(8,128)S(1)}, f32[512,256]{1,0:T(8,128)S(1)}, u32[]{:S(2)}, u32[]{:S(2)}) collective-permute-start(f32[512,256]{1,0:T(8,128)S(1)} %get-tuple-element.39), channel_id=1, source_target_pairs={{0,32},{8,40},{16,48},{24,56},{32,64},{40,72},{48,80},{56,88},{64,... | collective-permute-start | bytes 1572872 | tf_op jit(solution)/shard_map/ppermute | solution.py:438
  92.0 12.2 %collective-permute-start.10 = (f32[128,256]{1,0:T(8,128)S(1)}, f32[128,256]{1,0:T(8,128)S(1)}, u32[]{:S(2)}, u32[]{:S(2)}) collective-permute-start(f32[128,256]{1,0:T(8,128)S(1)} %get-tuple-element.68), channel_id=1, source_target_pairs={{0,32},{8,40},{16,48},{24,56},{32,64},{40,72},{48,80},{56,88},{64,... | collective-permute-start | bytes 393224 | tf_op jit(solution)/shard_map/ppermute | solution.py:451
  98.9 8.0 %collective-permute-start.11 = (f32[128,256]{1,0:T(8,128)S(1)}, f32[128,256]{1,0:T(8,128)S(1)}, u32[]{:S(2)}, u32[]{:S(2)}) collective-permute-start(f32[128,256]{1,0:T(8,128)S(1)} %get-tuple-element.67), channel_id=1, source_target_pairs={{0,64},{8,72},{16,80},{24,88},{32,96},{40,104},{48,112},{56,120},{... | collective-permute-start | bytes 393224 | tf_op jit(solution)/shard_map/ppermute | solution.py:451
  98.9 8.0 %collective-permute-start.12 = (f32[128,256]{1,0:T(8,128)S(1)}, f32[128,256]{1,0:T(8,128)S(1)}, u32[]{:S(2)}, u32[]{:S(2)}) collective-permute-start(f32[128,256]{1,0:T(8,128)S(1)} %get-tuple-element.66), channel_id=1, source_target_pairs={{0,96},{8,104},{16,112},{24,120},{32,0},{40,8},{48,16},{56,24},{64... | collective-permute-start | bytes 393224 | tf_op jit(solution)/shard_map/ppermute | solution.py:451
  101.8 8.6 %collective-permute-start.16 = (f32[128,256]{1,0:T(8,128)S(1)}, f32[128,256]{1,0:T(8,128)S(1)}, u32[]{:S(2)}, u32[]{:S(2)}) collective-permute-start(f32[128,256]{1,0:T(8,128)S(1)} %get-tuple-element.64), channel_id=1, source_target_pairs={{0,8},{8,16},{16,24},{24,0},{32,40},{40,48},{48,56},{56,32},{64,72... | collective-permute-start | bytes 393224 | tf_op jit(solution)/shard_map/ppermute | solution.py:452
  101.9 8.5 %collective-permute-start.17 = (f32[128,256]{1,0:T(8,128)S(1)}, f32[128,256]{1,0:T(8,128)S(1)}, u32[]{:S(2)}, u32[]{:S(2)}) collective-permute-start(f32[128,256]{1,0:T(8,128)S(1)} %get-tuple-element.63), channel_id=1, source_target_pairs={{0,16},{8,24},{16,0},{24,8},{32,48},{40,56},{48,32},{56,40},{64,80... | collective-permute-start | bytes 393224 | tf_op jit(solution)/shard_map/ppermute | solution.py:452
  104.2 6.8 %collective-permute-start.18 = (f32[128,256]{1,0:T(8,128)S(1)}, f32[128,256]{1,0:T(8,128)S(1)}, u32[]{:S(2)}, u32[]{:S(2)}) collective-permute-start(f32[128,256]{1,0:T(8,128)S(1)} %get-tuple-element.62), channel_id=1, source_target_pairs={{0,24},{8,0},{16,8},{24,16},{32,56},{40,32},{48,40},{56,48},{64,88... | collective-permute-start | bytes 393224 | tf_op jit(solution)/shard_map/ppermute | solution.py:452
  113.3 5.5 %collective-permute-start.21 = (f32[128,256]{1,0:T(8,128)S(1)}, f32[128,256]{1,0:T(8,128)S(1)}, u32[]{:S(2)}, u32[]{:S(2)}) collective-permute-start(f32[128,256]{1,0:T(8,128)S(1)} %get-tuple-element.44), channel_id=1, source_target_pairs={{0,96},{8,104},{16,112},{24,120},{32,0},{40,8},{48,16},{56,24},{64... | collective-permute-start | bytes 393224 | tf_op jit(solution)/shard_map/ppermute | solution.py:460
  114.3 6.7 %collective-permute-start.20 = (f32[128,256]{1,0:T(8,128)S(1)}, f32[128,256]{1,0:T(8,128)S(1)}, u32[]{:S(2)}, u32[]{:S(2)}) collective-permute-start(f32[128,256]{1,0:T(8,128)S(1)} %get-tuple-element.44), channel_id=1, source_target_pairs={{0,64},{8,72},{16,80},{24,88},{32,96},{40,104},{48,112},{56,120},{... | collective-permute-start | bytes 393224 | tf_op jit(solution)/shard_map/ppermute | solution.py:460
  114.6 7.7 %collective-permute-start.19 = (f32[128,256]{1,0:T(8,128)S(1)}, f32[128,256]{1,0:T(8,128)S(1)}, u32[]{:S(2)}, u32[]{:S(2)}) collective-permute-start(f32[128,256]{1,0:T(8,128)S(1)} %get-tuple-element.44), channel_id=1, source_target_pairs={{0,32},{8,40},{16,48},{24,56},{32,64},{40,72},{48,80},{56,88},{64,... | collective-permute-start | bytes 393224 | tf_op jit(solution)/shard_map/ppermute | solution.py:460
  115.5 6.8 %collective-permute-start.24 = (f32[128,256]{1,0:T(8,128)S(1)}, f32[128,256]{1,0:T(8,128)S(1)}, u32[]{:S(2)}, u32[]{:S(2)}) collective-permute-start(f32[128,256]{1,0:T(8,128)S(1)} %get-tuple-element.45), channel_id=1, source_target_pairs={{0,24},{8,0},{16,8},{24,16},{32,56},{40,32},{48,40},{56,48},{64,88... | collective-permute-start | bytes 393224 | tf_op jit(solution)/shard_map/ppermute | solution.py:461
  118.0 6.6 %collective-permute-start.23 = (f32[128,256]{1,0:T(8,128)S(1)}, f32[128,256]{1,0:T(8,128)S(1)}, u32[]{:S(2)}, u32[]{:S(2)}) collective-permute-start(f32[128,256]{1,0:T(8,128)S(1)} %get-tuple-element.45), channel_id=1, source_target_pairs={{0,16},{8,24},{16,0},{24,8},{32,48},{40,56},{48,32},{56,40},{64,80... | collective-permute-start | bytes 393224 | tf_op jit(solution)/shard_map/ppermute | solution.py:461
  118.8 7.1 %collective-permute-start.22 = (f32[128,256]{1,0:T(8,128)S(1)}, f32[128,256]{1,0:T(8,128)S(1)}, u32[]{:S(2)}, u32[]{:S(2)}) collective-permute-start(f32[128,256]{1,0:T(8,128)S(1)} %get-tuple-element.45), channel_id=1, source_target_pairs={{0,8},{8,16},{16,24},{24,0},{32,40},{40,48},{48,56},{56,32},{64,72... | collective-permute-start | bytes 393224 | tf_op jit(solution)/shard_map/ppermute | solution.py:461
  121.0 4.9 %collective-permute-start.25 = (f32[160,256]{1,0:T(8,128)S(1)}, f32[160,256]{1,0:T(8,128)S(1)}, u32[]{:S(2)}, u32[]{:S(2)}) collective-permute-start(f32[160,256]{1,0:T(8,128)S(1)} %get-tuple-element.46), channel_id=1, source_target_pairs={{0,1},{1,0},{2,3},{3,2},{4,5},{5,4},{6,7},{7,6},{8,9},{9,8},{10,11... | collective-permute-start | bytes 491528 | tf_op jit(solution)/shard_map/ppermute | solution.py:465
  125.9 23.3 %collective-permute-start.32 = (f32[512,256]{1,0:T(8,128)S(1)}, f32[512,256]{1,0:T(8,128)S(1)}, u32[]{:S(2)}, u32[]{:S(2)}) collective-permute-start(f32[512,256]{1,0:T(8,128)S(1)} %pad_maximum_fusion.refs_4_), channel_id=1, source_target_pairs={{0,8},{8,16},{16,24},{24,0},{32,40},{40,48},{48,56},{56,32},{64,72... | collective-permute-start | bytes 1572872 | tf_op jit(solution)/shard_map/ppermute | solution.py:468
  126.1 4.2 %collective-permute-start.28 = (f32[40,256]{1,0:T(8,128)S(1)}, f32[40,256]{1,0:T(8,128)S(1)}, u32[]{:S(2)}, u32[]{:S(2)}) collective-permute-start(f32[40,256]{1,0:T(8,128)S(1)} %get-tuple-element.71), channel_id=1, source_target_pairs={{0,6},{1,7},{2,0},{3,1},{4,2},{5,3},{6,4},{7,5},{8,14},{9,15},{10,... | collective-permute-start | bytes 122888 | tf_op jit(solution)/shard_map/ppermute | solution.py:475
  128.5 5.6 %collective-permute-start.27 = (f32[40,256]{1,0:T(8,128)S(1)}, f32[40,256]{1,0:T(8,128)S(1)}, u32[]{:S(2)}, u32[]{:S(2)}) collective-permute-start(f32[40,256]{1,0:T(8,128)S(1)} %get-tuple-element.72), channel_id=1, source_target_pairs={{0,4},{1,5},{2,6},{3,7},{4,0},{5,1},{6,2},{7,3},{8,12},{9,13},{10,... | collective-permute-start | bytes 122888 | tf_op jit(solution)/shard_map/ppermute | solution.py:475
  128.5 5.7 %collective-permute-start.26 = (f32[40,256]{1,0:T(8,128)S(1)}, f32[40,256]{1,0:T(8,128)S(1)}, u32[]{:S(2)}, u32[]{:S(2)}) collective-permute-start(f32[40,256]{1,0:T(8,128)S(1)} %get-tuple-element.70), channel_id=1, source_target_pairs={{0,2},{1,3},{2,4},{3,5},{4,6},{5,7},{6,0},{7,1},{8,10},{9,11},{10,... | collective-permute-start | bytes 122888 | tf_op jit(solution)/shard_map/ppermute | solution.py:475
  134.2 6.9 %collective-permute-start.30 = (f32[40,256]{1,0:T(8,128)S(1)}, f32[40,256]{1,0:T(8,128)S(1)}, u32[]{:S(2)}, u32[]{:S(2)}) collective-permute-start(f32[40,256]{1,0:T(8,128)S(1)} %fusion.1), channel_id=1, source_target_pairs={{0,8},{8,16},{16,24},{24,0},{32,40},{40,48},{48,56},{56,32},{64,72... | collective-permute-start | bytes 122888 | tf_op jit(solution)/shard_map/ppermute | solution.py:477
  134.8 8.2 %collective-permute-start.31 = (f32[40,256]{1,0:T(8,128)S(1)}, f32[40,256]{1,0:T(8,128)S(1)}, u32[]{:S(2)}, u32[]{:S(2)}) collective-permute-start(f32[40,256]{1,0:T(8,128)S(1)} %fusion.1), channel_id=1, source_target_pairs={{0,24},{8,0},{16,8},{24,16},{32,56},{40,32},{48,40},{56,48},{64,88... | collective-permute-start | bytes 122888 | tf_op jit(solution)/shard_map/ppermute | solution.py:477
  137.6 7.4 %collective-permute-start.29 = (f32[40,256]{1,0:T(8,128)S(1)}, f32[40,256]{1,0:T(8,128)S(1)}, u32[]{:S(2)}, u32[]{:S(2)}) collective-permute-start(f32[40,256]{1,0:T(8,128)S(1)} %fusion.1), channel_id=1, source_target_pairs={{0,16},{8,24},{16,0},{24,8},{32,48},{40,56},{48,32},{56,40},{64,80... | collective-permute-start | bytes 122888 | tf_op jit(solution)/shard_map/ppermute | solution.py:477
  139.0 12.8 %collective-permute-start.33 = (f32[512,256]{1,0:T(8,128)S(1)}, f32[512,256]{1,0:T(8,128)S(1)}, u32[]{:S(2)}, u32[]{:S(2)}) collective-permute-start(f32[512,256]{1,0:T(8,128)S(1)} %pad_maximum_fusion.refs_4_), channel_id=1, source_target_pairs={{0,16},{8,24},{16,0},{24,8},{32,48},{40,56},{48,32},{56,40},{64,80... | collective-permute-start | bytes 1572872 | tf_op jit(solution)/shard_map/ppermute | solution.py:468
  141.1 18.0 %collective-permute-start.34 = (f32[512,256]{1,0:T(8,128)S(1)}, f32[512,256]{1,0:T(8,128)S(1)}, u32[]{:S(2)}, u32[]{:S(2)}) collective-permute-start(f32[512,256]{1,0:T(8,128)S(1)} %pad_maximum_fusion.refs_4_), channel_id=1, source_target_pairs={{0,24},{8,0},{16,8},{24,16},{32,56},{40,32},{48,40},{56,48},{64,88... | collective-permute-start | bytes 1572872 | tf_op jit(solution)/shard_map/ppermute | solution.py:468
  143.1 16.0 %collective-permute-start.35 = (f32[512,256]{1,0:T(8,128)S(1)}, f32[512,256]{1,0:T(8,128)S(1)}, u32[]{:S(2)}, u32[]{:S(2)}) collective-permute-start(f32[512,256]{1,0:T(8,128)S(1)} %pad_maximum_fusion.1.refs_8_), channel_id=1, source_target_pairs={{0,32},{8,40},{16,48},{24,56},{32,64},{40,72},{48,80},{56,88},{64,... | collective-permute-start | bytes 1572872 | tf_op jit(solution)/shard_map/ppermute | solution.py:469
  145.0 18.1 %collective-permute-start.36 = (f32[512,256]{1,0:T(8,128)S(1)}, f32[512,256]{1,0:T(8,128)S(1)}, u32[]{:S(2)}, u32[]{:S(2)}) collective-permute-start(f32[512,256]{1,0:T(8,128)S(1)} %pad_maximum_fusion.1.refs_8_), channel_id=1, source_target_pairs={{0,64},{8,72},{16,80},{24,88},{32,96},{40,104},{48,112},{56,120},{... | collective-permute-start | bytes 1572872 | tf_op jit(solution)/shard_map/ppermute | solution.py:469
  149.2 14.5 %collective-permute-start.37 = (f32[512,256]{1,0:T(8,128)S(1)}, f32[512,256]{1,0:T(8,128)S(1)}, u32[]{:S(2)}, u32[]{:S(2)}) collective-permute-start(f32[512,256]{1,0:T(8,128)S(1)} %pad_maximum_fusion.1.refs_8_), channel_id=1, source_target_pairs={{0,96},{8,104},{16,112},{24,120},{32,0},{40,8},{48,16},{56,24},{64... | collective-permute-start | bytes 1572872 | tf_op jit(solution)/shard_map/ppermute | solution.py:469
  168.1 11.3 %collective-permute-start.38 = (f32[1024,256]{1,0:T(8,128)S(1)}, f32[1024,256]{1,0:T(8,128)S(1)}, u32[]{:S(2)}, u32[]{:S(2)}) collective-permute-start(f32[1024,256]{1,0:T(8,128)S(1)} %get-tuple-element.53), channel_id=1, source_target_pairs={{0,1},{1,0},{2,3},{3,2},{4,5},{5,4},{6,7},{7,6},{8,9},{9,8},{10,11... | collective-permute-start | bytes 3145736 | tf_op jit(solution)/shard_map/ppermute | solution.py:483
  170.9 18.6 %collective-permute-start.44 = (f32[80,256]{1,0:T(8,128)S(1)}, f32[80,256]{1,0:T(8,128)S(1)}, u32[]{:S(2)}, u32[]{:S(2)}) collective-permute-start(f32[80,256]{1,0:T(8,128)S(1)} %constant_dynamic-update-slice_fusion), channel_id=1, source_target_pairs={{0,32},{8,40},{16,48},{24,56},{32,64},{40,72},{48,80},{56,88},{64,... | collective-permute-start | bytes 245768 | tf_op jit(solution)/shard_map/ppermute | solution.py:484
  177.2 12.3 %collective-permute-start.45 = (f32[80,256]{1,0:T(8,128)S(1)}, f32[80,256]{1,0:T(8,128)S(1)}, u32[]{:S(2)}, u32[]{:S(2)}) collective-permute-start(f32[80,256]{1,0:T(8,128)S(1)} %constant_dynamic-update-slice_fusion), channel_id=1, source_target_pairs={{0,96},{8,104},{16,112},{24,120},{32,0},{40,8},{48,16},{56,24},{64... | collective-permute-start | bytes 245768 | tf_op jit(solution)/shard_map/ppermute | solution.py:484
  177.2 12.3 %collective-permute-start.43 = (f32[80,256]{1,0:T(8,128)S(1)}, f32[80,256]{1,0:T(8,128)S(1)}, u32[]{:S(2)}, u32[]{:S(2)}) collective-permute-start(f32[80,256]{1,0:T(8,128)S(1)} %constant_dynamic-update-slice_fusion), channel_id=1, source_target_pairs={{0,64},{8,72},{16,80},{24,88},{32,96},{40,104},{48,112},{56,120},{... | collective-permute-start | bytes 245768 | tf_op jit(solution)/shard_map/ppermute | solution.py:484
  179.6 26.4 %collective-permute-start.39 = (f32[256,256]{1,0:T(8,128)S(1)}, f32[256,256]{1,0:T(8,128)S(1)}, u32[]{:S(2)}, u32[]{:S(2)}) collective-permute-start(f32[256,256]{1,0:T(8,128)S(1)} %get-tuple-element.60), channel_id=1, source_target_pairs={{0,2},{1,3},{2,4},{3,5},{4,6},{5,7},{6,0},{7,1},{8,10},{9,11},{10,... | collective-permute-start | bytes 786440 | tf_op jit(solution)/shard_map/ppermute | solution.py:489
  179.6 26.3 %collective-permute-start.40 = (f32[256,256]{1,0:T(8,128)S(1)}, f32[256,256]{1,0:T(8,128)S(1)}, u32[]{:S(2)}, u32[]{:S(2)}) collective-permute-start(f32[256,256]{1,0:T(8,128)S(1)} %get-tuple-element.59), channel_id=1, source_target_pairs={{0,4},{1,5},{2,6},{3,7},{4,0},{5,1},{6,2},{7,3},{8,12},{9,13},{10,... | collective-permute-start | bytes 786440 | tf_op jit(solution)/shard_map/ppermute | solution.py:489
  189.5 16.4 %collective-permute-start.41 = (f32[256,256]{1,0:T(8,128)S(1)}, f32[256,256]{1,0:T(8,128)S(1)}, u32[]{:S(2)}, u32[]{:S(2)}) collective-permute-start(f32[256,256]{1,0:T(8,128)S(1)} %get-tuple-element.58), channel_id=1, source_target_pairs={{0,6},{1,7},{2,0},{3,1},{4,2},{5,3},{6,4},{7,5},{8,14},{9,15},{10,... | collective-permute-start | bytes 786440 | tf_op jit(solution)/shard_map/ppermute | solution.py:489
  189.6 10.5 %collective-permute-start.46 = (f32[80,256]{1,0:T(8,128)S(1)}, f32[80,256]{1,0:T(8,128)S(1)}, u32[]{:S(2)}, u32[]{:S(2)}) collective-permute-start(f32[80,256]{1,0:T(8,128)S(1)} %add_add_fusion.refs_4_), channel_id=1, source_target_pairs={{0,2},{1,3},{2,4},{3,5},{4,6},{5,7},{6,0},{7,1},{8,10},{9,11},{10,... | collective-permute-start | bytes 245768 | tf_op jit(solution)/shard_map/ppermute | solution.py:490
  191.6 12.5 %collective-permute-start.47 = (f32[80,256]{1,0:T(8,128)S(1)}, f32[80,256]{1,0:T(8,128)S(1)}, u32[]{:S(2)}, u32[]{:S(2)}) collective-permute-start(f32[80,256]{1,0:T(8,128)S(1)} %add_add_fusion.refs_4_), channel_id=1, source_target_pairs={{0,4},{1,5},{2,6},{3,7},{4,0},{5,1},{6,2},{7,3},{8,12},{9,13},{10,... | collective-permute-start | bytes 245768 | tf_op jit(solution)/shard_map/ppermute | solution.py:490
  200.0 5.9 %collective-permute-start.48 = (f32[80,256]{1,0:T(8,128)S(1)}, f32[80,256]{1,0:T(8,128)S(1)}, u32[]{:S(2)}, u32[]{:S(2)}) collective-permute-start(f32[80,256]{1,0:T(8,128)S(1)} %add_add_fusion.refs_4_), channel_id=1, source_target_pairs={{0,6},{1,7},{2,0},{3,1},{4,2},{5,3},{6,4},{7,5},{8,14},{9,15},{10,... | collective-permute-start | bytes 245768 | tf_op jit(solution)/shard_map/ppermute | solution.py:490
  (5 other events, 120.8 us)

commit v4 on v3

--- a/solution.py
+++ b/solution.py
@@ -8,7 +8,6 @@
 from jax.experimental.pallas import tpu as pltpu
 from jax.sharding import PartitionSpec as P
 
-precise = lax.Precision.HIGHEST
 F = 256
 BS = 64
 NODE = 256
@@ -180,15 +179,17 @@
     )(count, pltpu.with_memory_space_constraint(vals, pltpu.HBM))
 
 
-def aggregate_kernel(n_src, n_dst, *refs):
-    source_at, target_at, count = refs[:3]
-    blocks = refs[3]
-    sources = refs[4 : 4 + n_src]
-    targets = refs[4 + n_src : 4 + n_src + n_dst]
-    held, split, total, in_sems, out_sems = refs[4 + n_src + n_dst :]
-    step = pl.program_id(0)
+def aggregate_kernel(n_src, n_dst, source_at, target_at, count, blocks, *refs):
+    sources, targets = refs[:n_src], refs[n_src : n_src + n_dst]
+    held, split, total, stage, in_sems, out_sems, block_sems = refs[n_src + n_dst :]
     in_rows = sources[0].shape[0]
     out_rows = targets[0].shape[0]
+    full = count[0] // STEP
+
+    def fetch(step, slot):
+        return pltpu.make_async_copy(
+            blocks.at[pl.ds(step * STEP, STEP)], stage.at[slot], block_sems.at[slot]
+        )
 
     def load(n):
         return pltpu.make_async_copy(
@@ -200,80 +201,76 @@
             total.at[pl.ds(n * out_rows, out_rows)], targets[n], out_sems.at[n]
         )
 
-    @pl.when(step == 0)
-    def _():
-        for n in range(n_src):
-            load(n).start()
-        total[...] = jnp.zeros_like(total)
-        per = in_rows // BS
-        for n in range(n_src):
-            load(n).wait()
-
-            def one(k, carry):
-                at = n * per + k
-                rows = held[pl.ds(pl.multiple_of(at * BS, BS), BS), :]
-                high = rows.astype(bf16)
-                low = (rows - high.astype(f32)).astype(bf16)
-                split[at, 0:BS, :] = high
-                split[at, BS : 2 * BS, :] = low
-                split[at, 2 * BS :, :] = high
-                return carry
-
-            lax.fori_loop(0, per, one, 0, unroll=2)
-
-    def slots(number):
+    for n in range(n_src):
+        load(n).start()
+    fetch(0, 0).start()
+    total[...] = jnp.zeros_like(total)
+    per = in_rows // BS
+    for n in range(n_src):
+        load(n).wait()
+
+        def one_block(k, carry):
+            at = n * per + k
+            rows = held[pl.ds(pl.multiple_of(at * BS, BS), BS), :]
+            high = rows.astype(bf16)
+            low = (rows - high.astype(f32)).astype(bf16)
+            split[at, 0:BS, :] = high
+            split[at, BS : 2 * BS, :] = low
+            split[at, 2 * BS :, :] = high
+            return carry
+
+        lax.fori_loop(0, per, one_block, 0, unroll=2)
+
+    def slots(step, place, number):
         for slot in range(number):
             at = step * STEP + slot
             term = jnp.dot(
-                blocks[slot][:, :DEPTH], split[source_at[at]], preferred_element_type=f32
+                stage[place, slot][:, :DEPTH], split[source_at[at]], preferred_element_type=f32
             )
             into = pl.ds(pl.multiple_of(target_at[at] * BS, BS), BS)
             total[into, :] += term
 
-    @pl.when((step + 1) * STEP <= count[0])
+    def one_step(step, carry):
+        place = step & 1
+        fetch(step, place).wait()
+
+        @pl.when(step + 1 < full)
+        def _():
+            fetch(step + 1, 1 - place).start()
+
+        slots(step, place, STEP)
+        return carry
+
+    lax.fori_loop(0, full, one_step, 0)
+
+    @pl.when(count[0] == LEAST)
     def _():
-        slots(STEP)
-
-    @pl.when((step == 0) & (count[0] == LEAST))
-    def _():
-        slots(LEAST)
-
-    @pl.when(step == pl.num_programs(0) - 1)
-    def _():
-        for n in range(n_dst):
-            keep(n).start()
-        for n in range(n_dst):
-            keep(n).wait()
+        fetch(0, 0).wait()
+        slots(0, 0, LEAST)
+
+    for n in range(n_dst):
+        keep(n).start()
+    for n in range(n_dst):
+        keep(n).wait()
 
 
 def aggregate(blocks, sources, source_at, target_at, count, n_dst, out_rows):
     n_src = len(sources)
     total_in = sum(s.shape[0] for s in sources)
-    steps = SLOTS // STEP
     return pl.pallas_call(
         functools.partial(aggregate_kernel, n_src, n_dst),
         out_shape=[jax.ShapeDtypeStruct((out_rows // n_dst, F), f32)] * n_dst,
-        grid_spec=pltpu.PrefetchScalarGridSpec(
-            num_scalar_prefetch=3,
-            grid=(steps,),
-            in_specs=[
-                pl.BlockSpec(
-                    (STEP, BS, F),
-                    lambda s, a, b, n: (
-                        jnp.minimum(s, jnp.maximum(n[0] // STEP, 1) - 1), 0, 0
-                    ),
-                )
-            ]
-            + [anywhere()] * n_src,
-            out_specs=[anywhere()] * n_dst,
-            scratch_shapes=[
-                pltpu.VMEM((total_in, F), f32),
-                pltpu.VMEM((total_in // BS, DEPTH, F), bf16),
-                pltpu.VMEM((out_rows, F), f32),
-                pltpu.SemaphoreType.DMA((n_src,)),
-                pltpu.SemaphoreType.DMA((n_dst,)),
-            ],
-        ),
+        in_specs=[pl.BlockSpec(memory_space=pltpu.SMEM)] * 3 + [anywhere()] * (n_src + 1),
+        out_specs=[anywhere()] * n_dst,
+        scratch_shapes=[
+            pltpu.VMEM((total_in, F), f32),
+            pltpu.VMEM((total_in // BS, DEPTH, F), bf16),
+            pltpu.VMEM((out_rows, F), f32),
+            pltpu.VMEM((2, STEP, BS, F), bf16),
+            pltpu.SemaphoreType.DMA((n_src,)),
+            pltpu.SemaphoreType.DMA((n_dst,)),
+            pltpu.SemaphoreType.DMA((2,)),
+        ],
         cost_estimate=pl.CostEstimate(
             flops=2 * SLOTS * BS * F * F, bytes_accessed=16 << 20, transcendentals=0
         ),
@@ -285,6 +282,20 @@
         pltpu.with_memory_space_constraint(blocks, pltpu.HBM),
         *sources,
     )
+
+
+def halves(rows):
+    high = rows.astype(bf16)
+    return high, (rows - high.astype(f32)).astype(bf16)
+
+
+def product(left, right, dims):
+    (a, b), (c, d) = halves(left), halves(right)
+
+    def dot(u, v):
+        return lax.dot_general(u, v, (dims, ((), ())), preferred_element_type=f32)
+
+    return dot(a, c) + (dot(a, d) + dot(b, c))
 
 
 def middle_kernel(*refs):
@@ -302,15 +313,12 @@
                     pl.ds(side * NODE + q * BS + odd, 32, stride=2), :
                 ]
     rows = hidden[...]
-    preact = jnp.dot(rows, weight[...], precision=precise, preferred_element_type=f32)
+    preact = product(rows, weight[...], ((1,), (0,)))
     preact = preact + bias[...]
     squashed = 1.0 / (1.0 + jnp.exp(-preact))
     grad_pre = turned[...] * squashed * (1.0 + preact * (1.0 - squashed))
     turned[...] = preact * squashed
-    grad = lax.dot_general(
-        grad_pre, weight[...], (((1,), (1,)), ((), ())), precision=precise,
-        preferred_element_type=f32,
-    )
+    grad = product(grad_pre, weight[...], ((1,), (1,)))
     grad_a[...] = grad[:half]
     grad_b[...] = grad[half:]
     for side in range(2):
@@ -321,7 +329,7 @@
                     pl.ds(q * BS + odd * 32, 32), lanes
                 ]
         output[:, lanes] = strip[side * NODE : (side + 1) * NODE]
-    turned[...] = jnp.dot(rows.T, grad_pre, precision=precise, preferred_element_type=f32)
+    turned[...] = product(rows.T, grad_pre, ((1,), (0,)))
     local_b = jnp.sum(grad_pre, axis=0, keepdims=True)
     for f in range(SIDE):
         ahead = ((where[0] + f) & 3) * 2

time: 208 us -> 207 us (level)
  Pallas kernels: 23.2 us -> 21 us
where the time goes in v4:
time: 207 us; the launch traced here: 206 us
  starting transfers between devices  102 us (49%)
  waiting for transfers between devices  56.8 us (27%)
  blocking collectives  23.3 us (11%)
  Pallas kernels  21 us (10%)
    all_to_all x1, blocking collectives, on_device(): lax.all_to_all(sent, ('row', 'col'), split_axis=0, concat_axis=0, tiled=T...  23.3 us
    ppermute x3, starting transfers between devices, on_device(): lax.ppermute(half[4 + e], 'row', row_hop(e, 0))  18.6 us
    ppermute x3, starting transfers between devices, on_device(): lax.ppermute(half[d], 'row', row_hop(0, d))  12.4 us
    ppermute x3, waiting for transfers between devices, on_device(): lax.ppermute(own, 'col', col_hop(f, 0))  11.1 us
    ppermute x3, starting transfers between devices, on_device(): lax.ppermute(sums_x[f], 'col', col_hop(f, 0))  9.94 us
    ppermute x3, waiting for transfers between devices, on_device(): got_w = [lax.ppermute(sums, 'col', col_hop(f, 0)) for f in (1, 2, 3)]  9.75 us
    ppermute x3, starting transfers between devices, on_device(): lax.ppermute(sum_a[e], 'row', row_hop(e, 0))  9.59 us
    ppermute x3, starting transfers between devices, on_device(): got_w = [lax.ppermute(sums, 'row', row_hop(e, 0)) for e in (1, 3, 2)]  9.13 us
  transfers between devices with their start and end apart: 49, of which 19 were waited for; matrix products, arithmetic and copies ran while one was open for 1% of the time, Pallas kernels for 4%

profile of v4, /device:TPU:0, one launch (start us, length us, event | category | flops | bytes accessed | tf_op | source)
XLA Modules:
  0.0 206.4 jit_solution(9905377107006589930)
XLA Ops:
  0.6 1.4 pack.1
  2.0 23.3 %all_to_all.5.got = f32[128,2,384]{2,1,0:T(2,128)S(1)} all-to-all(f32[128,2,384]{2,1,0:T(2,128)S(1)} %pack.1), channel_id=1, replica_groups=mesh['row'=16,'col'=8] {'row','col'}, dimensions={0} | all-to-all | bytes 786432 | tf_op jit(solution)/shard_map/all_to_all | solution.py:432
  26.2 1.7 collective-permute-start.3
  27.9 1.4 collective-permute-start.5
  29.3 11.0 %collective-permute-done.1.refs_2_ = f32[256,256]{1,0:T(8,128)S(1)} collective-permute-done((f32[256,256]{1,0:T(8,128)S(1)}, f32[256,256]{1,0:T(8,128)S(1)}, u32[]{:S(2)}, u32[]{:S(2)}) %collective-permute-start.1) | collective-permute-done | bytes 262176 | tf_op jit(solution)/shard_map/ppermute | solution.py:436
  42.3 3.9 %prepare.1.blocks = bf16[256,64,256]{2,1,0:T(8,128)(2,1)} custom-call(s32[1]{0:T(128)} %bitcast.12.count, f32[256,4096]{1,0:T(8,128)} %bitcast.20), custom_call_target="tpu_custom_call" | custom-call | flops 100000000 | bytes 12582912 | tf_op jit(solution)/shard_map/prepare/pallas_call | solution.py:166
  46.2 3.5 %shard_map.120 = (f32[512,256]{1,0:T(8,128)S(1)}, f32[512,256]{1,0:T(8,128)S(1)}, f32[512,256]{1,0:T(8,128)S(1)}, f32[512,256]{1,0:T(8,128)S(1)}, f32[512,256]{1...) custom-call(s32[256]{0:T(256)S(1)} %bitcast.15, s32[256]{0:T(256)S(1)} %bitcast.16, ...), custom_call_target="tpu_custom_call" | custom-call | flops 2147483648 | bytes 16777216 | tf_op jit(solution)/shard_map/pallas_call | solution.py:260
  49.7 10.2 %collective-permute-start.7 = (f32[512,256]{1,0:T(8,128)S(1)}, f32[512,256]{1,0:T(8,128)S(1)}, u32[]{:S(2)}, u32[]{:S(2)}) collective-permute-start(f32[512,256]{1,0:T(8,128)S(1)} %get-tuple-element.33), channel_id=1, source_target_pairs={{0,8},{8,16},{16,24},{24,0},{32,40},{40,48},{48,56},{56,32},{64,72... | collective-permute-start | bytes 1572872 | tf_op jit(solution)/shard_map/ppermute | solution.py:445
  60.0 2.1 %collective-permute-start.8 = (f32[512,256]{1,0:T(8,128)S(1)}, f32[512,256]{1,0:T(8,128)S(1)}, u32[]{:S(2)}, u32[]{:S(2)}) collective-permute-start(f32[512,256]{1,0:T(8,128)S(1)} %get-tuple-element.36), channel_id=1, source_target_pairs={{0,16},{8,24},{16,0},{24,8},{32,48},{40,56},{48,32},{56,40},{64,80... | collective-permute-start | bytes 1572872 | tf_op jit(solution)/shard_map/ppermute | solution.py:445
  62.1 2.0 collective-permute-start.15
  64.1 1.1 collective-permute-start.14
  65.2 6.0 %collective-permute-done.7 = f32[512,256]{1,0:T(8,128)S(1)} collective-permute-done((f32[512,256]{1,0:T(8,128)S(1)}, f32[512,256]{1,0:T(8,128)S(1)}, u32[]{:S(2)}, u32[]{:S(2)}) %collective-permute-start.7) | collective-permute-done | bytes 524320 | tf_op jit(solution)/shard_map/ppermute | solution.py:445
  71.2 15.5 %collective-permute-start.13 = (f32[512,256]{1,0:T(8,128)S(1)}, f32[512,256]{1,0:T(8,128)S(1)}, u32[]{:S(2)}, u32[]{:S(2)}) collective-permute-start(f32[512,256]{1,0:T(8,128)S(1)} %get-tuple-element.39), channel_id=1, source_target_pairs={{0,32},{8,40},{16,48},{24,56},{32,64},{40,72},{48,80},{56,88},{64,... | collective-permute-start | bytes 1572872 | tf_op jit(solution)/shard_map/ppermute | solution.py:446
  86.7 5.1 %prepare_back.1.blocks = bf16[256,64,256]{2,1,0:T(8,128)(2,1)} custom-call(s32[1]{0:T(128)} %bitcast.11.count, f32[256,4096]{1,0:T(8,128)} %bitcast.21), custom_call_target="tpu_custom_call" | custom-call | flops 100000000 | bytes 12582912 | tf_op jit(solution)/shard_map/prepare_back/pallas_call | solution.py:166
  91.9 6.8 %collective-permute-start.10 = (f32[128,256]{1,0:T(8,128)S(1)}, f32[128,256]{1,0:T(8,128)S(1)}, u32[]{:S(2)}, u32[]{:S(2)}) collective-permute-start(f32[128,256]{1,0:T(8,128)S(1)} %get-tuple-element.68), channel_id=1, source_target_pairs={{0,32},{8,40},{16,48},{24,56},{32,64},{40,72},{48,80},{56,88},{64,... | collective-permute-start | bytes 393224 | tf_op jit(solution)/shard_map/ppermute | solution.py:459
  98.8 2.8 %collective-permute-start.12 = (f32[128,256]{1,0:T(8,128)S(1)}, f32[128,256]{1,0:T(8,128)S(1)}, u32[]{:S(2)}, u32[]{:S(2)}) collective-permute-start(f32[128,256]{1,0:T(8,128)S(1)} %get-tuple-element.66), channel_id=1, source_target_pairs={{0,96},{8,104},{16,112},{24,120},{32,0},{40,8},{48,16},{56,24},{64... | collective-permute-start | bytes 393224 | tf_op jit(solution)/shard_map/ppermute | solution.py:459
  101.8 2.4 %collective-permute-start.17 = (f32[128,256]{1,0:T(8,128)S(1)}, f32[128,256]{1,0:T(8,128)S(1)}, u32[]{:S(2)}, u32[]{:S(2)}) collective-permute-start(f32[128,256]{1,0:T(8,128)S(1)} %get-tuple-element.63), channel_id=1, source_target_pairs={{0,16},{8,24},{16,0},{24,8},{32,48},{40,56},{48,32},{56,40},{64,80... | collective-permute-start | bytes 393224 | tf_op jit(solution)/shard_map/ppermute | solution.py:460
  104.1 2.5 %collective-permute-start.18 = (f32[128,256]{1,0:T(8,128)S(1)}, f32[128,256]{1,0:T(8,128)S(1)}, u32[]{:S(2)}, u32[]{:S(2)}) collective-permute-start(f32[128,256]{1,0:T(8,128)S(1)} %get-tuple-element.62), channel_id=1, source_target_pairs={{0,24},{8,0},{16,8},{24,16},{32,56},{40,32},{48,40},{56,48},{64,88... | collective-permute-start | bytes 393224 | tf_op jit(solution)/shard_map/ppermute | solution.py:460
  106.8 3.5 %collective-permute-done.16.refs_6_ = f32[128,256]{1,0:T(8,128)S(1)} collective-permute-done((f32[128,256]{1,0:T(8,128)S(1)}, f32[128,256]{1,0:T(8,128)S(1)}, u32[]{:S(2)}, u32[]{:S(2)}) %collective-permute-start.16) | collective-permute-done | bytes 131104 | tf_op jit(solution)/shard_map/ppermute | solution.py:460
  110.9 1.7 middle.1
  112.6 1.0 collective-permute-start.21
  114.8 2.5 %collective-permute-start.24 = (f32[128,256]{1,0:T(8,128)S(1)}, f32[128,256]{1,0:T(8,128)S(1)}, u32[]{:S(2)}, u32[]{:S(2)}) collective-permute-start(f32[128,256]{1,0:T(8,128)S(1)} %get-tuple-element.45), channel_id=1, source_target_pairs={{0,24},{8,0},{16,8},{24,16},{32,56},{40,32},{48,40},{56,48},{64,88... | collective-permute-start | bytes 393224 | tf_op jit(solution)/shard_map/ppermute | solution.py:469
  118.6 1.8 collective-permute-done.20
  120.4 1.3 collective-permute-done.19
  121.7 2.2 %collective-permute-done.23 = f32[128,256]{1,0:T(8,128)S(1)} collective-permute-done((f32[128,256]{1,0:T(8,128)S(1)}, f32[128,256]{1,0:T(8,128)S(1)}, u32[]{:S(2)}, u32[]{:S(2)}) %collective-permute-start.23) | collective-permute-done | bytes 131104 | tf_op jit(solution)/shard_map/ppermute | solution.py:469
  123.9 1.3 collective-permute-done.22
  125.4 2.5 %collective-permute-start.28 = (f32[40,256]{1,0:T(8,128)S(1)}, f32[40,256]{1,0:T(8,128)S(1)}, u32[]{:S(2)}, u32[]{:S(2)}) collective-permute-start(f32[40,256]{1,0:T(8,128)S(1)} %get-tuple-element.71), channel_id=1, source_target_pairs={{0,6},{1,7},{2,0},{3,1},{4,2},{5,3},{6,4},{7,5},{8,14},{9,15},{10,... | collective-permute-start | bytes 122888 | tf_op jit(solution)/shard_map/ppermute | solution.py:483
  127.9 0.9 collective-permute-start.26
  129.5 3.9 %collective-permute-done.27 = f32[40,256]{1,0:T(8,128)S(1)} collective-permute-done((f32[40,256]{1,0:T(8,128)S(1)}, f32[40,256]{1,0:T(8,128)S(1)}, u32[]{:S(2)}, u32[]{:S(2)}) %collective-permute-start.27) | collective-permute-done | bytes 40992 | tf_op jit(solution)/shard_map/ppermute | solution.py:483
  134.2 2.7 %collective-permute-start.31 = (f32[40,256]{1,0:T(8,128)S(1)}, f32[40,256]{1,0:T(8,128)S(1)}, u32[]{:S(2)}, u32[]{:S(2)}) collective-permute-start(f32[40,256]{1,0:T(8,128)S(1)} %fusion.1), channel_id=1, source_target_pairs={{0,24},{8,0},{16,8},{24,16},{32,56},{40,32},{48,40},{56,48},{64,88... | collective-permute-start | bytes 122888 | tf_op jit(solution)/shard_map/ppermute | solution.py:485
  136.9 1.4 collective-permute-start.29
  138.3 2.1 %collective-permute-start.33 = (f32[512,256]{1,0:T(8,128)S(1)}, f32[512,256]{1,0:T(8,128)S(1)}, u32[]{:S(2)}, u32[]{:S(2)}) collective-permute-start(f32[512,256]{1,0:T(8,128)S(1)} %pad_maximum_fusion.refs_0_), channel_id=1, source_target_pairs={{0,16},{8,24},{16,0},{24,8},{32,48},{40,56},{48,32},{56,40},{64,80... | collective-permute-start | bytes 1572872 | tf_op jit(solution)/shard_map/ppermute | solution.py:476
  140.4 1.9 collective-permute-start.34
  142.4 1.9 collective-permute-start.35
  144.3 4.2 %collective-permute-start.36 = (f32[512,256]{1,0:T(8,128)S(1)}, f32[512,256]{1,0:T(8,128)S(1)}, u32[]{:S(2)}, u32[]{:S(2)}) collective-permute-start(f32[512,256]{1,0:T(8,128)S(1)} %pad_maximum_fusion.1.refs_4_), channel_id=1, source_target_pairs={{0,64},{8,72},{16,80},{24,88},{32,96},{40,104},{48,112},{56,120},{... | collective-permute-start | bytes 1572872 | tf_op jit(solution)/shard_map/ppermute | solution.py:477
  148.5 2.5 %collective-permute-start.37 = (f32[512,256]{1,0:T(8,128)S(1)}, f32[512,256]{1,0:T(8,128)S(1)}, u32[]{:S(2)}, u32[]{:S(2)}) collective-permute-start(f32[512,256]{1,0:T(8,128)S(1)} %pad_maximum_fusion.1.refs_4_), channel_id=1, source_target_pairs={{0,96},{8,104},{16,112},{24,120},{32,0},{40,8},{48,16},{56,24},{64... | collective-permute-start | bytes 1572872 | tf_op jit(solution)/shard_map/ppermute | solution.py:477
  151.1 7.3 %collective-permute-done.34.refs_3_ = f32[512,256]{1,0:T(8,128)S(1)} collective-permute-done((f32[512,256]{1,0:T(8,128)S(1)}, f32[512,256]{1,0:T(8,128)S(1)}, u32[]{:S(2)}, u32[]{:S(2)}) %collective-permute-start.34) | collective-permute-done | bytes 524320 | tf_op jit(solution)/shard_map/ppermute | solution.py:476
  158.4 4.0 %collective-permute-done.36.refs_6_ = f32[512,256]{1,0:T(8,128)S(1)} collective-permute-done((f32[512,256]{1,0:T(8,128)S(1)}, f32[512,256]{1,0:T(8,128)S(1)}, u32[]{:S(2)}, u32[]{:S(2)}) %collective-permute-start.36) | collective-permute-done | bytes 524320 | tf_op jit(solution)/shard_map/ppermute | solution.py:477
  163.0 3.4 %shard_map.121 = (f32[1024,256]{1,0:T(8,128)S(1)}, f32[1024,256]{1,0:T(8,128)S(1)}) custom-call(s32[256]{0:T(256)S(1)} %bitcast.18, s32[256]{0:T(256)S(1)} %bitcast.17, s32[1]{0:T(128)} %bitcast.14.count, bf16[256,64,256]{2,1,0:T(8,128)(2,1)} %prepare_back.1.blocks, f32[512,256]{1,0:T(8,128)S(1)} %pad_maximum_fusion.refs_0_, ...), custom_call_target="tpu_custom_call" | custom-call | flops 2147483648 | bytes 16777216 | tf_op jit(solution)/shard_map/pallas_call | solution.py:260
  167.0 2.2 %collective-permute-done.42 = f32[40,256]{1,0:T(8,128)S(1)} collective-permute-done((f32[40,256]{1,0:T(8,128)S(1)}, f32[40,256]{1,0:T(8,128)S(1)}, u32[]{:S(2)}, u32[]{:S(2)}) %collective-permute-start.42) | collective-permute-done | bytes 40992 | tf_op jit(solution)/shard_map/ppermute | solution.py:488
  169.2 7.0 %collective-permute-start.44 = (f32[80,256]{1,0:T(8,128)S(1)}, f32[80,256]{1,0:T(8,128)S(1)}, u32[]{:S(2)}, u32[]{:S(2)}) collective-permute-start(f32[80,256]{1,0:T(8,128)S(1)} %constant_dynamic-update-slice_fusion), channel_id=1, source_target_pairs={{0,32},{8,40},{16,48},{24,56},{32,64},{40,72},{48,80},{56,88},{64,... | collective-permute-start | bytes 245768 | tf_op jit(solution)/shard_map/ppermute | solution.py:492
  176.2 2.1 %collective-permute-start.43 = (f32[80,256]{1,0:T(8,128)S(1)}, f32[80,256]{1,0:T(8,128)S(1)}, u32[]{:S(2)}, u32[]{:S(2)}) collective-permute-start(f32[80,256]{1,0:T(8,128)S(1)} %constant_dynamic-update-slice_fusion), channel_id=1, source_target_pairs={{0,64},{8,72},{16,80},{24,88},{32,96},{40,104},{48,112},{56,120},{... | collective-permute-start | bytes 245768 | tf_op jit(solution)/shard_map/ppermute | solution.py:492
  178.7 9.9 %collective-permute-start.40 = (f32[256,256]{1,0:T(8,128)S(1)}, f32[256,256]{1,0:T(8,128)S(1)}, u32[]{:S(2)}, u32[]{:S(2)}) collective-permute-start(f32[256,256]{1,0:T(8,128)S(1)} %get-tuple-element.59), channel_id=1, source_target_pairs={{0,4},{1,5},{2,6},{3,7},{4,0},{5,1},{6,2},{7,3},{8,12},{9,13},{10,... | collective-permute-start | bytes 786440 | tf_op jit(solution)/shard_map/ppermute | solution.py:497
  188.6 2.1 %collective-permute-start.46 = (f32[80,256]{1,0:T(8,128)S(1)}, f32[80,256]{1,0:T(8,128)S(1)}, u32[]{:S(2)}, u32[]{:S(2)}) collective-permute-start(f32[80,256]{1,0:T(8,128)S(1)} %add_add_fusion.refs_4_), channel_id=1, source_target_pairs={{0,2},{1,3},{2,4},{3,5},{4,6},{5,7},{6,0},{7,1},{8,10},{9,11},{10,... | collective-permute-start | bytes 245768 | tf_op jit(solution)/shard_map/ppermute | solution.py:498
  191.4 7.7 %collective-permute-done.46.refs_5_ = f32[80,256]{1,0:T(8,128)S(1)} collective-permute-done((f32[80,256]{1,0:T(8,128)S(1)}, f32[80,256]{1,0:T(8,128)S(1)}, u32[]{:S(2)}, u32[]{:S(2)}) %collective-permute-start.46) | collective-permute-done | bytes 81952 | tf_op jit(solution)/shard_map/ppermute | solution.py:498
  199.1 3.8 %collective-permute-start.48 = (f32[80,256]{1,0:T(8,128)S(1)}, f32[80,256]{1,0:T(8,128)S(1)}, u32[]{:S(2)}, u32[]{:S(2)}) collective-permute-start(f32[80,256]{1,0:T(8,128)S(1)} %add_add_fusion.refs_4_), channel_id=1, source_target_pairs={{0,6},{1,7},{2,0},{3,1},{4,2},{5,3},{6,4},{7,5},{8,14},{9,15},{10,... | collective-permute-start | bytes 245768 | tf_op jit(solution)/shard_map/ppermute | solution.py:498
  203.2 1.7 collective-permute-done.48.refs_7_
  204.9 1.5 finish.1
  (82 shorter events, 9.9 us)
Async XLA Ops:
  25.9 14.4 %collective-permute-start.1 = (f32[256,256]{1,0:T(8,128)S(1)}, f32[256,256]{1,0:T(8,128)S(1)}, u32[]{:S(2)}, u32[]{:S(2)}) collective-permute-start(f32[256,256]{1,0:T(8,128)S(1)} %place.1.refs_0_), channel_id=1, source_target_pairs={{0,2},{1,3},{2,4},{3,5},{4,6},{5,7},{6,0},{7,1},{8,10},{9,11},{10,... | collective-permute-start | bytes 786440 | tf_op jit(solution)/shard_map/ppermute | solution.py:436
  26.2 14.1 %collective-permute-start.3 = (f32[256,256]{1,0:T(8,128)S(1)}, f32[256,256]{1,0:T(8,128)S(1)}, u32[]{:S(2)}, u32[]{:S(2)}) collective-permute-start(f32[256,256]{1,0:T(8,128)S(1)} %place.1.refs_0_), channel_id=1, source_target_pairs={{0,4},{1,5},{2,6},{3,7},{4,0},{5,1},{6,2},{7,3},{8,12},{9,13},{10,... | collective-permute-start | bytes 786440 | tf_op jit(solution)/shard_map/ppermute | solution.py:436
  27.9 13.0 %collective-permute-start.5 = (f32[256,256]{1,0:T(8,128)S(1)}, f32[256,256]{1,0:T(8,128)S(1)}, u32[]{:S(2)}, u32[]{:S(2)}) collective-permute-start(f32[256,256]{1,0:T(8,128)S(1)} %place.1.refs_0_), channel_id=1, source_target_pairs={{0,6},{1,7},{2,0},{3,1},{4,2},{5,3},{6,4},{7,5},{8,14},{9,15},{10,... | collective-permute-start | bytes 786440 | tf_op jit(solution)/shard_map/ppermute | solution.py:436
  29.3 16.9 %collective-permute-start = (f32[256,256]{1,0:T(8,128)S(1)}, f32[256,256]{1,0:T(8,128)S(1)}, u32[]{:S(2)}, u32[]{:S(2)}) collective-permute-start(f32[256,256]{1,0:T(8,128)S(1)} %place.1.refs_0_), channel_id=1, source_target_pairs={{0,1},{1,0},{2,3},{3,2},{4,5},{5,4},{6,7},{7,6},{8,9},{9,8},{10,11... | collective-permute-start | bytes 786440 | tf_op jit(solution)/shard_map/ppermute | solution.py:439
  40.3 5.9 %collective-permute-start.2 = (f32[256,256]{1,0:T(8,128)S(1)}, f32[256,256]{1,0:T(8,128)S(1)}, u32[]{:S(2)}, u32[]{:S(2)}) collective-permute-start(f32[256,256]{1,0:T(8,128)S(1)} %collective-permute-done.1.refs_2_), channel_id=1, source_target_pairs={{0,1},{1,0},{2,3},{3,2},{4,5},{5,4},{6,7},{7,6},{8,9},{9,8},{10,11... | collective-permute-start | bytes 786440 | tf_op jit(solution)/shard_map/ppermute | solution.py:439
  40.3 5.9 %collective-permute-start.4 = (f32[256,256]{1,0:T(8,128)S(1)}, f32[256,256]{1,0:T(8,128)S(1)}, u32[]{:S(2)}, u32[]{:S(2)}) collective-permute-start(f32[256,256]{1,0:T(8,128)S(1)} %collective-permute-done.3.refs_4_), channel_id=1, source_target_pairs={{0,1},{1,0},{2,3},{3,2},{4,5},{5,4},{6,7},{7,6},{8,9},{9,8},{10,11... | collective-permute-start | bytes 786440 | tf_op jit(solution)/shard_map/ppermute | solution.py:439
  40.9 5.3 %collective-permute-start.6 = (f32[256,256]{1,0:T(8,128)S(1)}, f32[256,256]{1,0:T(8,128)S(1)}, u32[]{:S(2)}, u32[]{:S(2)}) collective-permute-start(f32[256,256]{1,0:T(8,128)S(1)} %collective-permute-done.5.refs_6_), channel_id=1, source_target_pairs={{0,1},{1,0},{2,3},{3,2},{4,5},{5,4},{6,7},{7,6},{8,9},{9,8},{10,11... | collective-permute-start | bytes 786440 | tf_op jit(solution)/shard_map/ppermute | solution.py:439
  49.7 21.5 %collective-permute-start.7 = (f32[512,256]{1,0:T(8,128)S(1)}, f32[512,256]{1,0:T(8,128)S(1)}, u32[]{:S(2)}, u32[]{:S(2)}) collective-permute-start(f32[512,256]{1,0:T(8,128)S(1)} %get-tuple-element.33), channel_id=1, source_target_pairs={{0,8},{8,16},{16,24},{24,0},{32,40},{40,48},{48,56},{56,32},{64,72... | collective-permute-start | bytes 1572872 | tf_op jit(solution)/shard_map/ppermute | solution.py:445
  60.0 31.8 %collective-permute-start.9 = (f32[512,256]{1,0:T(8,128)S(1)}, f32[512,256]{1,0:T(8,128)S(1)}, u32[]{:S(2)}, u32[]{:S(2)}) collective-permute-start(f32[512,256]{1,0:T(8,128)S(1)} %get-tuple-element.37), channel_id=1, source_target_pairs={{0,24},{8,0},{16,8},{24,16},{32,56},{40,32},{48,40},{56,48},{64,88... | collective-permute-start | bytes 1572872 | tf_op jit(solution)/shard_map/ppermute | solution.py:445
  60.0 31.8 %collective-permute-start.8 = (f32[512,256]{1,0:T(8,128)S(1)}, f32[512,256]{1,0:T(8,128)S(1)}, u32[]{:S(2)}, u32[]{:S(2)}) collective-permute-start(f32[512,256]{1,0:T(8,128)S(1)} %get-tuple-element.36), channel_id=1, source_target_pairs={{0,16},{8,24},{16,0},{24,8},{32,48},{40,56},{48,32},{56,40},{64,80... | collective-permute-start | bytes 1572872 | tf_op jit(solution)/shard_map/ppermute | solution.py:445
  62.1 36.7 %collective-permute-start.15 = (f32[512,256]{1,0:T(8,128)S(1)}, f32[512,256]{1,0:T(8,128)S(1)}, u32[]{:S(2)}, u32[]{:S(2)}) collective-permute-start(f32[512,256]{1,0:T(8,128)S(1)} %get-tuple-element.41), channel_id=1, source_target_pairs={{0,96},{8,104},{16,112},{24,120},{32,0},{40,8},{48,16},{56,24},{64... | collective-permute-start | bytes 1572872 | tf_op jit(solution)/shard_map/ppermute | solution.py:446
  64.1 37.4 %collective-permute-start.14 = (f32[512,256]{1,0:T(8,128)S(1)}, f32[512,256]{1,0:T(8,128)S(1)}, u32[]{:S(2)}, u32[]{:S(2)}) collective-permute-start(f32[512,256]{1,0:T(8,128)S(1)} %get-tuple-element.40), channel_id=1, source_target_pairs={{0,64},{8,72},{16,80},{24,88},{32,96},{40,104},{48,112},{56,120},{... | collective-permute-start | bytes 1572872 | tf_op jit(solution)/shard_map/ppermute | solution.py:446
  71.2 30.3 %collective-permute-start.13 = (f32[512,256]{1,0:T(8,128)S(1)}, f32[512,256]{1,0:T(8,128)S(1)}, u32[]{:S(2)}, u32[]{:S(2)}) collective-permute-start(f32[512,256]{1,0:T(8,128)S(1)} %get-tuple-element.39), channel_id=1, source_target_pairs={{0,32},{8,40},{16,48},{24,56},{32,64},{40,72},{48,80},{56,88},{64,... | collective-permute-start | bytes 1572872 | tf_op jit(solution)/shard_map/ppermute | solution.py:446
  91.9 12.2 %collective-permute-start.10 = (f32[128,256]{1,0:T(8,128)S(1)}, f32[128,256]{1,0:T(8,128)S(1)}, u32[]{:S(2)}, u32[]{:S(2)}) collective-permute-start(f32[128,256]{1,0:T(8,128)S(1)} %get-tuple-element.68), channel_id=1, source_target_pairs={{0,32},{8,40},{16,48},{24,56},{32,64},{40,72},{48,80},{56,88},{64,... | collective-permute-start | bytes 393224 | tf_op jit(solution)/shard_map/ppermute | solution.py:459
  98.8 8.0 %collective-permute-start.11 = (f32[128,256]{1,0:T(8,128)S(1)}, f32[128,256]{1,0:T(8,128)S(1)}, u32[]{:S(2)}, u32[]{:S(2)}) collective-permute-start(f32[128,256]{1,0:T(8,128)S(1)} %get-tuple-element.67), channel_id=1, source_target_pairs={{0,64},{8,72},{16,80},{24,88},{32,96},{40,104},{48,112},{56,120},{... | collective-permute-start | bytes 393224 | tf_op jit(solution)/shard_map/ppermute | solution.py:459
  98.8 8.0 %collective-permute-start.12 = (f32[128,256]{1,0:T(8,128)S(1)}, f32[128,256]{1,0:T(8,128)S(1)}, u32[]{:S(2)}, u32[]{:S(2)}) collective-permute-start(f32[128,256]{1,0:T(8,128)S(1)} %get-tuple-element.66), channel_id=1, source_target_pairs={{0,96},{8,104},{16,112},{24,120},{32,0},{40,8},{48,16},{56,24},{64... | collective-permute-start | bytes 393224 | tf_op jit(solution)/shard_map/ppermute | solution.py:459
  101.7 8.6 %collective-permute-start.16 = (f32[128,256]{1,0:T(8,128)S(1)}, f32[128,256]{1,0:T(8,128)S(1)}, u32[]{:S(2)}, u32[]{:S(2)}) collective-permute-start(f32[128,256]{1,0:T(8,128)S(1)} %get-tuple-element.64), channel_id=1, source_target_pairs={{0,8},{8,16},{16,24},{24,0},{32,40},{40,48},{48,56},{56,32},{64,72... | collective-permute-start | bytes 393224 | tf_op jit(solution)/shard_map/ppermute | solution.py:460
  101.8 8.5 %collective-permute-start.17 = (f32[128,256]{1,0:T(8,128)S(1)}, f32[128,256]{1,0:T(8,128)S(1)}, u32[]{:S(2)}, u32[]{:S(2)}) collective-permute-start(f32[128,256]{1,0:T(8,128)S(1)} %get-tuple-element.63), channel_id=1, source_target_pairs={{0,16},{8,24},{16,0},{24,8},{32,48},{40,56},{48,32},{56,40},{64,80... | collective-permute-start | bytes 393224 | tf_op jit(solution)/shard_map/ppermute | solution.py:460
  104.1 6.8 %collective-permute-start.18 = (f32[128,256]{1,0:T(8,128)S(1)}, f32[128,256]{1,0:T(8,128)S(1)}, u32[]{:S(2)}, u32[]{:S(2)}) collective-permute-start(f32[128,256]{1,0:T(8,128)S(1)} %get-tuple-element.62), channel_id=1, source_target_pairs={{0,24},{8,0},{16,8},{24,16},{32,56},{40,32},{48,40},{56,48},{64,88... | collective-permute-start | bytes 393224 | tf_op jit(solution)/shard_map/ppermute | solution.py:460
  112.6 5.5 %collective-permute-start.21 = (f32[128,256]{1,0:T(8,128)S(1)}, f32[128,256]{1,0:T(8,128)S(1)}, u32[]{:S(2)}, u32[]{:S(2)}) collective-permute-start(f32[128,256]{1,0:T(8,128)S(1)} %get-tuple-element.44), channel_id=1, source_target_pairs={{0,96},{8,104},{16,112},{24,120},{32,0},{40,8},{48,16},{56,24},{64... | collective-permute-start | bytes 393224 | tf_op jit(solution)/shard_map/ppermute | solution.py:468
  113.7 6.7 %collective-permute-start.20 = (f32[128,256]{1,0:T(8,128)S(1)}, f32[128,256]{1,0:T(8,128)S(1)}, u32[]{:S(2)}, u32[]{:S(2)}) collective-permute-start(f32[128,256]{1,0:T(8,128)S(1)} %get-tuple-element.44), channel_id=1, source_target_pairs={{0,64},{8,72},{16,80},{24,88},{32,96},{40,104},{48,112},{56,120},{... | collective-permute-start | bytes 393224 | tf_op jit(solution)/shard_map/ppermute | solution.py:468
  113.9 7.7 %collective-permute-start.19 = (f32[128,256]{1,0:T(8,128)S(1)}, f32[128,256]{1,0:T(8,128)S(1)}, u32[]{:S(2)}, u32[]{:S(2)}) collective-permute-start(f32[128,256]{1,0:T(8,128)S(1)} %get-tuple-element.44), channel_id=1, source_target_pairs={{0,32},{8,40},{16,48},{24,56},{32,64},{40,72},{48,80},{56,88},{64,... | collective-permute-start | bytes 393224 | tf_op jit(solution)/shard_map/ppermute | solution.py:468
  114.8 6.8 %collective-permute-start.24 = (f32[128,256]{1,0:T(8,128)S(1)}, f32[128,256]{1,0:T(8,128)S(1)}, u32[]{:S(2)}, u32[]{:S(2)}) collective-permute-start(f32[128,256]{1,0:T(8,128)S(1)} %get-tuple-element.45), channel_id=1, source_target_pairs={{0,24},{8,0},{16,8},{24,16},{32,56},{40,32},{48,40},{56,48},{64,88... | collective-permute-start | bytes 393224 | tf_op jit(solution)/shard_map/ppermute | solution.py:469
  117.3 6.6 %collective-permute-start.23 = (f32[128,256]{1,0:T(8,128)S(1)}, f32[128,256]{1,0:T(8,128)S(1)}, u32[]{:S(2)}, u32[]{:S(2)}) collective-permute-start(f32[128,256]{1,0:T(8,128)S(1)} %get-tuple-element.45), channel_id=1, source_target_pairs={{0,16},{8,24},{16,0},{24,8},{32,48},{40,56},{48,32},{56,40},{64,80... | collective-permute-start | bytes 393224 | tf_op jit(solution)/shard_map/ppermute | solution.py:469
  118.1 7.1 %collective-permute-start.22 = (f32[128,256]{1,0:T(8,128)S(1)}, f32[128,256]{1,0:T(8,128)S(1)}, u32[]{:S(2)}, u32[]{:S(2)}) collective-permute-start(f32[128,256]{1,0:T(8,128)S(1)} %get-tuple-element.45), channel_id=1, source_target_pairs={{0,8},{8,16},{16,24},{24,0},{32,40},{40,48},{48,56},{56,32},{64,72... | collective-permute-start | bytes 393224 | tf_op jit(solution)/shard_map/ppermute | solution.py:469
  120.4 4.9 %collective-permute-start.25 = (f32[160,256]{1,0:T(8,128)S(1)}, f32[160,256]{1,0:T(8,128)S(1)}, u32[]{:S(2)}, u32[]{:S(2)}) collective-permute-start(f32[160,256]{1,0:T(8,128)S(1)} %get-tuple-element.46), channel_id=1, source_target_pairs={{0,1},{1,0},{2,3},{3,2},{4,5},{5,4},{6,7},{7,6},{8,9},{9,8},{10,11... | collective-permute-start | bytes 491528 | tf_op jit(solution)/shard_map/ppermute | solution.py:473
  125.3 23.3 %collective-permute-start.32 = (f32[512,256]{1,0:T(8,128)S(1)}, f32[512,256]{1,0:T(8,128)S(1)}, u32[]{:S(2)}, u32[]{:S(2)}) collective-permute-start(f32[512,256]{1,0:T(8,128)S(1)} %pad_maximum_fusion.refs_0_), channel_id=1, source_target_pairs={{0,8},{8,16},{16,24},{24,0},{32,40},{40,48},{48,56},{56,32},{64,72... | collective-permute-start | bytes 1572872 | tf_op jit(solution)/shard_map/ppermute | solution.py:476
  125.4 4.1 %collective-permute-start.28 = (f32[40,256]{1,0:T(8,128)S(1)}, f32[40,256]{1,0:T(8,128)S(1)}, u32[]{:S(2)}, u32[]{:S(2)}) collective-permute-start(f32[40,256]{1,0:T(8,128)S(1)} %get-tuple-element.71), channel_id=1, source_target_pairs={{0,6},{1,7},{2,0},{3,1},{4,2},{5,3},{6,4},{7,5},{8,14},{9,15},{10,... | collective-permute-start | bytes 122888 | tf_op jit(solution)/shard_map/ppermute | solution.py:483
  127.9 5.6 %collective-permute-start.27 = (f32[40,256]{1,0:T(8,128)S(1)}, f32[40,256]{1,0:T(8,128)S(1)}, u32[]{:S(2)}, u32[]{:S(2)}) collective-permute-start(f32[40,256]{1,0:T(8,128)S(1)} %get-tuple-element.72), channel_id=1, source_target_pairs={{0,4},{1,5},{2,6},{3,7},{4,0},{5,1},{6,2},{7,3},{8,12},{9,13},{10,... | collective-permute-start | bytes 122888 | tf_op jit(solution)/shard_map/ppermute | solution.py:483
  127.9 5.7 %collective-permute-start.26 = (f32[40,256]{1,0:T(8,128)S(1)}, f32[40,256]{1,0:T(8,128)S(1)}, u32[]{:S(2)}, u32[]{:S(2)}) collective-permute-start(f32[40,256]{1,0:T(8,128)S(1)} %get-tuple-element.70), channel_id=1, source_target_pairs={{0,2},{1,3},{2,4},{3,5},{4,6},{5,7},{6,0},{7,1},{8,10},{9,11},{10,... | collective-permute-start | bytes 122888 | tf_op jit(solution)/shard_map/ppermute | solution.py:483
  133.5 6.9 %collective-permute-start.30 = (f32[40,256]{1,0:T(8,128)S(1)}, f32[40,256]{1,0:T(8,128)S(1)}, u32[]{:S(2)}, u32[]{:S(2)}) collective-permute-start(f32[40,256]{1,0:T(8,128)S(1)} %fusion.1), channel_id=1, source_target_pairs={{0,8},{8,16},{16,24},{24,0},{32,40},{40,48},{48,56},{56,32},{64,72... | collective-permute-start | bytes 122888 | tf_op jit(solution)/shard_map/ppermute | solution.py:485
  134.2 8.2 %collective-permute-start.31 = (f32[40,256]{1,0:T(8,128)S(1)}, f32[40,256]{1,0:T(8,128)S(1)}, u32[]{:S(2)}, u32[]{:S(2)}) collective-permute-start(f32[40,256]{1,0:T(8,128)S(1)} %fusion.1), channel_id=1, source_target_pairs={{0,24},{8,0},{16,8},{24,16},{32,56},{40,32},{48,40},{56,48},{64,88... | collective-permute-start | bytes 122888 | tf_op jit(solution)/shard_map/ppermute | solution.py:485
  136.9 7.4 %collective-permute-start.29 = (f32[40,256]{1,0:T(8,128)S(1)}, f32[40,256]{1,0:T(8,128)S(1)}, u32[]{:S(2)}, u32[]{:S(2)}) collective-permute-start(f32[40,256]{1,0:T(8,128)S(1)} %fusion.1), channel_id=1, source_target_pairs={{0,16},{8,24},{16,0},{24,8},{32,48},{40,56},{48,32},{56,40},{64,80... | collective-permute-start | bytes 122888 | tf_op jit(solution)/shard_map/ppermute | solution.py:485
  138.3 12.8 %collective-permute-start.33 = (f32[512,256]{1,0:T(8,128)S(1)}, f32[512,256]{1,0:T(8,128)S(1)}, u32[]{:S(2)}, u32[]{:S(2)}) collective-permute-start(f32[512,256]{1,0:T(8,128)S(1)} %pad_maximum_fusion.refs_0_), channel_id=1, source_target_pairs={{0,16},{8,24},{16,0},{24,8},{32,48},{40,56},{48,32},{56,40},{64,80... | collective-permute-start | bytes 1572872 | tf_op jit(solution)/shard_map/ppermute | solution.py:476
  140.4 18.0 %collective-permute-start.34 = (f32[512,256]{1,0:T(8,128)S(1)}, f32[512,256]{1,0:T(8,128)S(1)}, u32[]{:S(2)}, u32[]{:S(2)}) collective-permute-start(f32[512,256]{1,0:T(8,128)S(1)} %pad_maximum_fusion.refs_0_), channel_id=1, source_target_pairs={{0,24},{8,0},{16,8},{24,16},{32,56},{40,32},{48,40},{56,48},{64,88... | collective-permute-start | bytes 1572872 | tf_op jit(solution)/shard_map/ppermute | solution.py:476
  142.4 16.0 %collective-permute-start.35 = (f32[512,256]{1,0:T(8,128)S(1)}, f32[512,256]{1,0:T(8,128)S(1)}, u32[]{:S(2)}, u32[]{:S(2)}) collective-permute-start(f32[512,256]{1,0:T(8,128)S(1)} %pad_maximum_fusion.1.refs_4_), channel_id=1, source_target_pairs={{0,32},{8,40},{16,48},{24,56},{32,64},{40,72},{48,80},{56,88},{64,... | collective-permute-start | bytes 1572872 | tf_op jit(solution)/shard_map/ppermute | solution.py:477
  144.3 18.1 %collective-permute-start.36 = (f32[512,256]{1,0:T(8,128)S(1)}, f32[512,256]{1,0:T(8,128)S(1)}, u32[]{:S(2)}, u32[]{:S(2)}) collective-permute-start(f32[512,256]{1,0:T(8,128)S(1)} %pad_maximum_fusion.1.refs_4_), channel_id=1, source_target_pairs={{0,64},{8,72},{16,80},{24,88},{32,96},{40,104},{48,112},{56,120},{... | collective-permute-start | bytes 1572872 | tf_op jit(solution)/shard_map/ppermute | solution.py:477
  148.5 14.5 %collective-permute-start.37 = (f32[512,256]{1,0:T(8,128)S(1)}, f32[512,256]{1,0:T(8,128)S(1)}, u32[]{:S(2)}, u32[]{:S(2)}) collective-permute-start(f32[512,256]{1,0:T(8,128)S(1)} %pad_maximum_fusion.1.refs_4_), channel_id=1, source_target_pairs={{0,96},{8,104},{16,112},{24,120},{32,0},{40,8},{48,16},{56,24},{64... | collective-permute-start | bytes 1572872 | tf_op jit(solution)/shard_map/ppermute | solution.py:477
  166.4 11.9 %collective-permute-start.38 = (f32[1024,256]{1,0:T(8,128)S(1)}, f32[1024,256]{1,0:T(8,128)S(1)}, u32[]{:S(2)}, u32[]{:S(2)}) collective-permute-start(f32[1024,256]{1,0:T(8,128)S(1)} %get-tuple-element.53), channel_id=1, source_target_pairs={{0,1},{1,0},{2,3},{3,2},{4,5},{5,4},{6,7},{7,6},{8,9},{9,8},{10,11... | collective-permute-start | bytes 3145736 | tf_op jit(solution)/shard_map/ppermute | solution.py:491
  169.2 19.3 %collective-permute-start.44 = (f32[80,256]{1,0:T(8,128)S(1)}, f32[80,256]{1,0:T(8,128)S(1)}, u32[]{:S(2)}, u32[]{:S(2)}) collective-permute-start(f32[80,256]{1,0:T(8,128)S(1)} %constant_dynamic-update-slice_fusion), channel_id=1, source_target_pairs={{0,32},{8,40},{16,48},{24,56},{32,64},{40,72},{48,80},{56,88},{64,... | collective-permute-start | bytes 245768 | tf_op jit(solution)/shard_map/ppermute | solution.py:492
  176.2 12.3 %collective-permute-start.45 = (f32[80,256]{1,0:T(8,128)S(1)}, f32[80,256]{1,0:T(8,128)S(1)}, u32[]{:S(2)}, u32[]{:S(2)}) collective-permute-start(f32[80,256]{1,0:T(8,128)S(1)} %constant_dynamic-update-slice_fusion), channel_id=1, source_target_pairs={{0,96},{8,104},{16,112},{24,120},{32,0},{40,8},{48,16},{56,24},{64... | collective-permute-start | bytes 245768 | tf_op jit(solution)/shard_map/ppermute | solution.py:492
  176.2 12.3 %collective-permute-start.43 = (f32[80,256]{1,0:T(8,128)S(1)}, f32[80,256]{1,0:T(8,128)S(1)}, u32[]{:S(2)}, u32[]{:S(2)}) collective-permute-start(f32[80,256]{1,0:T(8,128)S(1)} %constant_dynamic-update-slice_fusion), channel_id=1, source_target_pairs={{0,64},{8,72},{16,80},{24,88},{32,96},{40,104},{48,112},{56,120},{... | collective-permute-start | bytes 245768 | tf_op jit(solution)/shard_map/ppermute | solution.py:492
  178.6 26.4 %collective-permute-start.39 = (f32[256,256]{1,0:T(8,128)S(1)}, f32[256,256]{1,0:T(8,128)S(1)}, u32[]{:S(2)}, u32[]{:S(2)}) collective-permute-start(f32[256,256]{1,0:T(8,128)S(1)} %get-tuple-element.60), channel_id=1, source_target_pairs={{0,2},{1,3},{2,4},{3,5},{4,6},{5,7},{6,0},{7,1},{8,10},{9,11},{10,... | collective-permute-start | bytes 786440 | tf_op jit(solution)/shard_map/ppermute | solution.py:497
  178.7 26.3 %collective-permute-start.40 = (f32[256,256]{1,0:T(8,128)S(1)}, f32[256,256]{1,0:T(8,128)S(1)}, u32[]{:S(2)}, u32[]{:S(2)}) collective-permute-start(f32[256,256]{1,0:T(8,128)S(1)} %get-tuple-element.59), channel_id=1, source_target_pairs={{0,4},{1,5},{2,6},{3,7},{4,0},{5,1},{6,2},{7,3},{8,12},{9,13},{10,... | collective-permute-start | bytes 786440 | tf_op jit(solution)/shard_map/ppermute | solution.py:497
  188.5 16.4 %collective-permute-start.41 = (f32[256,256]{1,0:T(8,128)S(1)}, f32[256,256]{1,0:T(8,128)S(1)}, u32[]{:S(2)}, u32[]{:S(2)}) collective-permute-start(f32[256,256]{1,0:T(8,128)S(1)} %get-tuple-element.58), channel_id=1, source_target_pairs={{0,6},{1,7},{2,0},{3,1},{4,2},{5,3},{6,4},{7,5},{8,14},{9,15},{10,... | collective-permute-start | bytes 786440 | tf_op jit(solution)/shard_map/ppermute | solution.py:497
  188.6 10.5 %collective-permute-start.46 = (f32[80,256]{1,0:T(8,128)S(1)}, f32[80,256]{1,0:T(8,128)S(1)}, u32[]{:S(2)}, u32[]{:S(2)}) collective-permute-start(f32[80,256]{1,0:T(8,128)S(1)} %add_add_fusion.refs_4_), channel_id=1, source_target_pairs={{0,2},{1,3},{2,4},{3,5},{4,6},{5,7},{6,0},{7,1},{8,10},{9,11},{10,... | collective-permute-start | bytes 245768 | tf_op jit(solution)/shard_map/ppermute | solution.py:498
  190.7 12.5 %collective-permute-start.47 = (f32[80,256]{1,0:T(8,128)S(1)}, f32[80,256]{1,0:T(8,128)S(1)}, u32[]{:S(2)}, u32[]{:S(2)}) collective-permute-start(f32[80,256]{1,0:T(8,128)S(1)} %add_add_fusion.refs_4_), channel_id=1, source_target_pairs={{0,4},{1,5},{2,6},{3,7},{4,0},{5,1},{6,2},{7,3},{8,12},{9,13},{10,... | collective-permute-start | bytes 245768 | tf_op jit(solution)/shard_map/ppermute | solution.py:498
  199.1 5.9 %collective-permute-start.48 = (f32[80,256]{1,0:T(8,128)S(1)}, f32[80,256]{1,0:T(8,128)S(1)}, u32[]{:S(2)}, u32[]{:S(2)}) collective-permute-start(f32[80,256]{1,0:T(8,128)S(1)} %add_add_fusion.refs_4_), channel_id=1, source_target_pairs={{0,6},{1,7},{2,0},{3,1},{4,2},{5,3},{6,4},{7,5},{8,14},{9,15},{10,... | collective-permute-start | bytes 245768 | tf_op jit(solution)/shard_map/ppermute | solution.py:498
  (5 other events, 120.8 us)

commit v5 on v4

--- a/solution.py
+++ b/solution.py
@@ -44,6 +44,10 @@
         for y in range(SIDE)
         for x in range(SIDE)
     ]
+
+
+def row_flip(bit):
+    return [(y * SIDE + x, (y ^ bit) * SIDE + x) for y in range(SIDE) for x in range(SIDE)]
 
 
 def alternate(first, second):
@@ -485,16 +489,16 @@
     got_w = [lax.ppermute(sums, "row", row_hop(0, d)) for d in (1, 3, 2)]
     sums = (sums + got_w[2]) + (got_w[0] + got_w[1])
     bwd_from, sums = lax.optimization_barrier((bwd_from, sums))
-    got_w = lax.ppermute(sums, "col", col_hop(0, 1))
-    sums = jnp.concatenate([sums, got_w], axis=0)
+    sums = sums + lax.ppermute(sums, "row", row_flip(1))
     keep, give = aggregate(bwd_blocks, column, bwd_from, bwd_to, count, 2, COLS * NODE)
     taken = lax.ppermute(give, "col", col_hop(0, 1))
-    got_w = [lax.ppermute(sums, "row", row_hop(e, 0)) for e in (1, 3, 2)]
-    sums = (sums + got_w[2]) + (got_w[0] + got_w[1])
+    sums = sums + lax.ppermute(sums, "row", row_flip(2))
     sums_x = [
         keep[k * NODE : (k + 1) * NODE] + taken[k * NODE : (k + 1) * NODE] for k in range(SIDE)
     ]
     got_x, _ = alternate(lambda f: lax.ppermute(sums_x[f], "col", col_hop(f, 0)), None)
+    got_w = lax.ppermute(sums, "col", col_hop(0, 1))
+    sums = jnp.concatenate([sums, got_w], axis=0)
     got_w = [lax.ppermute(sums, "col", col_hop(f, 0)) for f in (1, 2, 3)]
     grad_x, grad_w, grad_bias = finish(sums_x[:1] + got_x, [sums] + got_w, where)
     return (output, grad_x, grad_w, grad_bias.reshape(F))

time: 207 us -> 209 us (level)
  waiting for transfers between devices: 56.8 us -> 65.5 us
  starting transfers between devices: 102 us -> 95.9 us
    ppermute x3 -> x2, waiting for transfers between devices: 0.01 us -> 7.64 us  [the longest x1 5.5 us: on_device(): sums = sums + lax.ppermute(sums, 'row', row_flip(2))]
    ppermute x3, waiting for transfers between devices: 9.75 us -> 12.9 us  [on_device(): got_w = [lax.ppermute(sums, 'col', col_hop(f, 0)) for f in (1, 2, 3)]]
    ppermute x3, starting transfers between devices: 6.59 us -> 4.35 us  [on_device(): got_w = [lax.ppermute(sums, 'col', col_hop(f, 0)) for f in (1, 2, 3)]]
    ppermute x1, waiting for transfers between devices: 2.2 us -> 0.01 us  [on_device(): got_w = lax.ppermute(sums, 'col', col_hop(0, 1))]
    ppermute x3 -> x2, starting transfers between devices: 9.13 us -> 7.07 us  [the longest x1 7.07 us: on_device(): sums = sums + lax.ppermute(sums, 'row', row_flip(1))]
  transfers between devices with their start and end apart: 49 -> 48, of which waited for: 19 -> 20; matrix products, arithmetic and copies ran while one was open for 1% -> 1% of each run, Pallas kernels for 4% -> 4%
where the time goes in v5:
time: 209 us
  starting transfers between devices  95.9 us (46%)
  waiting for transfers between devices  65.5 us (31%)
  blocking collectives  23.3 us (11%)
  Pallas kernels  21 us (10%)
    all_to_all x1, blocking collectives, on_device(): lax.all_to_all(sent, ('row', 'col'), split_axis=0, concat_axis=0, tiled=T...  23.3 us
    ppermute x3, starting transfers between devices, on_device(): lax.ppermute(half[4 + e], 'row', row_hop(e, 0))  18.6 us
    ppermute x3, waiting for transfers between devices, on_device(): got_w = [lax.ppermute(sums, 'col', col_hop(f, 0)) for f in (1, 2, 3)]  12.9 us
    ppermute x3, starting transfers between devices, on_device(): lax.ppermute(half[d], 'row', row_hop(0, d))  12.3 us
    ppermute x3, waiting for transfers between devices, on_device(): lax.ppermute(own, 'col', col_hop(f, 0))  11.1 us
    ppermute x3, starting transfers between devices, on_device(): lax.ppermute(sum_a[e], 'row', row_hop(e, 0))  9.57 us
    pallas_call x2, Pallas kernels, prepare(): pl.pallas_call(functools.partial(prepare_kernel, flip), out_shape=pltpu.H...  8.97 us
    ppermute x3, starting transfers between devices, on_device(): lax.ppermute(near_b, 'row', row_hop(e, 0))  8.64 us
  transfers between devices with their start and end apart: 48, of which 20 were waited for; matrix products, arithmetic and copies ran while one was open for 1% of the time, Pallas kernels for 4%

profile of v5, /device:TPU:0, one launch (start us, length us, event | category | flops | bytes accessed | tf_op | source)
XLA Modules:
  0.0 208.7 jit_solution(16240347130853285674)
XLA Ops:
  0.6 1.4 pack.1
  2.0 23.3 %all_to_all.5.got = f32[128,2,384]{2,1,0:T(2,128)S(1)} all-to-all(f32[128,2,384]{2,1,0:T(2,128)S(1)} %pack.1), channel_id=1, replica_groups=mesh['row'=16,'col'=8] {'row','col'}, dimensions={0} | all-to-all | bytes 786432 | tf_op jit(solution)/shard_map/all_to_all | solution.py:436
  26.2 1.7 collective-permute-start.3
  27.9 1.4 collective-permute-start.5
  29.3 11.0 %collective-permute-done.1.refs_2_ = f32[256,256]{1,0:T(8,128)S(1)} collective-permute-done((f32[256,256]{1,0:T(8,128)S(1)}, f32[256,256]{1,0:T(8,128)S(1)}, u32[]{:S(2)}, u32[]{:S(2)}) %collective-permute-start.1) | collective-permute-done | bytes 262176 | tf_op jit(solution)/shard_map/ppermute | solution.py:440
  42.3 3.9 %prepare.1.blocks = bf16[256,64,256]{2,1,0:T(8,128)(2,1)} custom-call(s32[1]{0:T(128)} %bitcast.12.count, f32[256,4096]{1,0:T(8,128)} %bitcast.20), custom_call_target="tpu_custom_call" | custom-call | flops 100000000 | bytes 12582912 | tf_op jit(solution)/shard_map/prepare/pallas_call | solution.py:170
  46.2 3.5 %shard_map.120 = (f32[512,256]{1,0:T(8,128)S(1)}, f32[512,256]{1,0:T(8,128)S(1)}, f32[512,256]{1,0:T(8,128)S(1)}, f32[512,256]{1,0:T(8,128)S(1)}, f32[512,256]{1...) custom-call(s32[256]{0:T(256)S(1)} %bitcast.15, s32[256]{0:T(256)S(1)} %bitcast.16, ...), custom_call_target="tpu_custom_call" | custom-call | flops 2147483648 | bytes 16777216 | tf_op jit(solution)/shard_map/pallas_call | solution.py:264
  49.7 10.2 %collective-permute-start.7 = (f32[512,256]{1,0:T(8,128)S(1)}, f32[512,256]{1,0:T(8,128)S(1)}, u32[]{:S(2)}, u32[]{:S(2)}) collective-permute-start(f32[512,256]{1,0:T(8,128)S(1)} %get-tuple-element.33), channel_id=1, source_target_pairs={{0,8},{8,16},{16,24},{24,0},{32,40},{40,48},{48,56},{56,32},{64,72... | collective-permute-start | bytes 1572872 | tf_op jit(solution)/shard_map/ppermute | solution.py:449
  59.9 2.1 %collective-permute-start.8 = (f32[512,256]{1,0:T(8,128)S(1)}, f32[512,256]{1,0:T(8,128)S(1)}, u32[]{:S(2)}, u32[]{:S(2)}) collective-permute-start(f32[512,256]{1,0:T(8,128)S(1)} %get-tuple-element.36), channel_id=1, source_target_pairs={{0,16},{8,24},{16,0},{24,8},{32,48},{40,56},{48,32},{56,40},{64,80... | collective-permute-start | bytes 1572872 | tf_op jit(solution)/shard_map/ppermute | solution.py:449
  62.1 2.0 collective-permute-start.15
  64.1 1.1 collective-permute-start.14
  65.2 6.0 %collective-permute-done.7 = f32[512,256]{1,0:T(8,128)S(1)} collective-permute-done((f32[512,256]{1,0:T(8,128)S(1)}, f32[512,256]{1,0:T(8,128)S(1)}, u32[]{:S(2)}, u32[]{:S(2)}) %collective-permute-start.7) | collective-permute-done | bytes 524320 | tf_op jit(solution)/shard_map/ppermute | solution.py:449
  71.2 15.5 %collective-permute-start.13 = (f32[512,256]{1,0:T(8,128)S(1)}, f32[512,256]{1,0:T(8,128)S(1)}, u32[]{:S(2)}, u32[]{:S(2)}) collective-permute-start(f32[512,256]{1,0:T(8,128)S(1)} %get-tuple-element.39), channel_id=1, source_target_pairs={{0,32},{8,40},{16,48},{24,56},{32,64},{40,72},{48,80},{56,88},{64,... | collective-permute-start | bytes 1572872 | tf_op jit(solution)/shard_map/ppermute | solution.py:450
  86.7 5.1 %prepare_back.1.blocks = bf16[256,64,256]{2,1,0:T(8,128)(2,1)} custom-call(s32[1]{0:T(128)} %bitcast.11.count, f32[256,4096]{1,0:T(8,128)} %bitcast.21), custom_call_target="tpu_custom_call" | custom-call | flops 100000000 | bytes 12582912 | tf_op jit(solution)/shard_map/prepare_back/pallas_call | solution.py:170
  91.9 6.8 %collective-permute-start.10 = (f32[128,256]{1,0:T(8,128)S(1)}, f32[128,256]{1,0:T(8,128)S(1)}, u32[]{:S(2)}, u32[]{:S(2)}) collective-permute-start(f32[128,256]{1,0:T(8,128)S(1)} %get-tuple-element.68), channel_id=1, source_target_pairs={{0,32},{8,40},{16,48},{24,56},{32,64},{40,72},{48,80},{56,88},{64,... | collective-permute-start | bytes 393224 | tf_op jit(solution)/shard_map/ppermute | solution.py:463
  98.7 2.8 %collective-permute-start.12 = (f32[128,256]{1,0:T(8,128)S(1)}, f32[128,256]{1,0:T(8,128)S(1)}, u32[]{:S(2)}, u32[]{:S(2)}) collective-permute-start(f32[128,256]{1,0:T(8,128)S(1)} %get-tuple-element.66), channel_id=1, source_target_pairs={{0,96},{8,104},{16,112},{24,120},{32,0},{40,8},{48,16},{56,24},{64... | collective-permute-start | bytes 393224 | tf_op jit(solution)/shard_map/ppermute | solution.py:463
  101.8 2.4 %collective-permute-start.17 = (f32[128,256]{1,0:T(8,128)S(1)}, f32[128,256]{1,0:T(8,128)S(1)}, u32[]{:S(2)}, u32[]{:S(2)}) collective-permute-start(f32[128,256]{1,0:T(8,128)S(1)} %get-tuple-element.63), channel_id=1, source_target_pairs={{0,16},{8,24},{16,0},{24,8},{32,48},{40,56},{48,32},{56,40},{64,80... | collective-permute-start | bytes 393224 | tf_op jit(solution)/shard_map/ppermute | solution.py:464
  104.1 2.5 %collective-permute-start.18 = (f32[128,256]{1,0:T(8,128)S(1)}, f32[128,256]{1,0:T(8,128)S(1)}, u32[]{:S(2)}, u32[]{:S(2)}) collective-permute-start(f32[128,256]{1,0:T(8,128)S(1)} %get-tuple-element.62), channel_id=1, source_target_pairs={{0,24},{8,0},{16,8},{24,16},{32,56},{40,32},{48,40},{56,48},{64,88... | collective-permute-start | bytes 393224 | tf_op jit(solution)/shard_map/ppermute | solution.py:464
  106.7 3.5 %collective-permute-done.16.refs_6_ = f32[128,256]{1,0:T(8,128)S(1)} collective-permute-done((f32[128,256]{1,0:T(8,128)S(1)}, f32[128,256]{1,0:T(8,128)S(1)}, u32[]{:S(2)}, u32[]{:S(2)}) %collective-permute-start.16) | collective-permute-done | bytes 131104 | tf_op jit(solution)/shard_map/ppermute | solution.py:464
  110.9 1.7 middle.1
  112.6 1.0 collective-permute-start.21
  114.8 2.5 %collective-permute-start.24 = (f32[128,256]{1,0:T(8,128)S(1)}, f32[128,256]{1,0:T(8,128)S(1)}, u32[]{:S(2)}, u32[]{:S(2)}) collective-permute-start(f32[128,256]{1,0:T(8,128)S(1)} %get-tuple-element.45), channel_id=1, source_target_pairs={{0,24},{8,0},{16,8},{24,16},{32,56},{40,32},{48,40},{56,48},{64,88... | collective-permute-start | bytes 393224 | tf_op jit(solution)/shard_map/ppermute | solution.py:473
  118.5 1.8 collective-permute-done.20
  120.3 1.3 collective-permute-done.19
  121.6 2.2 %collective-permute-done.23 = f32[128,256]{1,0:T(8,128)S(1)} collective-permute-done((f32[128,256]{1,0:T(8,128)S(1)}, f32[128,256]{1,0:T(8,128)S(1)}, u32[]{:S(2)}, u32[]{:S(2)}) %collective-permute-start.23) | collective-permute-done | bytes 131104 | tf_op jit(solution)/shard_map/ppermute | solution.py:473
  123.9 1.3 collective-permute-done.22
  125.4 2.5 %collective-permute-start.28 = (f32[40,256]{1,0:T(8,128)S(1)}, f32[40,256]{1,0:T(8,128)S(1)}, u32[]{:S(2)}, u32[]{:S(2)}) collective-permute-start(f32[40,256]{1,0:T(8,128)S(1)} %get-tuple-element.71), channel_id=1, source_target_pairs={{0,6},{1,7},{2,0},{3,1},{4,2},{5,3},{6,4},{7,5},{8,14},{9,15},{10,... | collective-permute-start | bytes 122888 | tf_op jit(solution)/shard_map/ppermute | solution.py:487
  127.9 0.9 collective-permute-start.26
  129.5 3.9 %collective-permute-done.27 = f32[40,256]{1,0:T(8,128)S(1)} collective-permute-done((f32[40,256]{1,0:T(8,128)S(1)}, f32[40,256]{1,0:T(8,128)S(1)}, u32[]{:S(2)}, u32[]{:S(2)}) %collective-permute-start.27) | collective-permute-done | bytes 40992 | tf_op jit(solution)/shard_map/ppermute | solution.py:487
  134.2 2.7 %collective-permute-start.31 = (f32[40,256]{1,0:T(8,128)S(1)}, f32[40,256]{1,0:T(8,128)S(1)}, u32[]{:S(2)}, u32[]{:S(2)}) collective-permute-start(f32[40,256]{1,0:T(8,128)S(1)} %fusion.1), channel_id=1, source_target_pairs={{0,24},{8,0},{16,8},{24,16},{32,56},{40,32},{48,40},{56,48},{64,88... | collective-permute-start | bytes 122888 | tf_op jit(solution)/shard_map/ppermute | solution.py:489
  136.9 1.4 collective-permute-start.29
  138.3 2.1 %collective-permute-start.33 = (f32[512,256]{1,0:T(8,128)S(1)}, f32[512,256]{1,0:T(8,128)S(1)}, u32[]{:S(2)}, u32[]{:S(2)}) collective-permute-start(f32[512,256]{1,0:T(8,128)S(1)} %pad_maximum_fusion.refs_0_), channel_id=1, source_target_pairs={{0,16},{8,24},{16,0},{24,8},{32,48},{40,56},{48,32},{56,40},{64,80... | collective-permute-start | bytes 1572872 | tf_op jit(solution)/shard_map/ppermute | solution.py:480
  140.4 1.9 collective-permute-start.34
  142.4 1.9 collective-permute-start.35
  144.3 4.2 %collective-permute-start.36 = (f32[512,256]{1,0:T(8,128)S(1)}, f32[512,256]{1,0:T(8,128)S(1)}, u32[]{:S(2)}, u32[]{:S(2)}) collective-permute-start(f32[512,256]{1,0:T(8,128)S(1)} %pad_maximum_fusion.1.refs_4_), channel_id=1, source_target_pairs={{0,64},{8,72},{16,80},{24,88},{32,96},{40,104},{48,112},{56,120},{... | collective-permute-start | bytes 1572872 | tf_op jit(solution)/shard_map/ppermute | solution.py:481
  148.5 2.5 %collective-permute-start.37 = (f32[512,256]{1,0:T(8,128)S(1)}, f32[512,256]{1,0:T(8,128)S(1)}, u32[]{:S(2)}, u32[]{:S(2)}) collective-permute-start(f32[512,256]{1,0:T(8,128)S(1)} %pad_maximum_fusion.1.refs_4_), channel_id=1, source_target_pairs={{0,96},{8,104},{16,112},{24,120},{32,0},{40,8},{48,16},{56,24},{64... | collective-permute-start | bytes 1572872 | tf_op jit(solution)/shard_map/ppermute | solution.py:481
  151.1 7.4 %collective-permute-done.34.refs_3_ = f32[512,256]{1,0:T(8,128)S(1)} collective-permute-done((f32[512,256]{1,0:T(8,128)S(1)}, f32[512,256]{1,0:T(8,128)S(1)}, u32[]{:S(2)}, u32[]{:S(2)}) %collective-permute-start.34) | collective-permute-done | bytes 524320 | tf_op jit(solution)/shard_map/ppermute | solution.py:480
  158.4 3.9 %collective-permute-done.36.refs_6_ = f32[512,256]{1,0:T(8,128)S(1)} collective-permute-done((f32[512,256]{1,0:T(8,128)S(1)}, f32[512,256]{1,0:T(8,128)S(1)}, u32[]{:S(2)}, u32[]{:S(2)}) %collective-permute-start.36) | collective-permute-done | bytes 524320 | tf_op jit(solution)/shard_map/ppermute | solution.py:481
  163.0 3.4 %shard_map.121 = (f32[1024,256]{1,0:T(8,128)S(1)}, f32[1024,256]{1,0:T(8,128)S(1)}) custom-call(s32[256]{0:T(256)S(1)} %bitcast.18, s32[256]{0:T(256)S(1)} %bitcast.17, s32[1]{0:T(128)} %bitcast.14.count, bf16[256,64,256]{2,1,0:T(8,128)(2,1)} %prepare_back.1.blocks, f32[512,256]{1,0:T(8,128)S(1)} %pad_maximum_fusion.refs_0_, ...), custom_call_target="tpu_custom_call" | custom-call | flops 2147483648 | bytes 16777216 | tf_op jit(solution)/shard_map/pallas_call | solution.py:264
  166.5 7.1 %collective-permute-start.42 = (f32[40,256]{1,0:T(8,128)S(1)}, f32[40,256]{1,0:T(8,128)S(1)}, u32[]{:S(2)}, u32[]{:S(2)}) collective-permute-start(f32[40,256]{1,0:T(8,128)S(1)} %add_add_fusion), channel_id=1, source_target_pairs={{0,32},{8,40},{16,48},{24,56},{32,0},{40,8},{48,16},{56,24},{64,96... | collective-permute-start | bytes 122888 | tf_op jit(solution)/shard_map/ppermute | solution.py:492
  173.6 2.1 %collective-permute-done.42 = f32[40,256]{1,0:T(8,128)S(1)} collective-permute-done((f32[40,256]{1,0:T(8,128)S(1)}, f32[40,256]{1,0:T(8,128)S(1)}, u32[]{:S(2)}, u32[]{:S(2)}) %collective-permute-start.42) | collective-permute-done | bytes 40992 | tf_op jit(solution)/shard_map/ppermute | solution.py:492
  175.8 5.5 %collective-permute-done.43 = f32[40,256]{1,0:T(8,128)S(1)} collective-permute-done((f32[40,256]{1,0:T(8,128)S(1)}, f32[40,256]{1,0:T(8,128)S(1)}, u32[]{:S(2)}, u32[]{:S(2)}) %collective-permute-start.43) | collective-permute-done | bytes 40992 | tf_op jit(solution)/shard_map/ppermute | solution.py:495
  181.6 8.3 %collective-permute-start.40 = (f32[256,256]{1,0:T(8,128)S(1)}, f32[256,256]{1,0:T(8,128)S(1)}, u32[]{:S(2)}, u32[]{:S(2)}) collective-permute-start(f32[256,256]{1,0:T(8,128)S(1)} %get-tuple-element.59), channel_id=1, source_target_pairs={{0,4},{1,5},{2,6},{3,7},{4,0},{5,1},{6,2},{7,3},{8,12},{9,13},{10,... | collective-permute-start | bytes 786440 | tf_op jit(solution)/shard_map/ppermute | solution.py:499
  189.9 2.1 %collective-permute-start.45 = (f32[80,256]{1,0:T(8,128)S(1)}, f32[80,256]{1,0:T(8,128)S(1)}, u32[]{:S(2)}, u32[]{:S(2)}) collective-permute-start(f32[80,256]{1,0:T(8,128)S(1)} %pad_maximum_fusion.2.refs_4_), channel_id=1, source_target_pairs={{0,2},{1,3},{2,4},{3,5},{4,6},{5,7},{6,0},{7,1},{8,10},{9,11},{10,... | collective-permute-start | bytes 245768 | tf_op jit(solution)/shard_map/ppermute | solution.py:502
  192.0 10.8 %collective-permute-done.45.refs_5_ = f32[80,256]{1,0:T(8,128)S(1)} collective-permute-done((f32[80,256]{1,0:T(8,128)S(1)}, f32[80,256]{1,0:T(8,128)S(1)}, u32[]{:S(2)}, u32[]{:S(2)}) %collective-permute-start.45) | collective-permute-done | bytes 81952 | tf_op jit(solution)/shard_map/ppermute | solution.py:502
  202.8 2.3 %collective-permute-start.47 = (f32[80,256]{1,0:T(8,128)S(1)}, f32[80,256]{1,0:T(8,128)S(1)}, u32[]{:S(2)}, u32[]{:S(2)}) collective-permute-start(f32[80,256]{1,0:T(8,128)S(1)} %pad_maximum_fusion.2.refs_4_), channel_id=1, source_target_pairs={{0,6},{1,7},{2,0},{3,1},{4,2},{5,3},{6,4},{7,5},{8,14},{9,15},{10,... | collective-permute-start | bytes 245768 | tf_op jit(solution)/shard_map/ppermute | solution.py:502
  205.8 1.5 collective-permute-done.47.refs_7_
  207.2 1.5 finish.1
  (80 shorter events, 9.2 us)
Async XLA Ops:
  25.9 14.4 %collective-permute-start.1 = (f32[256,256]{1,0:T(8,128)S(1)}, f32[256,256]{1,0:T(8,128)S(1)}, u32[]{:S(2)}, u32[]{:S(2)}) collective-permute-start(f32[256,256]{1,0:T(8,128)S(1)} %place.1.refs_0_), channel_id=1, source_target_pairs={{0,2},{1,3},{2,4},{3,5},{4,6},{5,7},{6,0},{7,1},{8,10},{9,11},{10,... | collective-permute-start | bytes 786440 | tf_op jit(solution)/shard_map/ppermute | solution.py:440
  26.2 14.1 %collective-permute-start.3 = (f32[256,256]{1,0:T(8,128)S(1)}, f32[256,256]{1,0:T(8,128)S(1)}, u32[]{:S(2)}, u32[]{:S(2)}) collective-permute-start(f32[256,256]{1,0:T(8,128)S(1)} %place.1.refs_0_), channel_id=1, source_target_pairs={{0,4},{1,5},{2,6},{3,7},{4,0},{5,1},{6,2},{7,3},{8,12},{9,13},{10,... | collective-permute-start | bytes 786440 | tf_op jit(solution)/shard_map/ppermute | solution.py:440
  27.9 13.0 %collective-permute-start.5 = (f32[256,256]{1,0:T(8,128)S(1)}, f32[256,256]{1,0:T(8,128)S(1)}, u32[]{:S(2)}, u32[]{:S(2)}) collective-permute-start(f32[256,256]{1,0:T(8,128)S(1)} %place.1.refs_0_), channel_id=1, source_target_pairs={{0,6},{1,7},{2,0},{3,1},{4,2},{5,3},{6,4},{7,5},{8,14},{9,15},{10,... | collective-permute-start | bytes 786440 | tf_op jit(solution)/shard_map/ppermute | solution.py:440
  29.3 16.9 %collective-permute-start = (f32[256,256]{1,0:T(8,128)S(1)}, f32[256,256]{1,0:T(8,128)S(1)}, u32[]{:S(2)}, u32[]{:S(2)}) collective-permute-start(f32[256,256]{1,0:T(8,128)S(1)} %place.1.refs_0_), channel_id=1, source_target_pairs={{0,1},{1,0},{2,3},{3,2},{4,5},{5,4},{6,7},{7,6},{8,9},{9,8},{10,11... | collective-permute-start | bytes 786440 | tf_op jit(solution)/shard_map/ppermute | solution.py:443
  40.3 5.9 %collective-permute-start.2 = (f32[256,256]{1,0:T(8,128)S(1)}, f32[256,256]{1,0:T(8,128)S(1)}, u32[]{:S(2)}, u32[]{:S(2)}) collective-permute-start(f32[256,256]{1,0:T(8,128)S(1)} %collective-permute-done.1.refs_2_), channel_id=1, source_target_pairs={{0,1},{1,0},{2,3},{3,2},{4,5},{5,4},{6,7},{7,6},{8,9},{9,8},{10,11... | collective-permute-start | bytes 786440 | tf_op jit(solution)/shard_map/ppermute | solution.py:443
  40.3 5.9 %collective-permute-start.4 = (f32[256,256]{1,0:T(8,128)S(1)}, f32[256,256]{1,0:T(8,128)S(1)}, u32[]{:S(2)}, u32[]{:S(2)}) collective-permute-start(f32[256,256]{1,0:T(8,128)S(1)} %collective-permute-done.3.refs_4_), channel_id=1, source_target_pairs={{0,1},{1,0},{2,3},{3,2},{4,5},{5,4},{6,7},{7,6},{8,9},{9,8},{10,11... | collective-permute-start | bytes 786440 | tf_op jit(solution)/shard_map/ppermute | solution.py:443
  40.9 5.3 %collective-permute-start.6 = (f32[256,256]{1,0:T(8,128)S(1)}, f32[256,256]{1,0:T(8,128)S(1)}, u32[]{:S(2)}, u32[]{:S(2)}) collective-permute-start(f32[256,256]{1,0:T(8,128)S(1)} %collective-permute-done.5.refs_6_), channel_id=1, source_target_pairs={{0,1},{1,0},{2,3},{3,2},{4,5},{5,4},{6,7},{7,6},{8,9},{9,8},{10,11... | collective-permute-start | bytes 786440 | tf_op jit(solution)/shard_map/ppermute | solution.py:443
  49.7 21.5 %collective-permute-start.7 = (f32[512,256]{1,0:T(8,128)S(1)}, f32[512,256]{1,0:T(8,128)S(1)}, u32[]{:S(2)}, u32[]{:S(2)}) collective-permute-start(f32[512,256]{1,0:T(8,128)S(1)} %get-tuple-element.33), channel_id=1, source_target_pairs={{0,8},{8,16},{16,24},{24,0},{32,40},{40,48},{48,56},{56,32},{64,72... | collective-permute-start | bytes 1572872 | tf_op jit(solution)/shard_map/ppermute | solution.py:449
  59.9 31.8 %collective-permute-start.9 = (f32[512,256]{1,0:T(8,128)S(1)}, f32[512,256]{1,0:T(8,128)S(1)}, u32[]{:S(2)}, u32[]{:S(2)}) collective-permute-start(f32[512,256]{1,0:T(8,128)S(1)} %get-tuple-element.37), channel_id=1, source_target_pairs={{0,24},{8,0},{16,8},{24,16},{32,56},{40,32},{48,40},{56,48},{64,88... | collective-permute-start | bytes 1572872 | tf_op jit(solution)/shard_map/ppermute | solution.py:449
  59.9 31.8 %collective-permute-start.8 = (f32[512,256]{1,0:T(8,128)S(1)}, f32[512,256]{1,0:T(8,128)S(1)}, u32[]{:S(2)}, u32[]{:S(2)}) collective-permute-start(f32[512,256]{1,0:T(8,128)S(1)} %get-tuple-element.36), channel_id=1, source_target_pairs={{0,16},{8,24},{16,0},{24,8},{32,48},{40,56},{48,32},{56,40},{64,80... | collective-permute-start | bytes 1572872 | tf_op jit(solution)/shard_map/ppermute | solution.py:449
  62.1 36.6 %collective-permute-start.15 = (f32[512,256]{1,0:T(8,128)S(1)}, f32[512,256]{1,0:T(8,128)S(1)}, u32[]{:S(2)}, u32[]{:S(2)}) collective-permute-start(f32[512,256]{1,0:T(8,128)S(1)} %get-tuple-element.41), channel_id=1, source_target_pairs={{0,96},{8,104},{16,112},{24,120},{32,0},{40,8},{48,16},{56,24},{64... | collective-permute-start | bytes 1572872 | tf_op jit(solution)/shard_map/ppermute | solution.py:450
  64.1 37.4 %collective-permute-start.14 = (f32[512,256]{1,0:T(8,128)S(1)}, f32[512,256]{1,0:T(8,128)S(1)}, u32[]{:S(2)}, u32[]{:S(2)}) collective-permute-start(f32[512,256]{1,0:T(8,128)S(1)} %get-tuple-element.40), channel_id=1, source_target_pairs={{0,64},{8,72},{16,80},{24,88},{32,96},{40,104},{48,112},{56,120},{... | collective-permute-start | bytes 1572872 | tf_op jit(solution)/shard_map/ppermute | solution.py:450
  71.2 30.3 %collective-permute-start.13 = (f32[512,256]{1,0:T(8,128)S(1)}, f32[512,256]{1,0:T(8,128)S(1)}, u32[]{:S(2)}, u32[]{:S(2)}) collective-permute-start(f32[512,256]{1,0:T(8,128)S(1)} %get-tuple-element.39), channel_id=1, source_target_pairs={{0,32},{8,40},{16,48},{24,56},{32,64},{40,72},{48,80},{56,88},{64,... | collective-permute-start | bytes 1572872 | tf_op jit(solution)/shard_map/ppermute | solution.py:450
  91.9 12.2 %collective-permute-start.10 = (f32[128,256]{1,0:T(8,128)S(1)}, f32[128,256]{1,0:T(8,128)S(1)}, u32[]{:S(2)}, u32[]{:S(2)}) collective-permute-start(f32[128,256]{1,0:T(8,128)S(1)} %get-tuple-element.68), channel_id=1, source_target_pairs={{0,32},{8,40},{16,48},{24,56},{32,64},{40,72},{48,80},{56,88},{64,... | collective-permute-start | bytes 393224 | tf_op jit(solution)/shard_map/ppermute | solution.py:463
  98.7 8.0 %collective-permute-start.11 = (f32[128,256]{1,0:T(8,128)S(1)}, f32[128,256]{1,0:T(8,128)S(1)}, u32[]{:S(2)}, u32[]{:S(2)}) collective-permute-start(f32[128,256]{1,0:T(8,128)S(1)} %get-tuple-element.67), channel_id=1, source_target_pairs={{0,64},{8,72},{16,80},{24,88},{32,96},{40,104},{48,112},{56,120},{... | collective-permute-start | bytes 393224 | tf_op jit(solution)/shard_map/ppermute | solution.py:463
  98.7 8.0 %collective-permute-start.12 = (f32[128,256]{1,0:T(8,128)S(1)}, f32[128,256]{1,0:T(8,128)S(1)}, u32[]{:S(2)}, u32[]{:S(2)}) collective-permute-start(f32[128,256]{1,0:T(8,128)S(1)} %get-tuple-element.66), channel_id=1, source_target_pairs={{0,96},{8,104},{16,112},{24,120},{32,0},{40,8},{48,16},{56,24},{64... | collective-permute-start | bytes 393224 | tf_op jit(solution)/shard_map/ppermute | solution.py:463
  101.7 8.6 %collective-permute-start.16 = (f32[128,256]{1,0:T(8,128)S(1)}, f32[128,256]{1,0:T(8,128)S(1)}, u32[]{:S(2)}, u32[]{:S(2)}) collective-permute-start(f32[128,256]{1,0:T(8,128)S(1)} %get-tuple-element.64), channel_id=1, source_target_pairs={{0,8},{8,16},{16,24},{24,0},{32,40},{40,48},{48,56},{56,32},{64,72... | collective-permute-start | bytes 393224 | tf_op jit(solution)/shard_map/ppermute | solution.py:464
  101.8 8.5 %collective-permute-start.17 = (f32[128,256]{1,0:T(8,128)S(1)}, f32[128,256]{1,0:T(8,128)S(1)}, u32[]{:S(2)}, u32[]{:S(2)}) collective-permute-start(f32[128,256]{1,0:T(8,128)S(1)} %get-tuple-element.63), channel_id=1, source_target_pairs={{0,16},{8,24},{16,0},{24,8},{32,48},{40,56},{48,32},{56,40},{64,80... | collective-permute-start | bytes 393224 | tf_op jit(solution)/shard_map/ppermute | solution.py:464
  104.1 6.8 %collective-permute-start.18 = (f32[128,256]{1,0:T(8,128)S(1)}, f32[128,256]{1,0:T(8,128)S(1)}, u32[]{:S(2)}, u32[]{:S(2)}) collective-permute-start(f32[128,256]{1,0:T(8,128)S(1)} %get-tuple-element.62), channel_id=1, source_target_pairs={{0,24},{8,0},{16,8},{24,16},{32,56},{40,32},{48,40},{56,48},{64,88... | collective-permute-start | bytes 393224 | tf_op jit(solution)/shard_map/ppermute | solution.py:464
  112.6 5.5 %collective-permute-start.21 = (f32[128,256]{1,0:T(8,128)S(1)}, f32[128,256]{1,0:T(8,128)S(1)}, u32[]{:S(2)}, u32[]{:S(2)}) collective-permute-start(f32[128,256]{1,0:T(8,128)S(1)} %get-tuple-element.44), channel_id=1, source_target_pairs={{0,96},{8,104},{16,112},{24,120},{32,0},{40,8},{48,16},{56,24},{64... | collective-permute-start | bytes 393224 | tf_op jit(solution)/shard_map/ppermute | solution.py:472
  113.7 6.7 %collective-permute-start.20 = (f32[128,256]{1,0:T(8,128)S(1)}, f32[128,256]{1,0:T(8,128)S(1)}, u32[]{:S(2)}, u32[]{:S(2)}) collective-permute-start(f32[128,256]{1,0:T(8,128)S(1)} %get-tuple-element.44), channel_id=1, source_target_pairs={{0,64},{8,72},{16,80},{24,88},{32,96},{40,104},{48,112},{56,120},{... | collective-permute-start | bytes 393224 | tf_op jit(solution)/shard_map/ppermute | solution.py:472
  113.9 7.7 %collective-permute-start.19 = (f32[128,256]{1,0:T(8,128)S(1)}, f32[128,256]{1,0:T(8,128)S(1)}, u32[]{:S(2)}, u32[]{:S(2)}) collective-permute-start(f32[128,256]{1,0:T(8,128)S(1)} %get-tuple-element.44), channel_id=1, source_target_pairs={{0,32},{8,40},{16,48},{24,56},{32,64},{40,72},{48,80},{56,88},{64,... | collective-permute-start | bytes 393224 | tf_op jit(solution)/shard_map/ppermute | solution.py:472
  114.8 6.8 %collective-permute-start.24 = (f32[128,256]{1,0:T(8,128)S(1)}, f32[128,256]{1,0:T(8,128)S(1)}, u32[]{:S(2)}, u32[]{:S(2)}) collective-permute-start(f32[128,256]{1,0:T(8,128)S(1)} %get-tuple-element.45), channel_id=1, source_target_pairs={{0,24},{8,0},{16,8},{24,16},{32,56},{40,32},{48,40},{56,48},{64,88... | collective-permute-start | bytes 393224 | tf_op jit(solution)/shard_map/ppermute | solution.py:473
  117.3 6.6 %collective-permute-start.23 = (f32[128,256]{1,0:T(8,128)S(1)}, f32[128,256]{1,0:T(8,128)S(1)}, u32[]{:S(2)}, u32[]{:S(2)}) collective-permute-start(f32[128,256]{1,0:T(8,128)S(1)} %get-tuple-element.45), channel_id=1, source_target_pairs={{0,16},{8,24},{16,0},{24,8},{32,48},{40,56},{48,32},{56,40},{64,80... | collective-permute-start | bytes 393224 | tf_op jit(solution)/shard_map/ppermute | solution.py:473
  118.1 7.1 %collective-permute-start.22 = (f32[128,256]{1,0:T(8,128)S(1)}, f32[128,256]{1,0:T(8,128)S(1)}, u32[]{:S(2)}, u32[]{:S(2)}) collective-permute-start(f32[128,256]{1,0:T(8,128)S(1)} %get-tuple-element.45), channel_id=1, source_target_pairs={{0,8},{8,16},{16,24},{24,0},{32,40},{40,48},{48,56},{56,32},{64,72... | collective-permute-start | bytes 393224 | tf_op jit(solution)/shard_map/ppermute | solution.py:473
  120.3 4.9 %collective-permute-start.25 = (f32[160,256]{1,0:T(8,128)S(1)}, f32[160,256]{1,0:T(8,128)S(1)}, u32[]{:S(2)}, u32[]{:S(2)}) collective-permute-start(f32[160,256]{1,0:T(8,128)S(1)} %get-tuple-element.46), channel_id=1, source_target_pairs={{0,1},{1,0},{2,3},{3,2},{4,5},{5,4},{6,7},{7,6},{8,9},{9,8},{10,11... | collective-permute-start | bytes 491528 | tf_op jit(solution)/shard_map/ppermute | solution.py:477
  125.2 23.3 %collective-permute-start.32 = (f32[512,256]{1,0:T(8,128)S(1)}, f32[512,256]{1,0:T(8,128)S(1)}, u32[]{:S(2)}, u32[]{:S(2)}) collective-permute-start(f32[512,256]{1,0:T(8,128)S(1)} %pad_maximum_fusion.refs_0_), channel_id=1, source_target_pairs={{0,8},{8,16},{16,24},{24,0},{32,40},{40,48},{48,56},{56,32},{64,72... | collective-permute-start | bytes 1572872 | tf_op jit(solution)/shard_map/ppermute | solution.py:480
  125.4 4.2 %collective-permute-start.28 = (f32[40,256]{1,0:T(8,128)S(1)}, f32[40,256]{1,0:T(8,128)S(1)}, u32[]{:S(2)}, u32[]{:S(2)}) collective-permute-start(f32[40,256]{1,0:T(8,128)S(1)} %get-tuple-element.71), channel_id=1, source_target_pairs={{0,6},{1,7},{2,0},{3,1},{4,2},{5,3},{6,4},{7,5},{8,14},{9,15},{10,... | collective-permute-start | bytes 122888 | tf_op jit(solution)/shard_map/ppermute | solution.py:487
  127.9 5.6 %collective-permute-start.27 = (f32[40,256]{1,0:T(8,128)S(1)}, f32[40,256]{1,0:T(8,128)S(1)}, u32[]{:S(2)}, u32[]{:S(2)}) collective-permute-start(f32[40,256]{1,0:T(8,128)S(1)} %get-tuple-element.72), channel_id=1, source_target_pairs={{0,4},{1,5},{2,6},{3,7},{4,0},{5,1},{6,2},{7,3},{8,12},{9,13},{10,... | collective-permute-start | bytes 122888 | tf_op jit(solution)/shard_map/ppermute | solution.py:487
  127.9 5.7 %collective-permute-start.26 = (f32[40,256]{1,0:T(8,128)S(1)}, f32[40,256]{1,0:T(8,128)S(1)}, u32[]{:S(2)}, u32[]{:S(2)}) collective-permute-start(f32[40,256]{1,0:T(8,128)S(1)} %get-tuple-element.70), channel_id=1, source_target_pairs={{0,2},{1,3},{2,4},{3,5},{4,6},{5,7},{6,0},{7,1},{8,10},{9,11},{10,... | collective-permute-start | bytes 122888 | tf_op jit(solution)/shard_map/ppermute | solution.py:487
  133.5 6.9 %collective-permute-start.30 = (f32[40,256]{1,0:T(8,128)S(1)}, f32[40,256]{1,0:T(8,128)S(1)}, u32[]{:S(2)}, u32[]{:S(2)}) collective-permute-start(f32[40,256]{1,0:T(8,128)S(1)} %fusion.1), channel_id=1, source_target_pairs={{0,8},{8,16},{16,24},{24,0},{32,40},{40,48},{48,56},{56,32},{64,72... | collective-permute-start | bytes 122888 | tf_op jit(solution)/shard_map/ppermute | solution.py:489
  134.2 8.2 %collective-permute-start.31 = (f32[40,256]{1,0:T(8,128)S(1)}, f32[40,256]{1,0:T(8,128)S(1)}, u32[]{:S(2)}, u32[]{:S(2)}) collective-permute-start(f32[40,256]{1,0:T(8,128)S(1)} %fusion.1), channel_id=1, source_target_pairs={{0,24},{8,0},{16,8},{24,16},{32,56},{40,32},{48,40},{56,48},{64,88... | collective-permute-start | bytes 122888 | tf_op jit(solution)/shard_map/ppermute | solution.py:489
  136.9 7.4 %collective-permute-start.29 = (f32[40,256]{1,0:T(8,128)S(1)}, f32[40,256]{1,0:T(8,128)S(1)}, u32[]{:S(2)}, u32[]{:S(2)}) collective-permute-start(f32[40,256]{1,0:T(8,128)S(1)} %fusion.1), channel_id=1, source_target_pairs={{0,16},{8,24},{16,0},{24,8},{32,48},{40,56},{48,32},{56,40},{64,80... | collective-permute-start | bytes 122888 | tf_op jit(solution)/shard_map/ppermute | solution.py:489
  138.3 12.8 %collective-permute-start.33 = (f32[512,256]{1,0:T(8,128)S(1)}, f32[512,256]{1,0:T(8,128)S(1)}, u32[]{:S(2)}, u32[]{:S(2)}) collective-permute-start(f32[512,256]{1,0:T(8,128)S(1)} %pad_maximum_fusion.refs_0_), channel_id=1, source_target_pairs={{0,16},{8,24},{16,0},{24,8},{32,48},{40,56},{48,32},{56,40},{64,80... | collective-permute-start | bytes 1572872 | tf_op jit(solution)/shard_map/ppermute | solution.py:480
  140.4 18.0 %collective-permute-start.34 = (f32[512,256]{1,0:T(8,128)S(1)}, f32[512,256]{1,0:T(8,128)S(1)}, u32[]{:S(2)}, u32[]{:S(2)}) collective-permute-start(f32[512,256]{1,0:T(8,128)S(1)} %pad_maximum_fusion.refs_0_), channel_id=1, source_target_pairs={{0,24},{8,0},{16,8},{24,16},{32,56},{40,32},{48,40},{56,48},{64,88... | collective-permute-start | bytes 1572872 | tf_op jit(solution)/shard_map/ppermute | solution.py:480
  142.4 16.0 %collective-permute-start.35 = (f32[512,256]{1,0:T(8,128)S(1)}, f32[512,256]{1,0:T(8,128)S(1)}, u32[]{:S(2)}, u32[]{:S(2)}) collective-permute-start(f32[512,256]{1,0:T(8,128)S(1)} %pad_maximum_fusion.1.refs_4_), channel_id=1, source_target_pairs={{0,32},{8,40},{16,48},{24,56},{32,64},{40,72},{48,80},{56,88},{64,... | collective-permute-start | bytes 1572872 | tf_op jit(solution)/shard_map/ppermute | solution.py:481
  144.3 18.0 %collective-permute-start.36 = (f32[512,256]{1,0:T(8,128)S(1)}, f32[512,256]{1,0:T(8,128)S(1)}, u32[]{:S(2)}, u32[]{:S(2)}) collective-permute-start(f32[512,256]{1,0:T(8,128)S(1)} %pad_maximum_fusion.1.refs_4_), channel_id=1, source_target_pairs={{0,64},{8,72},{16,80},{24,88},{32,96},{40,104},{48,112},{56,120},{... | collective-permute-start | bytes 1572872 | tf_op jit(solution)/shard_map/ppermute | solution.py:481
  148.5 14.5 %collective-permute-start.37 = (f32[512,256]{1,0:T(8,128)S(1)}, f32[512,256]{1,0:T(8,128)S(1)}, u32[]{:S(2)}, u32[]{:S(2)}) collective-permute-start(f32[512,256]{1,0:T(8,128)S(1)} %pad_maximum_fusion.1.refs_4_), channel_id=1, source_target_pairs={{0,96},{8,104},{16,112},{24,120},{32,0},{40,8},{48,16},{56,24},{64... | collective-permute-start | bytes 1572872 | tf_op jit(solution)/shard_map/ppermute | solution.py:481
  166.5 14.8 %collective-permute-start.38 = (f32[1024,256]{1,0:T(8,128)S(1)}, f32[1024,256]{1,0:T(8,128)S(1)}, u32[]{:S(2)}, u32[]{:S(2)}) collective-permute-start(f32[1024,256]{1,0:T(8,128)S(1)} %get-tuple-element.53), channel_id=1, source_target_pairs={{0,1},{1,0},{2,3},{3,2},{4,5},{5,4},{6,7},{7,6},{8,9},{9,8},{10,11... | collective-permute-start | bytes 3145736 | tf_op jit(solution)/shard_map/ppermute | solution.py:494
  166.5 9.2 %collective-permute-start.42 = (f32[40,256]{1,0:T(8,128)S(1)}, f32[40,256]{1,0:T(8,128)S(1)}, u32[]{:S(2)}, u32[]{:S(2)}) collective-permute-start(f32[40,256]{1,0:T(8,128)S(1)} %add_add_fusion), channel_id=1, source_target_pairs={{0,32},{8,40},{16,48},{24,56},{32,0},{40,8},{48,16},{56,24},{64,96... | collective-permute-start | bytes 122888 | tf_op jit(solution)/shard_map/ppermute | solution.py:492
  175.8 5.5 %collective-permute-start.43 = (f32[40,256]{1,0:T(8,128)S(1)}, f32[40,256]{1,0:T(8,128)S(1)}, u32[]{:S(2)}, u32[]{:S(2)}) collective-permute-start(f32[40,256]{1,0:T(8,128)S(1)} %add.213), channel_id=1, source_target_pairs={{0,64},{8,72},{16,80},{24,88},{32,96},{40,104},{48,112},{56,120},{... | collective-permute-start | bytes 122888 | tf_op jit(solution)/shard_map/ppermute | solution.py:495
  181.3 8.6 %collective-permute-start.44 = (f32[40,256]{1,0:T(8,128)S(1)}, f32[40,256]{1,0:T(8,128)S(1)}, u32[]{:S(2)}, u32[]{:S(2)}) collective-permute-start(f32[40,256]{1,0:T(8,128)S(1)} %add.214), channel_id=1, source_target_pairs={{0,1},{1,0},{2,3},{3,2},{4,5},{5,4},{6,7},{7,6},{8,9},{9,8},{10,11... | collective-permute-start | bytes 122888 | tf_op jit(solution)/shard_map/ppermute | solution.py:500
  181.5 25.7 %collective-permute-start.39 = (f32[256,256]{1,0:T(8,128)S(1)}, f32[256,256]{1,0:T(8,128)S(1)}, u32[]{:S(2)}, u32[]{:S(2)}) collective-permute-start(f32[256,256]{1,0:T(8,128)S(1)} %get-tuple-element.60), channel_id=1, source_target_pairs={{0,2},{1,3},{2,4},{3,5},{4,6},{5,7},{6,0},{7,1},{8,10},{9,11},{10,... | collective-permute-start | bytes 786440 | tf_op jit(solution)/shard_map/ppermute | solution.py:499
  181.6 25.6 %collective-permute-start.40 = (f32[256,256]{1,0:T(8,128)S(1)}, f32[256,256]{1,0:T(8,128)S(1)}, u32[]{:S(2)}, u32[]{:S(2)}) collective-permute-start(f32[256,256]{1,0:T(8,128)S(1)} %get-tuple-element.59), channel_id=1, source_target_pairs={{0,4},{1,5},{2,6},{3,7},{4,0},{5,1},{6,2},{7,3},{8,12},{9,13},{10,... | collective-permute-start | bytes 786440 | tf_op jit(solution)/shard_map/ppermute | solution.py:499
  189.9 17.3 %collective-permute-start.41 = (f32[256,256]{1,0:T(8,128)S(1)}, f32[256,256]{1,0:T(8,128)S(1)}, u32[]{:S(2)}, u32[]{:S(2)}) collective-permute-start(f32[256,256]{1,0:T(8,128)S(1)} %get-tuple-element.58), channel_id=1, source_target_pairs={{0,6},{1,7},{2,0},{3,1},{4,2},{5,3},{6,4},{7,5},{8,14},{9,15},{10,... | collective-permute-start | bytes 786440 | tf_op jit(solution)/shard_map/ppermute | solution.py:499
  189.9 12.9 %collective-permute-start.45 = (f32[80,256]{1,0:T(8,128)S(1)}, f32[80,256]{1,0:T(8,128)S(1)}, u32[]{:S(2)}, u32[]{:S(2)}) collective-permute-start(f32[80,256]{1,0:T(8,128)S(1)} %pad_maximum_fusion.2.refs_4_), channel_id=1, source_target_pairs={{0,2},{1,3},{2,4},{3,5},{4,6},{5,7},{6,0},{7,1},{8,10},{9,11},{10,... | collective-permute-start | bytes 245768 | tf_op jit(solution)/shard_map/ppermute | solution.py:502
  192.0 13.7 %collective-permute-start.46 = (f32[80,256]{1,0:T(8,128)S(1)}, f32[80,256]{1,0:T(8,128)S(1)}, u32[]{:S(2)}, u32[]{:S(2)}) collective-permute-start(f32[80,256]{1,0:T(8,128)S(1)} %pad_maximum_fusion.2.refs_4_), channel_id=1, source_target_pairs={{0,4},{1,5},{2,6},{3,7},{4,0},{5,1},{6,2},{7,3},{8,12},{9,13},{10,... | collective-permute-start | bytes 245768 | tf_op jit(solution)/shard_map/ppermute | solution.py:502
  202.8 4.4 %collective-permute-start.47 = (f32[80,256]{1,0:T(8,128)S(1)}, f32[80,256]{1,0:T(8,128)S(1)}, u32[]{:S(2)}, u32[]{:S(2)}) collective-permute-start(f32[80,256]{1,0:T(8,128)S(1)} %pad_maximum_fusion.2.refs_4_), channel_id=1, source_target_pairs={{0,6},{1,7},{2,0},{3,1},{4,2},{5,3},{6,4},{7,5},{8,14},{9,15},{10,... | collective-permute-start | bytes 245768 | tf_op jit(solution)/shard_map/ppermute | solution.py:502
  (4 other events, 118.1 us)
